TPU v7x, 256 devices: a whole 4x4x8 slice. The times are simulated.
256 devices in a mesh: lat: 128 (over z, y, x), field: 2 (over core).
Axes of the slice: x: 4, y: 4, z: 8, core: 2. Of those that a mesh axis runs over, the one named last changes fastest.
Arguments:
- fields_grid: bfloat16 [2, 64, 2, 384, 1536], P('field', None, None, 'lat'), may hold values from -6 to 6
- basis: bfloat16 [1024, 384, 768], P('lat'), may hold values from -0.3125 to 0.3125
- order_table: int32 [128, 8], replicated, may hold values from -1 to 767, as said below
- panel_modes: int32 [2, 64], replicated, may hold values from 0 to 767, as said below
Outputs:
- panel: bfloat16 [2, 1024, 1536, 128], P('field', 'lat')
Inputs may be any that keep to these rules, and one draw needn't show every extreme that they name: `order_table`: each order 0 to 767 stands in exactly one slot; every other slot holds -1; some group has all 8 slots filled. `panel_modes`: row 1 is never smaller than row 0 in the same column; degree 767 appears.
All inputs are finite; a program needn't handle non-finite values.
Results may differ from a plain program's by a relative error of at most 0.0082.
Values may be sent and summed in bfloat16 or wider, within the bound.
No kernel may reach another device: no remote copies, remote signals or barrier semaphores. Data moves between devices by JAX's collectives and lax.ppermute only.
A program may use at most 64 MiB of HBM per device.

v0:
```python
import math

import jax
import jax.numpy as jnp
from jax import lax
from jax.sharding import PartitionSpec as P


def swapped(block, axis, bit):
    count = lax.axis_size(axis)
    route = []
    for low in range(count):
        high = low | 1 << bit
        if high != low and high < count:
            route += [(low, high), (high, low)]
    return lax.ppermute(block, axis, route)


def dft_table(orders, lon_count):
    valid_slot = orders >= 0
    safe_orders = jnp.maximum(orders, 0)
    products = lax.broadcasted_iota(jnp.int32, (lon_count, 1), 0) * safe_orders[None, :] % lon_count
    angles = products.astype(jnp.float32) * (2.0 * math.pi / lon_count)
    cosine = jnp.where(valid_slot[None, :], jnp.cos(angles), 0.0).astype(jnp.bfloat16)
    sine_table = jnp.where(valid_slot[None, :], -jnp.sin(angles), 0.0).astype(jnp.bfloat16)
    return jnp.stack([cosine, sine_table], axis=1)


def local(fields_grid, basis, order_table, panel_modes):
    grid_one = fields_grid[0]
    snap_count = grid_one.shape[0]
    pair_count = grid_one.shape[2]
    lon_count = grid_one.shape[3]
    slot_count = order_table.shape[1]
    deg_count = basis.shape[2]
    pair_total = basis.shape[1]
    mode_count = panel_modes.shape[1]
    orders = order_table.reshape(-1)
    slot_all = orders.shape[0]
    dft = dft_table(orders, lon_count)
    fourier = jnp.einsum("thjn,nrk->hkjrt", grid_one, dft, preferred_element_type=jnp.float32) * (
        1.0 / math.sqrt(lon_count)
    )
    fourier = fourier.reshape(2, slot_all, pair_count, 2 * snap_count)
    parity_parts = jnp.stack([fourier[0] + fourier[1], fourier[0] - fourier[1]]).astype(
        jnp.bfloat16
    )
    group_index = lax.axis_index("lat")
    my_orders = lax.dynamic_slice_in_dim(order_table, group_index, 1, 0)[0]
    my_odd = my_orders % 2 == 1
    basis_split = basis.reshape(slot_count, pair_total, deg_count // 2, 2)
    even_rows = basis_split[:, :, :, 0]
    odd_rows = basis_split[:, :, :, 1]
    degree = lax.broadcasted_iota(jnp.int32, (1, deg_count), 1)
    keep_mask = (degree >= my_orders[:, None]) & (my_orders >= 0)[:, None]
    received = lax.all_to_all(parity_parts, "lat", split_axis=1, concat_axis=2, tiled=True)
    first_parity = jnp.where(my_odd[:, None, None], received[1], received[0])
    second = jnp.where(my_odd[:, None, None], received[0], received[1])
    low_degrees = jnp.einsum(
        "sjh,sjc->shc", even_rows, first_parity, preferred_element_type=jnp.float32
    )
    high_degrees = jnp.einsum("sjh,sjc->shc", odd_rows, second, preferred_element_type=jnp.float32)
    joined = jnp.stack([low_degrees, high_degrees], axis=2).reshape(slot_count, deg_count, -1)
    coefficients = jnp.where(keep_mask[:, :, None], joined, 0.0).astype(jnp.bfloat16)
    mode_order = panel_modes[0]
    mode_degree = panel_modes[1]
    onehot = (my_orders[None, :] == mode_order[:, None]).astype(jnp.bfloat16)
    picked = jnp.take(coefficients, mode_degree, axis=1)
    local_values = jnp.einsum("ms,smc->mc", onehot, picked, preferred_element_type=jnp.float32)
    summed = lax.psum(local_values, "lat")
    other_field = swapped(summed.astype(jnp.bfloat16), "field", 0)
    columns = other_field.astype(jnp.float32).reshape(mode_count * 2, snap_count)
    centered = (columns - jnp.mean(columns, axis=1, keepdims=True)).astype(jnp.bfloat16)
    coef_rows = coefficients.reshape(slot_count * deg_count * 2, snap_count)
    panel_values = lax.dot_general(
        coef_rows, centered, (((1,), (1,)), ((), ())), preferred_element_type=jnp.float32
    )
    panel_values = panel_values * (1.0 / (snap_count - 1))
    return panel_values.astype(jnp.bfloat16).reshape(1, slot_count, 2 * deg_count, 2 * mode_count)


def solution(mesh):
    placed = (P("field", None, None, "lat", None), P("lat", None, None), P(), P())
    return jax.shard_map(
        local, mesh=mesh, in_specs=placed, out_specs=P("field", "lat", None, None), check_vma=False
    )
```

profile of v0, /device:TPU:2, one launch (start us, length us, event | category | flops | bytes accessed | tf_op | source)
XLA Modules:
  0.0 788.4 jit_solution(16079482596580234640)
XLA Ops:
  0.0 0.7 broadcast_maximum_fusion
  0.7 0.7 broadcast_compare_fusion
  1.4 0.1 copy.38
  1.5 0.1 max.11
  1.6 0.1 copy.37
  1.7 0.1 ge.51
  1.8 0.0 copy-start.2
  1.8 26.9 %select_convert_fusion.1 = (bf16[1536,1,1024]{2,0,1:T(8,128)(2,1)S(1)}, bf16[1536,1,1024]{2,0,1:T(8,128)(2,1)S(1)}) fusion(s32[1024]{0:T(1024)S(1)} %max.11, pred[1024]{0:T(1024)(128)(4,1)S(1)} %ge.51), kind=kLoop, calls=%fused_computation.11 | loop fusion | flops 22020096 | bytes 6296576 | tf_op jit(solution)/shard_map/convert_element_type | solution.py:24
  28.8 0.0 copy-done.2
  28.8 2.8 multiply_bitcast_fusion
  31.6 0.5 add_convert_fusion
  32.1 0.1 copy.40
  32.1 0.1 copy.41
  32.2 0.1 pad_maximum_fusion.1
  32.3 0.0 copy-start.1
  32.4 2.9 copy.42
  35.3 15.8 %all-to-all-start = ((bf16[2,1024,3,128]{3,0,2,1:T(2,128)(2,1)}), bf16[2,1024,3,128]{3,0,2,1:T(2,128)(2,1)}, u32[]{:S(2)}, u32[]{:S(2)}) async-start(bf16[2,1024,3,128]{3,0,2,1:T(2,128)(2,1)} %copy.42), calls=%async_computation | async-start | bytes 3145728 | tf_op jit(solution)/shard_map/all_to_all | solution.py:56
  51.2 0.0 copy-done.1
  51.2 0.2 dynamic-slice_reduce_fusion
  51.3 7.0 copy.46
  58.4 4.3 fusion.36
  62.6 2.9 copy.56
  65.6 0.0 copy-start.3
  65.6 3.2 copy.57
  68.8 0.0 copy-done.3
  68.9 0.1 compare_bitcast_fusion
  69.0 0.1 fusion.24
  69.1 23.2 %all-to-all-done = bf16[2,1024,3,128]{3,0,2,1:T(2,128)(2,1)} async-done(((bf16[2,1024,3,128]{3,0,2,1:T(2,128)(2,1)}), bf16[2,1024,3,128]{3,0,2,1:T(2,128)(2,1)}, u32[]{:S(2)}, u32[]{:S(2)}) %all-to-all-start) | async-done | bytes 1572896 | tf_op jit(solution)/shard_map/all_to_all | solution.py:56
  92.3 1.6 copy.69
  93.9 0.1 fusion.37
  94.0 0.0 copy-start
  94.0 0.1 copy.44
  94.1 0.1 copy.45
  94.3 0.3 bitcast_select_fusion.2
  94.6 1.1 copy-done
  95.7 0.7 fusion.14
  96.4 0.7 fusion.17
  97.1 0.2 pad_maximum_fusion
  97.3 1.4 copy.51
  98.7 2.5 fusion.9
  101.1 0.6 gather_fusion
  101.8 0.3 fusion.25
  102.0 677.7 %psum.7 = bf16[64,128]{1,0:T(8,128)(2,1)S(1)} all-reduce(f32[64,128]{1,0:T(8,128)S(1)} %bitcast.71), channel_id=1, replica_groups=mesh['lat'=128,'field'=2] {'lat'}, use_global_device_ids=true, to_apply=%region_0.1 | all-reduce | flops 8192 | bytes 49152 | tf_op jit(solution)/shard_map/psum | solution.py:70
  779.7 0.0 collective-permute-start
  779.7 1.4 copy.52
  781.1 3.9 convert_element_type.68
  785.1 0.0 collective-permute-done
  785.1 0.1 reshape.334
  785.1 0.1 reduce_sum.9
  785.3 0.1 div.10
  785.4 0.1 sub.26
  785.5 0.1 sub.27
  785.7 0.1 convert_element_type.72
  785.7 2.7 fusion
  (7 shorter events, 0.0 us)
Async XLA Ops:
  1.8 27.0 %copy-start.2 = (bf16[1,64,2,3,1536]{4,2,3,1,0:T(2,128)(2,1)S(1)}, bf16[1,64,2,3,1536]{4,2,3,1,0:T(2,128)(2,1)}, u32[]{:S(2)}) copy-start(bf16[1,64,2,3,1536]{4,2,3,1,0:T(2,128)(2,1)} %param.4) | copy-start | bytes 3538948
  32.3 18.8 %copy-start.1 = (s32[128,8]{0,1:T(8,128)S(1)}, s32[128,8]{0,1:T(8,128)}, u32[]{:S(2)}) copy-start(s32[128,8]{0,1:T(8,128)} %param.6) | copy-start | bytes 12292
  35.3 57.0 %all-to-all-start = ((bf16[2,1024,3,128]{3,0,2,1:T(2,128)(2,1)}), bf16[2,1024,3,128]{3,0,2,1:T(2,128)(2,1)}, u32[]{:S(2)}, u32[]{:S(2)}) async-start(bf16[2,1024,3,128]{3,0,2,1:T(2,128)(2,1)} %copy.42), calls=%async_computation | async-start | bytes 3145728 | tf_op jit(solution)/shard_map/all_to_all | solution.py:56
  65.6 3.3 copy-start.3
  94.0 1.7 copy-start
  779.7 5.3 collective-permute-start
where the time goes:
time: 797 us; the launch traced here: 788 us
  blocking collectives  678 us (85%)
  other arithmetic  32.2 us (4%)
  local copies, waits for them, and re-layouts  32.1 us (4%)
  waiting for transfers between devices  23.2 us (3%)
  starting transfers between devices  15.8 us (2%)
    psum x1, blocking collectives, local(): summed = lax.psum(local_values, 'lat')  678 us
    convert_element_type x1, other arithmetic, dft_table(): jnp.where(valid_slot[None, :], jnp.cos(angles), 0.0).astype(jnp.bfloat16)  26.9 us
    all_to_all x1, waiting for transfers between devices, local(): lax.all_to_all(parity_parts, 'lat', split_axis=1, concat_axis=2, tiled=True)  23.2 us
  transfers between devices with their start and end apart: 2, of which 1 were waited for; matrix products, arithmetic and copies ran while one was open for 3% of the time, Pallas kernels for 0%

commit v1 on v0

v1 whole, which is shorter than its diff:
```python
import math

import jax
import jax.numpy as jnp
import numpy as np
from jax import lax
from jax.sharding import PartitionSpec as P


def dft_table(lon_count, order_count):
    products = np.arange(lon_count)[:, None] * np.arange(order_count)[None, :] % lon_count
    angles = products * (2.0 * math.pi / lon_count)
    return np.stack([np.cos(angles), -np.sin(angles)], axis=1).astype(jnp.bfloat16)


def doubled(block, axis):
    count = lax.axis_size(axis)
    reach = 1
    while reach < count:
        block = block + lax.ppermute(block, axis, [(i, i ^ reach) for i in range(count)])
        reach *= 2
    return block


def local(fields_grid, basis, order_table, panel_modes):
    grid_one = fields_grid[0]
    snap_count, _, pair_count, lon_count = grid_one.shape
    group_count, slot_count = order_table.shape
    pair_total, deg_count = basis.shape[1], basis.shape[2]
    mode_count = panel_modes.shape[1]
    order_count = lon_count // 2
    orders = order_table.reshape(-1)
    slot_all = orders.shape[0]

    table = jnp.asarray(dft_table(lon_count, order_count))
    fourier = jnp.einsum("thjn,nrm->hjrtm", grid_one, table, preferred_element_type=jnp.float32)
    fourier = fourier * (1.0 / math.sqrt(lon_count))
    parts = jnp.stack([fourier[0] + fourier[1], fourier[0] - fourier[1]]).astype(jnp.bfloat16)
    parts = parts.reshape(2 * pair_count * 2 * snap_count, order_count)
    placed = (orders[:, None] == lax.broadcasted_iota(jnp.int32, (1, order_count), 1)).astype(
        jnp.bfloat16
    )
    sent = lax.dot_general(
        placed, parts, (((1,), (1,)), ((), ())), preferred_element_type=jnp.float32
    ).astype(jnp.bfloat16)
    sent = sent.reshape(group_count, slot_count * 2 * pair_count, 2 * snap_count)
    received = lax.all_to_all(sent, "lat", split_axis=0, concat_axis=0, tiled=True)
    received = received.reshape(group_count, slot_count, 2, pair_count, 2 * snap_count)

    group_index = lax.axis_index("lat")
    my_orders = lax.dynamic_slice_in_dim(order_table, group_index, 1, 0)[0]
    rows = received.transpose(1, 0, 3, 2, 4).reshape(slot_count, pair_total, 4 * snap_count)
    both = jnp.einsum("sjl,sjc->slc", basis, rows, preferred_element_type=jnp.float32)
    degree = lax.broadcasted_iota(jnp.int32, (1, deg_count), 1)
    odd = (degree - my_orders[:, None]) % 2 == 1
    keep = (degree >= my_orders[:, None]) & (my_orders >= 0)[:, None]
    chosen = jnp.where(odd[:, :, None], both[:, :, 2 * snap_count :], both[:, :, : 2 * snap_count])
    coefficients = jnp.where(keep[:, :, None], chosen, 0.0).astype(jnp.bfloat16)

    owned = (my_orders[None, :] == panel_modes[0][:, None]).astype(jnp.bfloat16)
    picked = jnp.take(coefficients, panel_modes[1], axis=1)
    values = jnp.einsum("ms,smc->mc", owned, picked, preferred_element_type=jnp.float32)
    values = lax.ppermute(values.astype(jnp.bfloat16), "field", [(0, 1), (1, 0)])
    columns = doubled(values, "lat").astype(jnp.float32).reshape(2 * mode_count, snap_count)
    centered = (columns - jnp.mean(columns, axis=1, keepdims=True)).astype(jnp.bfloat16)

    coef_rows = coefficients.reshape(slot_count * deg_count * 2, snap_count)
    panel_values = lax.dot_general(
        coef_rows, centered, (((1,), (1,)), ((), ())), preferred_element_type=jnp.float32
    )
    panel_values = panel_values * (1.0 / (snap_count - 1))
    return panel_values.astype(jnp.bfloat16).reshape(1, slot_count, 2 * deg_count, 2 * mode_count)


def solution(mesh):
    placed = (P("field", None, None, "lat", None), P("lat", None, None), P(), P())
    return jax.shard_map(
        local, mesh=mesh, in_specs=placed, out_specs=P("field", "lat", None, None), check_vma=False
    )
```

time: 797 us -> 117 us (0.15)
  blocking collectives: 678 us -> 0 us
  waiting for transfers between devices: 23.2 us -> 62.6 us
  other arithmetic: 32.2 us -> 1.3 us
  local copies, waits for them, and re-layouts: 32.1 us -> 14.3 us
  starting transfers between devices: 15.8 us -> 24.2 us
    psum x1 -> x0, blocking collectives: 678 us -> none  [local(): summed = lax.psum(local_values, 'lat')]
    convert_element_type x2 -> x3, other arithmetic: 29.4 us -> 0.56 us  [the longest x1 0.55 us: local(): coefficients = jnp.where(keep[:, :, None], chosen, 0.0).astype(jnp.bfloat16)]
    ppermute x1 -> x8, waiting for transfers between devices: 0.01 us -> 21.6 us  [the longest x7 20.4 us: doubled(): lax.ppermute(block, axis, [(i, i ^ reach) for i in range(count)])]
    all_to_all x1, waiting for transfers between devices: 23.2 us -> 41 us  [local(): lax.all_to_all(sent, 'lat', split_axis=0, concat_axis=0, tiled=True)]
    unnamed x11 -> x5, local copies, waits for them, and re-layouts: 14.3 us -> 0.79 us
    ppermute x1 -> x8, starting transfers between devices: 0.01 us -> 8.68 us  [the longest x7 8.59 us: doubled(): lax.ppermute(block, axis, [(i, i ^ reach) for i in range(count)])]
  transfers between devices with their start and end apart: 2 -> 9, of which waited for: 1 -> 9; matrix products, arithmetic and copies ran while one was open for 3% -> 5% of each run, Pallas kernels for 0% -> 0%
where the time goes in v1:
time: 117 us; the launch traced here: 116 us
  waiting for transfers between devices  62.6 us (54%)
  starting transfers between devices  24.2 us (21%)
  local copies, waits for them, and re-layouts  14.3 us (12%)
  matrix products  13.4 us (11%)
  other arithmetic  1.3 us (1%)
    all_to_all x1, waiting for transfers between devices, local(): lax.all_to_all(sent, 'lat', split_axis=0, concat_axis=0, tiled=True)  41 us
    ppermute x7, waiting for transfers between devices, doubled(): lax.ppermute(block, axis, [(i, i ^ reach) for i in range(count)])  20.4 us
    all_to_all x1, starting transfers between devices, local(): lax.all_to_all(sent, 'lat', split_axis=0, concat_axis=0, tiled=True)  15.6 us
    ppermute x7, starting transfers between devices, doubled(): lax.ppermute(block, axis, [(i, i ^ reach) for i in range(count)])  8.59 us
    dot_general x1, matrix products, local(): jnp.einsum('thjn,nrm->hjrtm', grid_one, table, preferred_element_type=jnp...  4.7 us
    dot_general x1, matrix products, local(): jnp.einsum('sjl,sjc->slc', basis, rows, preferred_element_type=jnp.float32)  4.18 us
    reshape x1, local copies, waits for them, and re-layouts, local(): coef_rows = coefficients.reshape(slot_count * deg_count * 2, snap_count)  3.92 us
    convert_element_type x2, local copies, waits for them, and re-layouts, local(): coefficients = jnp.where(keep[:, :, None], chosen, 0.0).astype(jnp.bfloat16)  2.75 us
  transfers between devices with their start and end apart: 9, of which 9 were waited for; matrix products, arithmetic and copies ran while one was open for 5% of the time, Pallas kernels for 0%

profile of v1, /device:TPU:2, one launch (start us, length us, event | category | flops | bytes accessed | tf_op | source)
XLA Modules:
  0.0 116.0 jit_solution(451920371530316573)
XLA Ops:
  0.0 0.8 copy.16
  0.8 0.1 eq.41
  0.9 4.7 %multiply_bitcast_fusion = f32[2,3,2,64,768]{4,3,1,0,2:T(8,128)S(1)} fusion(bf16[1536,2,768,1,1]{2,0,4,3,1:T(8,128)(2,1)} %constant.55, bf16[64,2,3,1536]{3,1,2,0:T(2,128)(2,1)} %bitcast.40), kind=kOutput, calls=%fused_computation.9 | convolution fusion | flops 1812529152 | bytes 8257536 | tf_op jit(solution)/shard_map/thjn,nrm->hjrtm/dot_general | solution.py:36
  5.6 0.3 add_convert_fusion
  5.9 0.1 pad_maximum_fusion
  6.0 0.1 copy.18
  6.1 1.6 %fusion.4 = bf16[1024,768]{1,0:T(8,128)(2,1)S(1)} fusion(bf16[768,768]{1,0:T(8,128)(2,1)S(1)} %bitcast.38, s32[1024]{0:T(1024)S(1)} %eq.41), kind=kOutput, calls=%fused_computation.10 | convolution fusion | flops 1209532416 | bytes 2756608 | tf_op jit(solution)/shard_map/dot_general | solution.py:43
  7.6 2.3 %reshape.147 = bf16[128,48,128]{2,1,0:T(8,128)(2,1)} reshape(bf16[1024,768]{1,0:T(8,128)(2,1)S(1)} %fusion.4) | data formatting | bytes 3145728 | tf_op jit(solution)/shard_map/reshape | solution.py:46
  9.9 0.0 copy-start
  9.9 0.0 copy-start.1
  9.9 15.6 %all-to-all-start = ((bf16[128,48,128]{2,1,0:T(8,128)(2,1)}), bf16[128,48,128]{2,1,0:T(8,128)(2,1)S(1)}, u32[]{:S(2)}, u32[]{:S(2)}) async-start(bf16[128,48,128]{2,1,0:T(8,128)(2,1)} %reshape.147), calls=%async_computation | async-start | bytes 3145728 | tf_op jit(solution)/shard_map/all_to_all | solution.py:47
  25.5 0.0 copy-done
  25.5 0.2 dynamic-slice_reduce_fusion
  25.7 0.0 copy-done.1
  25.7 0.1 compare_bitcast_fusion
  25.8 0.1 fusion.19
  25.9 41.0 %all-to-all-done = bf16[128,48,128]{2,1,0:T(8,128)(2,1)S(1)} async-done(((bf16[128,48,128]{2,1,0:T(8,128)(2,1)}), bf16[128,48,128]{2,1,0:T(8,128)(2,1)S(1)}, u32[]{:S(2)}, u32[]{:S(2)}) %all-to-all-start) | async-done | bytes 1572896 | tf_op jit(solution)/shard_map/all_to_all | solution.py:47
  66.9 0.4 copy.19
  67.3 1.6 %copy.20 = bf16[8,128,3,2,128]{4,3,2,1,0:T(2,128)(2,1)S(1)} copy(bf16[8,128,3,2,128]{4,1,2,3,0:T(8,128)(2,1)S(1)} %bitcast.37) | data formatting | bytes 3145728 | tf_op jit(solution)/shard_map/transpose | solution.py:52
  68.9 1.1 reshape.149
  70.0 4.2 %convolution_bitcast_fusion = bf16[8,768,256]{1,2,0:T(8,128)(2,1)S(1)} fusion(bf16[8,384,256]{2,1,0:T(8,128)(2,1)S(1)} %reshape.149, bf16[8,384,768]{2,1,0:T(8,128)(2,1)} %param.6), kind=kOutput, calls=%fused_computation.8 | convolution fusion | flops 1207959552 | bytes 9437184 | tf_op jit(solution)/shard_map/sjl,sjc->slc/dot_general | solution.py:53
  74.2 0.5 fusion.2
  74.7 1.2 %copy.23 = bf16[8,768,128]{2,0,1:T(8,128)(2,1)S(1)} copy(bf16[8,768,128]{1,2,0:T(8,128)(2,1)S(1)} %fusion.2) | data formatting | bytes 3145728 | tf_op jit(solution)/shard_map/convert_element_type | solution.py:58
  75.9 0.6 gather_fusion
  76.6 0.3 fusion.8
  76.8 0.1 collective-permute-start
  76.9 1.2 %collective-permute-done = bf16[64,128]{1,0:T(8,128)(2,1)S(1)} collective-permute-done((bf16[64,128]{1,0:T(8,128)(2,1)S(1)}, bf16[64,128]{1,0:T(8,128)(2,1)S(1)}, u32[]{:S(2)}, u32[]{:S(2)}) %collective-permute-start) | collective-permute-done | bytes 16416 | tf_op jit(solution)/shard_map/ppermute | solution.py:63
  78.1 1.5 %collective-permute-start.1 = (bf16[64,128]{1,0:T(8,128)(2,1)S(1)}, bf16[64,128]{1,0:T(8,128)(2,1)S(1)}, u32[]{:S(2)}, u32[]{:S(2)}) collective-permute-start(bf16[64,128]{1,0:T(8,128)(2,1)S(1)} %collective-permute-done), channel_id=1, source_target_pairs={{0,2},{2,0},{4,6},{6,4},{8,10},{10,8},{12,14},{14,12},{16,18},{18,... | collective-permute-start | bytes 49160 | tf_op jit(solution)/shard_map/ppermute | solution.py:20
  79.7 2.2 %collective-permute-done.1 = bf16[64,128]{1,0:T(8,128)(2,1)S(1)} collective-permute-done((bf16[64,128]{1,0:T(8,128)(2,1)S(1)}, bf16[64,128]{1,0:T(8,128)(2,1)S(1)}, u32[]{:S(2)}, u32[]{:S(2)}) %collective-permute-start.1) | collective-permute-done | bytes 16416 | tf_op jit(solution)/shard_map/ppermute | solution.py:20
  81.9 1.6 %collective-permute-start.2 = (bf16[64,128]{1,0:T(8,128)(2,1)S(1)}, bf16[64,128]{1,0:T(8,128)(2,1)S(1)}, u32[]{:S(2)}, u32[]{:S(2)}) collective-permute-start(bf16[64,128]{1,0:T(8,128)(2,1)S(1)} %add.66), channel_id=1, source_target_pairs={{0,4},{2,6},{4,0},{6,2},{8,12},{10,14},{12,8},{14,10},{16,20},{18,... | collective-permute-start | bytes 49160 | tf_op jit(solution)/shard_map/ppermute | solution.py:20
  83.4 3.8 %collective-permute-done.2 = bf16[64,128]{1,0:T(8,128)(2,1)S(1)} collective-permute-done((bf16[64,128]{1,0:T(8,128)(2,1)S(1)}, bf16[64,128]{1,0:T(8,128)(2,1)S(1)}, u32[]{:S(2)}, u32[]{:S(2)}) %collective-permute-start.2) | collective-permute-done | bytes 16416 | tf_op jit(solution)/shard_map/ppermute | solution.py:20
  87.2 0.8 collective-permute-start.3
  88.0 3.0 %collective-permute-done.3 = bf16[64,128]{1,0:T(8,128)(2,1)S(1)} collective-permute-done((bf16[64,128]{1,0:T(8,128)(2,1)S(1)}, bf16[64,128]{1,0:T(8,128)(2,1)S(1)}, u32[]{:S(2)}, u32[]{:S(2)}) %collective-permute-start.3) | collective-permute-done | bytes 16416 | tf_op jit(solution)/shard_map/ppermute | solution.py:20
  91.0 1.1 collective-permute-start.4
  92.2 4.2 %collective-permute-done.4 = bf16[64,128]{1,0:T(8,128)(2,1)S(1)} collective-permute-done((bf16[64,128]{1,0:T(8,128)(2,1)S(1)}, bf16[64,128]{1,0:T(8,128)(2,1)S(1)}, u32[]{:S(2)}, u32[]{:S(2)}) %collective-permute-start.4) | collective-permute-done | bytes 16416 | tf_op jit(solution)/shard_map/ppermute | solution.py:20
  96.4 1.7 %collective-permute-start.5 = (bf16[64,128]{1,0:T(8,128)(2,1)S(1)}, bf16[64,128]{1,0:T(8,128)(2,1)S(1)}, u32[]{:S(2)}, u32[]{:S(2)}) collective-permute-start(bf16[64,128]{1,0:T(8,128)(2,1)S(1)} %add.69), channel_id=1, source_target_pairs={{0,32},{2,34},{4,36},{6,38},{8,40},{10,42},{12,44},{14,46},{16,48}... | collective-permute-start | bytes 49160 | tf_op jit(solution)/shard_map/ppermute | solution.py:20
  98.0 2.2 %collective-permute-done.5 = bf16[64,128]{1,0:T(8,128)(2,1)S(1)} collective-permute-done((bf16[64,128]{1,0:T(8,128)(2,1)S(1)}, bf16[64,128]{1,0:T(8,128)(2,1)S(1)}, u32[]{:S(2)}, u32[]{:S(2)}) %collective-permute-start.5) | collective-permute-done | bytes 16416 | tf_op jit(solution)/shard_map/ppermute | solution.py:20
  100.2 1.2 %collective-permute-start.6 = (bf16[64,128]{1,0:T(8,128)(2,1)S(1)}, bf16[64,128]{1,0:T(8,128)(2,1)S(1)}, u32[]{:S(2)}, u32[]{:S(2)}) collective-permute-start(bf16[64,128]{1,0:T(8,128)(2,1)S(1)} %add.70), channel_id=1, source_target_pairs={{0,64},{2,66},{4,68},{6,70},{8,72},{10,74},{12,76},{14,78},{16,80}... | collective-permute-start | bytes 49160 | tf_op jit(solution)/shard_map/ppermute | solution.py:20
  101.4 3.6 %collective-permute-done.6 = bf16[64,128]{1,0:T(8,128)(2,1)S(1)} collective-permute-done((bf16[64,128]{1,0:T(8,128)(2,1)S(1)}, bf16[64,128]{1,0:T(8,128)(2,1)S(1)}, u32[]{:S(2)}, u32[]{:S(2)}) %collective-permute-start.6) | collective-permute-done | bytes 16416 | tf_op jit(solution)/shard_map/ppermute | solution.py:20
  105.0 0.7 collective-permute-start.7
  105.7 1.6 %copy.22 = bf16[8,768,128]{2,1,0:T(8,128)(2,1)} copy(bf16[8,768,128]{1,2,0:T(8,128)(2,1)S(1)} %fusion.2) | data formatting | bytes 3145728 | tf_op jit(solution)/shard_map/convert_element_type | solution.py:58
  107.2 3.9 %reshape.150 = bf16[12288,64]{1,0:T(8,128)(2,1)S(1)} reshape(bf16[8,768,128]{2,1,0:T(8,128)(2,1)} %copy.22) | data formatting | bytes 3145728 | tf_op jit(solution)/shard_map/reshape | solution.py:67
  111.1 1.5 %collective-permute-done.7 = bf16[64,128]{1,0:T(8,128)(2,1)S(1)} collective-permute-done((bf16[64,128]{1,0:T(8,128)(2,1)S(1)}, bf16[64,128]{1,0:T(8,128)(2,1)S(1)}, u32[]{:S(2)}, u32[]{:S(2)}) %collective-permute-start.7) | collective-permute-done | bytes 16416 | tf_op jit(solution)/shard_map/ppermute | solution.py:20
  112.7 0.1 reshape.151
  112.8 0.1 reduce_sum.9
  112.9 0.1 div.10
  113.0 0.1 sub.30
  113.2 0.1 sub.31
  113.3 0.1 convert_element_type.34
  113.4 2.7 %fusion = bf16[12288,128]{1,0:T(8,128)(2,1)} fusion(bf16[12288,64]{1,0:T(8,128)(2,1)S(1)} %reshape.150, bf16[128,64]{1,0:T(8,128)(2,1)S(1)} %convert_element_type.34), kind=kOutput, calls=%fused_computation.2 | convolution fusion | flops 204472320 | bytes 4734976 | tf_op jit(solution)/shard_map/dot_general | solution.py:68
  (15 shorter events, 0.1 us)
Async XLA Ops:
  9.9 15.6 %copy-start = (s32[128,8]{0,1:T(8,128)S(1)}, s32[128,8]{0,1:T(8,128)}, u32[]{:S(2)}) copy-start(s32[128,8]{0,1:T(8,128)} %param.7) | copy-start | bytes 12292
  9.9 15.8 %copy-start.1 = (s32[2,64]{1,0:T(2,128)S(1)}, s32[2,64]{1,0:T(2,128)}, u32[]{:S(2)}) copy-start(s32[2,64]{1,0:T(2,128)} %param.8) | copy-start | bytes 1540
  9.9 57.0 %all-to-all-start = ((bf16[128,48,128]{2,1,0:T(8,128)(2,1)}), bf16[128,48,128]{2,1,0:T(8,128)(2,1)S(1)}, u32[]{:S(2)}, u32[]{:S(2)}) async-start(bf16[128,48,128]{2,1,0:T(8,128)(2,1)} %reshape.147), calls=%async_computation | async-start | bytes 3145728 | tf_op jit(solution)/shard_map/all_to_all | solution.py:47
  76.8 1.3 %collective-permute-start = (bf16[64,128]{1,0:T(8,128)(2,1)S(1)}, bf16[64,128]{1,0:T(8,128)(2,1)S(1)}, u32[]{:S(2)}, u32[]{:S(2)}) collective-permute-start(bf16[64,128]{1,0:T(8,128)(2,1)S(1)} %convert_element_type.31), channel_id=1, source_target_pairs={{0,1},{1,0},{2,3},{3,2},{4,5},{5,4},{6,7},{7,6},{8,9},{9,8},{10,11... | collective-permute-start | bytes 49160 | tf_op jit(solution)/shard_map/ppermute | solution.py:63
  78.1 3.7 %collective-permute-start.1 = (bf16[64,128]{1,0:T(8,128)(2,1)S(1)}, bf16[64,128]{1,0:T(8,128)(2,1)S(1)}, u32[]{:S(2)}, u32[]{:S(2)}) collective-permute-start(bf16[64,128]{1,0:T(8,128)(2,1)S(1)} %collective-permute-done), channel_id=1, source_target_pairs={{0,2},{2,0},{4,6},{6,4},{8,10},{10,8},{12,14},{14,12},{16,18},{18,... | collective-permute-start | bytes 49160 | tf_op jit(solution)/shard_map/ppermute | solution.py:20
  81.9 5.3 %collective-permute-start.2 = (bf16[64,128]{1,0:T(8,128)(2,1)S(1)}, bf16[64,128]{1,0:T(8,128)(2,1)S(1)}, u32[]{:S(2)}, u32[]{:S(2)}) collective-permute-start(bf16[64,128]{1,0:T(8,128)(2,1)S(1)} %add.66), channel_id=1, source_target_pairs={{0,4},{2,6},{4,0},{6,2},{8,12},{10,14},{12,8},{14,10},{16,20},{18,... | collective-permute-start | bytes 49160 | tf_op jit(solution)/shard_map/ppermute | solution.py:20
  87.2 3.8 %collective-permute-start.3 = (bf16[64,128]{1,0:T(8,128)(2,1)S(1)}, bf16[64,128]{1,0:T(8,128)(2,1)S(1)}, u32[]{:S(2)}, u32[]{:S(2)}) collective-permute-start(bf16[64,128]{1,0:T(8,128)(2,1)S(1)} %add.67), channel_id=1, source_target_pairs={{0,8},{2,10},{4,12},{6,14},{8,0},{10,2},{12,4},{14,6},{16,24},{18,... | collective-permute-start | bytes 49160 | tf_op jit(solution)/shard_map/ppermute | solution.py:20
  91.0 5.3 %collective-permute-start.4 = (bf16[64,128]{1,0:T(8,128)(2,1)S(1)}, bf16[64,128]{1,0:T(8,128)(2,1)S(1)}, u32[]{:S(2)}, u32[]{:S(2)}) collective-permute-start(bf16[64,128]{1,0:T(8,128)(2,1)S(1)} %add.68), channel_id=1, source_target_pairs={{0,16},{2,18},{4,20},{6,22},{8,24},{10,26},{12,28},{14,30},{16,0},... | collective-permute-start | bytes 49160 | tf_op jit(solution)/shard_map/ppermute | solution.py:20
  96.4 3.8 %collective-permute-start.5 = (bf16[64,128]{1,0:T(8,128)(2,1)S(1)}, bf16[64,128]{1,0:T(8,128)(2,1)S(1)}, u32[]{:S(2)}, u32[]{:S(2)}) collective-permute-start(bf16[64,128]{1,0:T(8,128)(2,1)S(1)} %add.69), channel_id=1, source_target_pairs={{0,32},{2,34},{4,36},{6,38},{8,40},{10,42},{12,44},{14,46},{16,48}... | collective-permute-start | bytes 49160 | tf_op jit(solution)/shard_map/ppermute | solution.py:20
  100.2 4.7 %collective-permute-start.6 = (bf16[64,128]{1,0:T(8,128)(2,1)S(1)}, bf16[64,128]{1,0:T(8,128)(2,1)S(1)}, u32[]{:S(2)}, u32[]{:S(2)}) collective-permute-start(bf16[64,128]{1,0:T(8,128)(2,1)S(1)} %add.70), channel_id=1, source_target_pairs={{0,64},{2,66},{4,68},{6,70},{8,72},{10,74},{12,76},{14,78},{16,80}... | collective-permute-start | bytes 49160 | tf_op jit(solution)/shard_map/ppermute | solution.py:20
  105.0 7.7 %collective-permute-start.7 = (bf16[64,128]{1,0:T(8,128)(2,1)S(1)}, bf16[64,128]{1,0:T(8,128)(2,1)S(1)}, u32[]{:S(2)}, u32[]{:S(2)}) collective-permute-start(bf16[64,128]{1,0:T(8,128)(2,1)S(1)} %add.71), channel_id=1, source_target_pairs={{0,128},{2,130},{4,132},{6,134},{8,136},{10,138},{12,140},{14,142}... | collective-permute-start | bytes 49160 | tf_op jit(solution)/shard_map/ppermute | solution.py:20

commit v2 on v1

v2 whole, which is shorter than its diff:
```python
import math

import jax
import jax.numpy as jnp
import numpy as np
from jax import lax
from jax.experimental import pallas as pl
from jax.experimental.pallas import tpu as pltpu
from jax.sharding import PartitionSpec as P


def dft_table(lon_count, order_count):
    products = np.arange(lon_count)[:, None] * np.arange(order_count)[None, :] % lon_count
    angles = products * (2.0 * math.pi / lon_count)
    return np.stack([np.cos(angles), -np.sin(angles)], axis=1).astype(jnp.bfloat16)


def summed_other_field(block):
    count = lax.axis_size("lat")
    both = ("lat", "field")
    near = [(2 * i + f, 2 * i + 1 - f) for i in range(count) for f in range(2)]
    far = [(2 * i + f, 2 * (i ^ 1) + 1 - f) for i in range(count) for f in range(2)]
    block = lax.ppermute(block, both, near) + lax.ppermute(block, both, far)
    reach = 2
    while reach < count:
        block = block + lax.ppermute(block, "lat", [(i, i ^ reach) for i in range(count)])
        reach *= 2
    return block


def coefficient_kernel(orders_ref, parts_ref, place_ref, basis_ref, out_ref):
    order = orders_ref[pl.program_id(0)]
    wide = 2 * parts_ref.shape[3]
    pairs, degrees = basis_ref.shape[1], basis_ref.shape[2]
    parts = parts_ref[:, 0].reshape(2, pairs, wide // 2)
    by_pair = [
        lax.dot_general(
            parts[k], place_ref[...], (((0,), (0,)), ((), ())), preferred_element_type=jnp.float32
        ).astype(jnp.bfloat16)
        for k in range(2)
    ]
    both = jnp.dot(
        jnp.concatenate(by_pair, axis=0), basis_ref[0], preferred_element_type=jnp.float32
    )
    degree = lax.broadcasted_iota(jnp.int32, (1, degrees), 1)
    odd = ((degree - order) & 1) == 1
    keep = (degree >= order) & (order >= 0)
    chosen = jnp.where(odd, both[wide // 2 :], both[: wide // 2])
    out_ref[0] = jnp.where(keep, chosen, 0.0).astype(jnp.bfloat16)


def panel_kernel(coef_ref, centered_ref, out_ref, rows_ref, *, scale):
    degrees = coef_ref.shape[2]
    values = lax.dot_general(
        coef_ref[0], centered_ref[...], (((0,), (0,)), ((), ())), preferred_element_type=jnp.float32
    )
    values = values * scale
    half = values.shape[1] // 2
    rows_ref[pl.ds(0, degrees, stride=2), :] = values[:, :half]
    rows_ref[pl.ds(1, degrees, stride=2), :] = values[:, half:]
    out_ref[0, 0] = rows_ref[...].astype(jnp.bfloat16)


def local(fields_grid, basis, order_table, panel_modes):
    grid_one = fields_grid[0]
    snap_count, _, pair_count, lon_count = grid_one.shape
    group_count, slot_count = order_table.shape
    pair_total, deg_count = basis.shape[1], basis.shape[2]
    mode_count = panel_modes.shape[1]
    order_count = lon_count // 2
    wide = 2 * snap_count
    orders = order_table.reshape(-1)
    mode_order, mode_degree = panel_modes[0], panel_modes[1]
    group_index = lax.axis_index("lat")
    my_orders = lax.dynamic_slice_in_dim(order_table, group_index, 1, 0)[0]

    owned = my_orders[:, None] == mode_order[None, :]
    degree = lax.broadcasted_iota(jnp.int32, (1, deg_count, 1), 1)
    pick = (owned[:, None, :] & (degree == mode_degree[None, None, :])).astype(jnp.bfloat16)
    columns = jnp.einsum("sjl,slc->sjc", basis, pick, preferred_element_type=jnp.float32)
    columns = jnp.sum(columns, axis=0).astype(jnp.bfloat16)
    columns = columns.reshape(group_count, 1, pair_count * mode_count)
    columns = lax.all_to_all(columns, "lat", split_axis=0, concat_axis=0, tiled=True)
    columns = jnp.sum(columns.astype(jnp.float32), axis=(0, 1)).reshape(pair_count, mode_count)

    table = jnp.asarray(dft_table(lon_count, order_count))
    fourier = jnp.einsum("thjn,nrm->hjrtm", grid_one, table, preferred_element_type=jnp.float32)
    fourier = fourier * (1.0 / math.sqrt(lon_count))
    parts = jnp.stack([fourier[0] + fourier[1], fourier[0] - fourier[1]]).astype(jnp.bfloat16)
    parts = parts.reshape(2 * pair_count * wide, order_count)
    wanted = jnp.concatenate([orders, mode_order])
    placed = (wanted[:, None] == lax.broadcasted_iota(jnp.int32, (1, order_count), 1)).astype(
        jnp.bfloat16
    )
    sent = lax.dot_general(
        placed, parts, (((1,), (1,)), ((), ())), preferred_element_type=jnp.float32
    ).astype(jnp.bfloat16)
    mode_parts = sent[group_count * slot_count :].reshape(mode_count, 2, pair_count, wide)
    sent = sent[: group_count * slot_count]
    sent = sent.reshape(group_count, slot_count, 2 * pair_count, wide).transpose(0, 2, 1, 3)
    sent = sent.reshape(group_count, 2 * pair_count * slot_count, wide)
    received = lax.all_to_all(sent, "lat", split_axis=0, concat_axis=0, tiled=True)

    mode_odd = ((mode_degree - mode_order) % 2 == 1)[:, None, None]
    mode_side = jnp.where(mode_odd, mode_parts[:, 1], mode_parts[:, 0]).astype(jnp.float32)
    share = jnp.sum(mode_side * columns.T[:, :, None], axis=1)
    values = summed_other_field(share).astype(jnp.bfloat16).astype(jnp.float32)
    values = values.reshape(2 * mode_count, snap_count)
    centered = (values - jnp.mean(values, axis=1, keepdims=True)).astype(jnp.bfloat16).T
    blank = jnp.zeros_like(centered)
    centered = jnp.concatenate(
        [jnp.concatenate([centered, blank], 1), jnp.concatenate([blank, centered], 1)], 0
    )

    parts_in = received.transpose(1, 0, 2).reshape(2 * pair_count, slot_count, group_count, wide)
    source = lax.broadcasted_iota(jnp.int32, (pair_total, 1), 0)
    place = (
        pair_count * (source % group_count) + source // group_count
        == lax.broadcasted_iota(jnp.int32, (1, pair_total), 1)
    ).astype(jnp.bfloat16)
    coefficients = pl.pallas_call(
        coefficient_kernel,
        grid_spec=pltpu.PrefetchScalarGridSpec(
            num_scalar_prefetch=1,
            grid=(slot_count,),
            in_specs=[
                pl.BlockSpec((2 * pair_count, 1, group_count, wide), lambda s, o: (0, s, 0, 0)),
                pl.BlockSpec((pair_total, pair_total), lambda s, o: (0, 0)),
                pl.BlockSpec((1, pair_total, deg_count), lambda s, o: (s, 0, 0)),
            ],
            out_specs=pl.BlockSpec((1, wide, deg_count), lambda s, o: (s, 0, 0)),
        ),
        out_shape=jax.ShapeDtypeStruct((slot_count, wide, deg_count), jnp.bfloat16),
        name="coefficients",
    )(my_orders, parts_in, place, basis)
    return pl.pallas_call(
        lambda *refs: panel_kernel(*refs, scale=1.0 / (snap_count - 1)),
        grid=(slot_count,),
        in_specs=[
            pl.BlockSpec((1, wide, deg_count), lambda s: (s, 0, 0)),
            pl.BlockSpec((wide, 4 * mode_count), lambda s: (0, 0)),
        ],
        out_specs=pl.BlockSpec((1, 1, 2 * deg_count, 2 * mode_count), lambda s: (0, s, 0, 0)),
        scratch_shapes=[pltpu.VMEM((2 * deg_count, 2 * mode_count), jnp.float32)],
        out_shape=jax.ShapeDtypeStruct((1, slot_count, 2 * deg_count, 2 * mode_count), jnp.bfloat16),
        name="panel",
    )(coefficients, centered)


def solution(mesh):
    placed = (P("field", None, None, "lat", None), P("lat", None, None), P(), P())
    return jax.shard_map(
        local, mesh=mesh, in_specs=placed, out_specs=P("field", "lat", None, None), check_vma=False
    )
```

time: 117 us -> 111 us (0.949)
  waiting for transfers between devices: 62.6 us -> 34 us
  starting transfers between devices: 24.2 us -> 41.1 us
  Pallas kernels: 0 us -> 16.3 us
  local copies, waits for them, and re-layouts: 14.3 us -> 5.98 us
  matrix products: 13.4 us -> 9.95 us
  other arithmetic: 1.3 us -> 2.63 us
    all_to_all x1, waiting for transfers between devices: 41 us -> 0.01 us  [local(): lax.all_to_all(sent, 'lat', split_axis=0, concat_axis=0, tiled=True)]
    pallas_call x0 -> x2, Pallas kernels: none -> 16.3 us  [the longest x1 9.46 us: local(): pl.pallas_call(coefficient_kernel, grid_spec=pltpu.PrefetchScalarGridSpec...]
    all_to_all x0 -> x1, starting transfers between devices: none -> 15.4 us  [local(): lax.all_to_all(columns, 'lat', split_axis=0, concat_axis=0, tiled=True)]
    ppermute x8, waiting for transfers between devices: 21.6 us -> 30.1 us  [the longest x6 27.4 us: summed_other_field(): lax.ppermute(block, 'lat', [(i, i ^ reach) for i in range(count)])]
    ppermute x8, starting transfers between devices: 8.68 us -> 15.7 us  [the longest x6 14.6 us: summed_other_field(): lax.ppermute(block, 'lat', [(i, i ^ reach) for i in range(count)])]
    all_to_all x1, starting transfers between devices: 15.6 us -> 10 us  [local(): lax.all_to_all(sent, 'lat', split_axis=0, concat_axis=0, tiled=True)]
    reshape x4 -> x7, local copies, waits for them, and re-layouts: 7.31 us -> 2.37 us  [the longest x1 1.24 us: local(): sent = sent.reshape(group_count, 2 * pair_count * slot_count, wide)]
    all_to_all x0 -> x1, waiting for transfers between devices: none -> 3.88 us  [local(): lax.all_to_all(columns, 'lat', split_axis=0, concat_axis=0, tiled=True)]
  transfers between devices with their start and end apart: 9 -> 10, of which waited for: 9 -> 8; matrix products, arithmetic and copies ran while one was open for 5% -> 9% of each run, Pallas kernels for 0% -> 0%
where the time goes in v2:
time: 111 us; the launch traced here: 110 us
  starting transfers between devices  41.1 us (37%)
  waiting for transfers between devices  34 us (31%)
  Pallas kernels  16.3 us (15%)
  matrix products  9.95 us (9%)
  local copies, waits for them, and re-layouts  5.98 us (5%)
  other arithmetic  2.63 us (2%)
    ppermute x6, waiting for transfers between devices, summed_other_field(): lax.ppermute(block, 'lat', [(i, i ^ reach) for i in range(count)])  27.4 us
    all_to_all x1, starting transfers between devices, local(): lax.all_to_all(columns, 'lat', split_axis=0, concat_axis=0, tiled=True)  15.4 us
    ppermute x6, starting transfers between devices, summed_other_field(): lax.ppermute(block, 'lat', [(i, i ^ reach) for i in range(count)])  14.6 us
    all_to_all x1, starting transfers between devices, local(): lax.all_to_all(sent, 'lat', split_axis=0, concat_axis=0, tiled=True)  10 us
    pallas_call x1, Pallas kernels, local(): pl.pallas_call(coefficient_kernel, grid_spec=pltpu.PrefetchScalarGridSpec...  9.46 us
    pallas_call x1, Pallas kernels, local(): pl.pallas_call(lambda *refs: panel_kernel(*refs, scale=1.0 / (snap_count...  6.88 us
    dot_general x1, matrix products, local(): jnp.einsum('thjn,nrm->hjrtm', grid_one, table, preferred_element_type=jnp...  4.35 us
    dot_general x1, matrix products, local(): jnp.einsum('sjl,slc->sjc', basis, pick, preferred_element_type=jnp.float32)  3.97 us
  transfers between devices with their start and end apart: 10, of which 8 were waited for; matrix products, arithmetic and copies ran while one was open for 9% of the time, Pallas kernels for 0%

profile of v2, /device:TPU:2, one launch (start us, length us, event | category | flops | bytes accessed | tf_op | source)
XLA Modules:
  0.0 110.2 jit_solution(15232567551257167128)
XLA Ops:
  0.0 0.8 slice_bitcast_fusion.3
  0.8 0.1 iota_compare_fusion.3
  0.9 0.9 dynamic-slice_reduce_fusion.orders_ref
  1.7 0.0 copy-start.1
  1.7 0.1 broadcast_compare_fusion
  1.8 0.0 copy-start
  1.8 0.0 copy-start.3
  1.8 4.0 %fusion.11 = bf16[384,64]{0,1:T(8,128)(2,1)S(1)} fusion(bf16[8,384,768]{2,1,0:T(8,128)(2,1)} %basis_ref.1, pred[768,64]{0,1:T(8,128)(4,1)S(1)} %iota_compare_fusion.3, pred[8,64]{1,0:T(8,128)(4,1)S(1)} %broadcast_compare_fusion), kind=kOutput, calls=%fused_computation.14 | convolution fusion | flops 302407680 | bytes 4817408 | tf_op jit(solution)/shard_map/sjl,slc->sjc/dot_general | solution.py:80
  5.8 0.0 copy-done.1
  5.8 0.1 copy.22
  5.9 0.8 reshape.180
  6.7 15.4 %all-to-all-start.1 = ((bf16[128,1,192]{2,1,0:T(2,128)(2,1)}), bf16[128,1,192]{2,1,0:T(2,128)(2,1)S(1)}, u32[]{:S(2)}, u32[]{:S(2)}) async-start(bf16[128,1,192]{2,1,0:T(2,128)(2,1)} %reshape.180), calls=%async_computation.1 | async-start | bytes 262144 | tf_op jit(solution)/shard_map/all_to_all | solution.py:83
  22.1 0.0 copy-done
  22.1 0.1 copy.17
  22.2 0.1 reshape.166
  22.3 0.0 copy-done.3
  22.4 4.3 %multiply_bitcast_fusion = f32[2,3,2,64,768]{4,3,1,0,2:T(8,128)S(1)} fusion(bf16[1536,2,768,1,1]{2,0,4,3,1:T(8,128)(2,1)} %constant.72, bf16[64,2,3,1536]{3,1,2,0:T(2,128)(2,1)S(1)} %bitcast.56), kind=kOutput, calls=%fused_computation.2 | convolution fusion | flops 1812529152 | bytes 8257536 | tf_op jit(solution)/shard_map/thjn,nrm->hjrtm/dot_general | solution.py:87
  26.7 0.3 add_convert_fusion
  27.0 0.1 pad_maximum_fusion
  27.1 0.1 copy.19
  27.2 1.6 %convolution_convert_fusion = bf16[1088,768]{1,0:T(8,128)(2,1)S(1)} fusion(bf16[768,768]{1,0:T(8,128)(2,1)S(1)} %bitcast.54, s32[1088]{0:T(1024)S(1)} %pad_add_fusion), kind=kOutput, calls=%fused_computation | convolution fusion | flops 1285128192 | bytes 2855168 | tf_op jit(solution)/shard_map/dot_general | solution.py:95
  28.8 1.2 %slice_bitcast_fusion = bf16[128,48,128]{2,1,0:T(8,128)(2,1)} fusion(bf16[1088,768]{1,0:T(8,128)(2,1)S(1)} %convolution_convert_fusion), kind=kLoop, calls=%fused_computation.4 | loop fusion | bytes 3145728 | tf_op jit(solution)/shard_map/reshape | solution.py:101
  30.1 0.0 copy-start.2
  30.1 3.9 %all-to-all-done.1 = bf16[128,1,192]{2,1,0:T(2,128)(2,1)S(1)} async-done(((bf16[128,1,192]{2,1,0:T(2,128)(2,1)}), bf16[128,1,192]{2,1,0:T(2,128)(2,1)S(1)}, u32[]{:S(2)}, u32[]{:S(2)}) %all-to-all-start.1) | async-done | bytes 49184 | tf_op jit(solution)/shard_map/all_to_all | solution.py:83
  34.0 10.0 %all-to-all-start = ((bf16[128,48,128]{2,1,0:T(8,128)(2,1)}), bf16[128,48,128]{2,1,0:T(8,128)(2,1)S(1)}, u32[]{:S(2)}, u32[]{:S(2)}) async-start(bf16[128,48,128]{2,1,0:T(8,128)(2,1)} %slice_bitcast_fusion), calls=%async_computation | async-start | bytes 3145728 | tf_op jit(solution)/shard_map/all_to_all | solution.py:102
  44.0 0.0 copy-done.2
  44.1 0.2 convert_reduce_fusion
  44.3 0.1 reshape.172
  44.4 0.1 copy.24
  44.5 0.2 multiply_reduce_fusion
  44.7 0.1 collective-permute-start.1
  44.8 1.0 collective-permute-start
  45.8 2.8 %collective-permute-done.1 = f32[64,128]{1,0:T(8,128)S(1)} collective-permute-done((f32[64,128]{1,0:T(8,128)S(1)}, f32[64,128]{1,0:T(8,128)S(1)}, u32[]{:S(2)}, u32[]{:S(2)}) %collective-permute-start.1) | collective-permute-done | bytes 32800 | tf_op jit(solution)/shard_map/ppermute | solution.py:23
  48.5 0.0 collective-permute-done
  48.5 2.1 %collective-permute-start.2 = (f32[64,128]{1,0:T(8,128)S(1)}, f32[64,128]{1,0:T(8,128)S(1)}, u32[]{:S(2)}, u32[]{:S(2)}) collective-permute-start(f32[64,128]{1,0:T(8,128)S(1)} %add.72), channel_id=1, source_target_pairs={{0,4},{2,6},{4,0},{6,2},{8,12},{10,14},{12,8},{14,10},{16,20},{18,... | collective-permute-start | bytes 98312 | tf_op jit(solution)/shard_map/ppermute | solution.py:26
  50.7 3.9 %collective-permute-done.2 = f32[64,128]{1,0:T(8,128)S(1)} collective-permute-done((f32[64,128]{1,0:T(8,128)S(1)}, f32[64,128]{1,0:T(8,128)S(1)}, u32[]{:S(2)}, u32[]{:S(2)}) %collective-permute-start.2) | collective-permute-done | bytes 32800 | tf_op jit(solution)/shard_map/ppermute | solution.py:26
  54.5 1.8 %collective-permute-start.3 = (f32[64,128]{1,0:T(8,128)S(1)}, f32[64,128]{1,0:T(8,128)S(1)}, u32[]{:S(2)}, u32[]{:S(2)}) collective-permute-start(f32[64,128]{1,0:T(8,128)S(1)} %add.73), channel_id=1, source_target_pairs={{0,8},{2,10},{4,12},{6,14},{8,0},{10,2},{12,4},{14,6},{16,24},{18,... | collective-permute-start | bytes 98312 | tf_op jit(solution)/shard_map/ppermute | solution.py:26
  56.3 2.2 %collective-permute-done.3 = f32[64,128]{1,0:T(8,128)S(1)} collective-permute-done((f32[64,128]{1,0:T(8,128)S(1)}, f32[64,128]{1,0:T(8,128)S(1)}, u32[]{:S(2)}, u32[]{:S(2)}) %collective-permute-start.3) | collective-permute-done | bytes 32800 | tf_op jit(solution)/shard_map/ppermute | solution.py:26
  58.5 2.7 %collective-permute-start.4 = (f32[64,128]{1,0:T(8,128)S(1)}, f32[64,128]{1,0:T(8,128)S(1)}, u32[]{:S(2)}, u32[]{:S(2)}) collective-permute-start(f32[64,128]{1,0:T(8,128)S(1)} %add.74), channel_id=1, source_target_pairs={{0,16},{2,18},{4,20},{6,22},{8,24},{10,26},{12,28},{14,30},{16,0},... | collective-permute-start | bytes 98312 | tf_op jit(solution)/shard_map/ppermute | solution.py:26
  61.2 3.3 %collective-permute-done.4 = f32[64,128]{1,0:T(8,128)S(1)} collective-permute-done((f32[64,128]{1,0:T(8,128)S(1)}, f32[64,128]{1,0:T(8,128)S(1)}, u32[]{:S(2)}, u32[]{:S(2)}) %collective-permute-start.4) | collective-permute-done | bytes 32800 | tf_op jit(solution)/shard_map/ppermute | solution.py:26
  64.5 2.1 %collective-permute-start.5 = (f32[64,128]{1,0:T(8,128)S(1)}, f32[64,128]{1,0:T(8,128)S(1)}, u32[]{:S(2)}, u32[]{:S(2)}) collective-permute-start(f32[64,128]{1,0:T(8,128)S(1)} %add.75), channel_id=1, source_target_pairs={{0,32},{2,34},{4,36},{6,38},{8,40},{10,42},{12,44},{14,46},{16,48}... | collective-permute-start | bytes 98312 | tf_op jit(solution)/shard_map/ppermute | solution.py:26
  66.6 12.2 %collective-permute-done.5 = f32[64,128]{1,0:T(8,128)S(1)} collective-permute-done((f32[64,128]{1,0:T(8,128)S(1)}, f32[64,128]{1,0:T(8,128)S(1)}, u32[]{:S(2)}, u32[]{:S(2)}) %collective-permute-start.5) | collective-permute-done | bytes 32800 | tf_op jit(solution)/shard_map/ppermute | solution.py:26
  78.8 1.1 collective-permute-start.6
  79.8 3.7 %collective-permute-done.6 = f32[64,128]{1,0:T(8,128)S(1)} collective-permute-done((f32[64,128]{1,0:T(8,128)S(1)}, f32[64,128]{1,0:T(8,128)S(1)}, u32[]{:S(2)}, u32[]{:S(2)}) %collective-permute-start.6) | collective-permute-done | bytes 32800 | tf_op jit(solution)/shard_map/ppermute | solution.py:26
  83.6 4.9 %collective-permute-start.7 = (f32[64,128]{1,0:T(8,128)S(1)}, f32[64,128]{1,0:T(8,128)S(1)}, u32[]{:S(2)}, u32[]{:S(2)}) collective-permute-start(f32[64,128]{1,0:T(8,128)S(1)} %add.77), channel_id=1, source_target_pairs={{0,128},{2,130},{4,132},{6,134},{8,136},{10,138},{12,140},{14,142}... | collective-permute-start | bytes 98312 | tf_op jit(solution)/shard_map/ppermute | solution.py:26
  88.5 0.8 fusion.16.place_ref
  89.3 2.1 %collective-permute-done.7 = f32[64,128]{1,0:T(8,128)S(1)} collective-permute-done((f32[64,128]{1,0:T(8,128)S(1)}, f32[64,128]{1,0:T(8,128)S(1)}, u32[]{:S(2)}, u32[]{:S(2)}) %collective-permute-start.7) | collective-permute-done | bytes 32800 | tf_op jit(solution)/shard_map/ppermute | solution.py:26
  91.4 0.1 reshape.176
  91.5 0.1 copy.25
  91.5 0.1 reduce_sum.33
  91.7 0.6 fusion.19.refs_1_
  92.3 0.0 all-to-all-done
  92.3 1.6 %copy.20 = bf16[48,128,128]{2,1,0:T(8,128)(2,1)} copy(bf16[48,128,128]{2,0,1:T(8,128)(2,1)S(1)} %bitcast.52) | data formatting | bytes 3145728 | tf_op jit(solution)/shard_map/transpose | solution.py:115
  93.9 9.5 %coefficients.1.refs_0_ = bf16[8,128,768]{2,1,0:T(8,128)(2,1)} custom-call(s32[8]{0:T(128)} %copy-done.1, bf16[6,8,128,128]{3,2,1,0:T(8,128)(2,1)} %bitcast.53, bf16[384,384]{1,0:T(8,128)(2,1)} %fusion.16.place_ref, bf16[8,384,768]{2,1,0:T(8,128)(2,1)} %basis_ref.1), custom_call_target="tpu_custom_call" | custom-call | tf_op jit(solution)/shard_map/coefficients/pallas_call | solution.py:121
  103.4 6.9 %panel.1 = bf16[1,8,1536,128]{3,2,1,0:T(8,128)(2,1)} custom-call(bf16[8,128,768]{2,1,0:T(8,128)(2,1)} %coefficients.1.refs_0_, bf16[128,256]{1,0:T(8,128)(2,1)} %fusion.19.refs_1_), custom_call_target="tpu_custom_call" | custom-call | tf_op jit(solution)/shard_map/panel/pallas_call | solution.py:136
  (14 shorter events, 0.1 us)
Async XLA Ops:
  1.7 4.1 %copy-start.1 = (s32[8]{0:T(128)}, s32[8]{0:T(128)S(1)}, u32[]{:S(2)}) copy-start(s32[8]{0:T(128)S(1)} %dynamic-slice_reduce_fusion.orders_ref) | copy-start | bytes 100
  1.8 20.3 %copy-start = (s32[128,8]{0,1:T(8,128)S(1)}, s32[128,8]{0,1:T(8,128)}, u32[]{:S(2)}) copy-start(s32[128,8]{0,1:T(8,128)} %param.7) | copy-start | bytes 12292
  1.8 20.5 %copy-start.3 = (bf16[1,64,2,3,1536]{4,2,3,1,0:T(2,128)(2,1)S(1)}, bf16[1,64,2,3,1536]{4,2,3,1,0:T(2,128)(2,1)}, u32[]{:S(2)}) copy-start(bf16[1,64,2,3,1536]{4,2,3,1,0:T(2,128)(2,1)} %param.5) | copy-start | bytes 3538948
  6.7 27.3 %all-to-all-start.1 = ((bf16[128,1,192]{2,1,0:T(2,128)(2,1)}), bf16[128,1,192]{2,1,0:T(2,128)(2,1)S(1)}, u32[]{:S(2)}, u32[]{:S(2)}) async-start(bf16[128,1,192]{2,1,0:T(2,128)(2,1)} %reshape.180), calls=%async_computation.1 | async-start | bytes 262144 | tf_op jit(solution)/shard_map/all_to_all | solution.py:83
  30.1 14.0 %copy-start.2 = (s32[2,64]{1,0:T(2,128)S(1)}, s32[2,64]{1,0:T(2,128)}, u32[]{:S(2)}) copy-start(s32[2,64]{1,0:T(2,128)} %param.8) | copy-start | bytes 1540
  34.0 58.4 %all-to-all-start = ((bf16[128,48,128]{2,1,0:T(8,128)(2,1)}), bf16[128,48,128]{2,1,0:T(8,128)(2,1)S(1)}, u32[]{:S(2)}, u32[]{:S(2)}) async-start(bf16[128,48,128]{2,1,0:T(8,128)(2,1)} %slice_bitcast_fusion), calls=%async_computation | async-start | bytes 3145728 | tf_op jit(solution)/shard_map/all_to_all | solution.py:102
  44.7 3.9 %collective-permute-start.1 = (f32[64,128]{1,0:T(8,128)S(1)}, f32[64,128]{1,0:T(8,128)S(1)}, u32[]{:S(2)}, u32[]{:S(2)}) collective-permute-start(f32[64,128]{1,0:T(8,128)S(1)} %multiply_reduce_fusion), channel_id=1, source_target_pairs={{0,3},{1,2},{2,1},{3,0},{4,7},{5,6},{6,5},{7,4},{8,11},{9,10},{10,... | collective-permute-start | bytes 98312 | tf_op jit(solution)/shard_map/ppermute | solution.py:23
  44.8 3.8 %collective-permute-start = (f32[64,128]{1,0:T(8,128)S(1)}, f32[64,128]{1,0:T(8,128)S(1)}, u32[]{:S(2)}, u32[]{:S(2)}) collective-permute-start(f32[64,128]{1,0:T(8,128)S(1)} %multiply_reduce_fusion), channel_id=1, source_target_pairs={{0,1},{1,0},{2,3},{3,2},{4,5},{5,4},{6,7},{7,6},{8,9},{9,8},{10,11... | collective-permute-start | bytes 98312 | tf_op jit(solution)/shard_map/ppermute | solution.py:23
  48.5 6.0 %collective-permute-start.2 = (f32[64,128]{1,0:T(8,128)S(1)}, f32[64,128]{1,0:T(8,128)S(1)}, u32[]{:S(2)}, u32[]{:S(2)}) collective-permute-start(f32[64,128]{1,0:T(8,128)S(1)} %add.72), channel_id=1, source_target_pairs={{0,4},{2,6},{4,0},{6,2},{8,12},{10,14},{12,8},{14,10},{16,20},{18,... | collective-permute-start | bytes 98312 | tf_op jit(solution)/shard_map/ppermute | solution.py:26
  54.5 4.0 %collective-permute-start.3 = (f32[64,128]{1,0:T(8,128)S(1)}, f32[64,128]{1,0:T(8,128)S(1)}, u32[]{:S(2)}, u32[]{:S(2)}) collective-permute-start(f32[64,128]{1,0:T(8,128)S(1)} %add.73), channel_id=1, source_target_pairs={{0,8},{2,10},{4,12},{6,14},{8,0},{10,2},{12,4},{14,6},{16,24},{18,... | collective-permute-start | bytes 98312 | tf_op jit(solution)/shard_map/ppermute | solution.py:26
  58.5 5.9 %collective-permute-start.4 = (f32[64,128]{1,0:T(8,128)S(1)}, f32[64,128]{1,0:T(8,128)S(1)}, u32[]{:S(2)}, u32[]{:S(2)}) collective-permute-start(f32[64,128]{1,0:T(8,128)S(1)} %add.74), channel_id=1, source_target_pairs={{0,16},{2,18},{4,20},{6,22},{8,24},{10,26},{12,28},{14,30},{16,0},... | collective-permute-start | bytes 98312 | tf_op jit(solution)/shard_map/ppermute | solution.py:26
  64.5 14.3 %collective-permute-start.5 = (f32[64,128]{1,0:T(8,128)S(1)}, f32[64,128]{1,0:T(8,128)S(1)}, u32[]{:S(2)}, u32[]{:S(2)}) collective-permute-start(f32[64,128]{1,0:T(8,128)S(1)} %add.75), channel_id=1, source_target_pairs={{0,32},{2,34},{4,36},{6,38},{8,40},{10,42},{12,44},{14,46},{16,48}... | collective-permute-start | bytes 98312 | tf_op jit(solution)/shard_map/ppermute | solution.py:26
  78.8 4.8 %collective-permute-start.6 = (f32[64,128]{1,0:T(8,128)S(1)}, f32[64,128]{1,0:T(8,128)S(1)}, u32[]{:S(2)}, u32[]{:S(2)}) collective-permute-start(f32[64,128]{1,0:T(8,128)S(1)} %add.76), channel_id=1, source_target_pairs={{0,64},{2,66},{4,68},{6,70},{8,72},{10,74},{12,76},{14,78},{16,80}... | collective-permute-start | bytes 98312 | tf_op jit(solution)/shard_map/ppermute | solution.py:26
  83.6 7.8 %collective-permute-start.7 = (f32[64,128]{1,0:T(8,128)S(1)}, f32[64,128]{1,0:T(8,128)S(1)}, u32[]{:S(2)}, u32[]{:S(2)}) collective-permute-start(f32[64,128]{1,0:T(8,128)S(1)} %add.77), channel_id=1, source_target_pairs={{0,128},{2,130},{4,132},{6,134},{8,136},{10,138},{12,140},{14,142}... | collective-permute-start | bytes 98312 | tf_op jit(solution)/shard_map/ppermute | solution.py:26

commit v3 on v1

v3 whole, which is shorter than its diff:
```python
import functools
import math

import jax
import jax.numpy as jnp
import numpy as np
from jax import lax
from jax.experimental import pallas as pl
from jax.experimental.pallas import tpu as pltpu
from jax.sharding import PartitionSpec as P


def dft_table(lon_count, order_count):
    products = np.arange(lon_count // 2)[:, None] * np.arange(order_count)[None, :] % lon_count
    angles = products * (2.0 * math.pi / lon_count)
    return np.stack([np.cos(angles), -np.sin(angles)], axis=1).astype(jnp.bfloat16)


def stepped(block, reach):
    count = lax.axis_size("lat")
    return block + lax.ppermute(block, "lat", [(i, i ^ reach) for i in range(count)])


def swapped_pair_sum(block):
    count = lax.axis_size("lat")
    both = ("lat", "field")
    near = [(2 * i + f, 2 * i + 1 - f) for i in range(count) for f in range(2)]
    far = [(2 * i + f, 2 * (i ^ 1) + 1 - f) for i in range(count) for f in range(2)]
    return lax.ppermute(block, both, near) + lax.ppermute(block, both, far)


def column_kernel(orders_ref, modes_ref, basis_ref, out_ref, held_ref, total_ref, sems):
    group = lax.axis_index("lat")
    slots, pairs, degrees = held_ref.shape
    modes = modes_ref.shape[1]
    owned = [modes_ref[0:1, :] == orders_ref[s, group] for s in range(slots)]
    wanted = [jnp.max(row.astype(jnp.int32)) > 0 for row in owned]
    copies = [
        pltpu.make_async_copy(basis_ref.at[s], held_ref.at[s], sems.at[s]) for s in range(slots)
    ]
    for s in range(slots):
        pl.when(wanted[s])(copies[s].start)
    total_ref[...] = jnp.zeros_like(total_ref)
    here = lax.broadcasted_iota(jnp.int32, (degrees, modes), 0) == modes_ref[1:2, :]
    for s in range(slots):

        @pl.when(wanted[s])
        def _():
            pick = (here & owned[s]).astype(jnp.float32).astype(jnp.bfloat16)
            copies[s].wait()
            total_ref[...] += jnp.dot(held_ref[s], pick, preferred_element_type=jnp.float32)

    share = pairs // out_ref.shape[0]
    for j in range(share):
        rows = total_ref[pl.ds(j, out_ref.shape[0], stride=share), :]
        out_ref[:, j * modes : (j + 1) * modes] = rows.astype(jnp.bfloat16)


def coefficient_kernel(
    orders_ref, received_ref, basis_ref, out_ref, held_ref, place_ref, sems, *, first
):
    group = lax.axis_index("lat")
    here, pairs, degrees = held_ref.shape
    slots = orders_ref.shape[0]
    sources, _, wide = received_ref.shape
    share = pairs // sources
    copies = [
        pltpu.make_async_copy(basis_ref.at[first + s], held_ref.at[s], sems.at[s])
        for s in range(here)
    ]
    for copy in copies:
        copy.start()
    row = lax.broadcasted_iota(jnp.int32, (pairs, pairs), 0)
    column = lax.broadcasted_iota(jnp.int32, (pairs, pairs), 1)
    place_ref[...] = (
        (share * (row % sources) + row // sources == column).astype(jnp.float32).astype(jnp.bfloat16)
    )
    degree = lax.broadcasted_iota(jnp.int32, (1, degrees), 1)
    for s in range(here):
        by_pair = []
        for parity in range(2):
            part = jnp.concatenate(
                [
                    received_ref[:, (parity * share + j) * slots + first + s, :]
                    for j in range(share)
                ],
                axis=0,
            )
            ordered = lax.dot_general(
                part, place_ref[...], (((0,), (0,)), ((), ())), preferred_element_type=jnp.float32
            )
            by_pair.append(ordered.astype(jnp.bfloat16))
        copies[s].wait()
        both = jnp.dot(
            jnp.concatenate(by_pair, axis=0), held_ref[s], preferred_element_type=jnp.float32
        )
        order = orders_ref[first + s, group]
        odd = ((degree - order) & 1) == 1
        keep = (degree >= order) & (order >= 0)
        chosen = jnp.where(odd, both[wide:], both[:wide])
        out_ref[s] = jnp.where(keep, chosen, 0.0).astype(jnp.bfloat16)


def panel_kernel(first_ref, last_ref, centered_ref, out_ref, rows_ref, sems, *, scale):
    half = first_ref.shape[0]
    copies = []
    for s in range(2 * half):
        block = first_ref[s] if s < half else last_ref[s - half]
        values = lax.dot_general(
            block, centered_ref[...], (((0,), (0,)), ((), ())), preferred_element_type=jnp.float32
        )
        rows_ref[s] = (values * scale).astype(jnp.bfloat16).reshape(rows_ref.shape[1:])
        copies.append(pltpu.make_async_copy(rows_ref.at[s], out_ref.at[0, s], sems.at[s]))
        copies[-1].start()
    for copy in copies:
        copy.wait()


def local(fields_grid, basis, order_table, panel_modes):
    grid_one = fields_grid[0]
    snap_count, _, pair_count, lon_count = grid_one.shape
    group_count, slot_count = order_table.shape
    pair_total, deg_count = basis.shape[1], basis.shape[2]
    mode_count = panel_modes.shape[1]
    order_count = lon_count // 2
    wide = 2 * snap_count
    in_vmem = pl.BlockSpec(memory_space=pltpu.VMEM)
    in_smem = pl.BlockSpec(memory_space=pltpu.SMEM)
    anywhere = pl.BlockSpec(memory_space=pl.ANY)
    mode_order, mode_degree = panel_modes[0], panel_modes[1]
    orders_by_slot = order_table.T

    columns = pl.pallas_call(
        column_kernel,
        in_specs=[in_smem, in_vmem, anywhere],
        out_specs=in_vmem,
        out_shape=jax.ShapeDtypeStruct((group_count, pair_count * mode_count), jnp.bfloat16),
        scratch_shapes=[
            pltpu.VMEM((slot_count, pair_total, deg_count), jnp.bfloat16),
            pltpu.VMEM((pair_total, mode_count), jnp.float32),
            pltpu.SemaphoreType.DMA((slot_count,)),
        ],
        name="columns",
    )(orders_by_slot, panel_modes, basis)
    columns = columns.reshape(group_count, 1, pair_count * mode_count)
    columns = lax.all_to_all(columns, "lat", split_axis=0, concat_axis=0, tiled=True)
    columns = jnp.sum(columns.astype(jnp.float32), axis=(0, 1)).reshape(pair_count, mode_count)

    table = jnp.asarray(dft_table(lon_count, order_count))
    halves = [
        jnp.einsum("thjn,nrm->hjrtm", half, table, preferred_element_type=jnp.float32)
        for half in (grid_one[..., :order_count], grid_one[..., order_count:])
    ]
    sign = 1.0 - 2.0 * (lax.iota(jnp.int32, order_count) % 2).astype(jnp.float32)
    fourier = (halves[0] + halves[1] * sign) * (1.0 / math.sqrt(lon_count))
    parts = jnp.stack([fourier[0] + fourier[1], fourier[0] - fourier[1]]).astype(jnp.bfloat16)
    parts = parts.reshape(2 * pair_count * wide, order_count)

    def rows_of(wanted):
        placed = wanted[:, None] == lax.broadcasted_iota(jnp.int32, (1, order_count), 1)
        rows = lax.dot_general(
            placed.astype(jnp.bfloat16),
            parts,
            (((1,), (1,)), ((), ())),
            preferred_element_type=jnp.float32,
        )
        return rows.astype(jnp.bfloat16)

    sent = rows_of(order_table.reshape(-1))
    sent = sent.reshape(group_count, slot_count, 2 * pair_count, wide).transpose(0, 2, 1, 3)
    sent = sent.reshape(group_count, 2 * pair_count * slot_count, wide)
    received = lax.all_to_all(sent, "lat", split_axis=0, concat_axis=0, tiled=True)

    mode_parts = rows_of(mode_order).reshape(mode_count, 2, pair_count, wide)
    mode_odd = ((mode_degree - mode_order) % 2 == 1)[:, None, None]
    mode_side = jnp.where(mode_odd, mode_parts[:, 1], mode_parts[:, 0]).astype(jnp.float32)
    values = swapped_pair_sum(jnp.sum(mode_side * columns.T[:, :, None], axis=1))
    reach = 2
    while 4 * reach < group_count:
        values = stepped(values, reach)
        reach *= 2

    def coefficients(block, first):
        count = slot_count // 2
        return pl.pallas_call(
            functools.partial(coefficient_kernel, first=first),
            in_specs=[in_smem, in_vmem, anywhere],
            out_specs=in_vmem,
            out_shape=jax.ShapeDtypeStruct((count, wide, deg_count), jnp.bfloat16),
            scratch_shapes=[
                pltpu.VMEM((count, pair_total, deg_count), jnp.bfloat16),
                pltpu.VMEM((pair_total, pair_total), jnp.bfloat16),
                pltpu.SemaphoreType.DMA((count,)),
            ],
            name="coefficients",
        )(orders_by_slot, block, basis)

    values, received = lax.optimization_barrier((values, received))
    first_half = coefficients(received, 0)
    values = stepped(values, reach)
    values, first_half, received = lax.optimization_barrier((values, first_half, received))
    last_half = coefficients(received, slot_count // 2)
    values = stepped(values, 2 * reach)
    values, last_half = lax.optimization_barrier((values, last_half))

    values = lax.reduce_precision(values, 8, 7).reshape(2 * mode_count, snap_count)
    centered = (values - jnp.mean(values, axis=1, keepdims=True)).astype(jnp.bfloat16).T
    blank = jnp.zeros_like(centered)
    centered = jnp.concatenate(
        [jnp.concatenate([centered, blank], 1), jnp.concatenate([blank, centered], 1)], 0
    )
    return pl.pallas_call(
        functools.partial(panel_kernel, scale=1.0 / (snap_count - 1)),
        in_specs=[in_vmem, in_vmem, in_vmem],
        out_specs=anywhere,
        out_shape=jax.ShapeDtypeStruct((1, slot_count, 2 * deg_count, 2 * mode_count), jnp.bfloat16),
        scratch_shapes=[
            pltpu.VMEM((slot_count, 2 * deg_count, 2 * mode_count), jnp.bfloat16),
            pltpu.SemaphoreType.DMA((slot_count,)),
        ],
        name="panel",
    )(first_half, last_half, centered)


def solution(mesh):
    placed = (P("field", None, None, "lat", None), P("lat", None, None), P(), P())
    return jax.shard_map(
        local, mesh=mesh, in_specs=placed, out_specs=P("field", "lat", None, None), check_vma=False
    )
```

time: 117 us -> 104 us (0.89)
  waiting for transfers between devices: 62.6 us -> 35.3 us
  Pallas kernels: 0 us -> 17.2 us
  starting transfers between devices: 24.2 us -> 38.8 us
  local copies, waits for them, and re-layouts: 14.3 us -> 4.41 us
  matrix products: 13.4 us -> 5.4 us
    all_to_all x1, waiting for transfers between devices: 41 us -> 6.92 us  [local(): lax.all_to_all(sent, 'lat', split_axis=0, concat_axis=0, tiled=True)]
    pallas_call x0 -> x4, Pallas kernels: none -> 17.2 us  [the longest x2 11.8 us: coefficients(): pl.pallas_call(functools.partial(coefficient_kernel, first=first), in_spe...]
    all_to_all x0 -> x1, starting transfers between devices: none -> 16.8 us  [local(): lax.all_to_all(columns, 'lat', split_axis=0, concat_axis=0, tiled=True)]
    dot_general x5 -> x4, matrix products: 13.4 us -> 5.4 us  [the longest x2 3.19 us: rows_of(): lax.dot_general(placed.astype(jnp.bfloat16), parts, (((1,), (1,)), ((), (...]
    all_to_all x1, starting transfers between devices: 15.6 us -> 9.31 us  [local(): lax.all_to_all(sent, 'lat', split_axis=0, concat_axis=0, tiled=True)]
    reshape x4 -> x5, local copies, waits for them, and re-layouts: 7.31 us -> 1.86 us  [the longest x1 1.59 us: local(): columns = columns.reshape(group_count, 1, pair_count * mode_count)]
    all_to_all x0 -> x1, waiting for transfers between devices: none -> 4.56 us  [local(): lax.all_to_all(columns, 'lat', split_axis=0, concat_axis=0, tiled=True)]
    ppermute x8, starting transfers between devices: 8.68 us -> 12.7 us  [the longest x6 11.6 us: stepped(): lax.ppermute(block, 'lat', [(i, i ^ reach) for i in range(count)])]
  transfers between devices with their start and end apart: 9 -> 10, of which waited for: 9 -> 8; matrix products, arithmetic and copies ran while one was open for 5% -> 7% of each run, Pallas kernels for 0% -> 11%
where the time goes in v3:
time: 104 us; the launch traced here: 103 us
  starting transfers between devices  38.8 us (37%)
  waiting for transfers between devices  35.3 us (34%)
  Pallas kernels  17.2 us (17%)
  matrix products  5.4 us (5%)
  local copies, waits for them, and re-layouts  4.41 us (4%)
  other arithmetic  1.63 us (2%)
    ppermute x6, waiting for transfers between devices, stepped(): lax.ppermute(block, 'lat', [(i, i ^ reach) for i in range(count)])  21.3 us
    all_to_all x1, starting transfers between devices, local(): lax.all_to_all(columns, 'lat', split_axis=0, concat_axis=0, tiled=True)  16.8 us
    pallas_call x2, Pallas kernels, coefficients(): pl.pallas_call(functools.partial(coefficient_kernel, first=first), in_spe...  11.8 us
    ppermute x6, starting transfers between devices, stepped(): lax.ppermute(block, 'lat', [(i, i ^ reach) for i in range(count)])  11.6 us
    all_to_all x1, starting transfers between devices, local(): lax.all_to_all(sent, 'lat', split_axis=0, concat_axis=0, tiled=True)  9.31 us
    all_to_all x1, waiting for transfers between devices, local(): lax.all_to_all(sent, 'lat', split_axis=0, concat_axis=0, tiled=True)  6.92 us
    all_to_all x1, waiting for transfers between devices, local(): lax.all_to_all(columns, 'lat', split_axis=0, concat_axis=0, tiled=True)  4.56 us
    pallas_call x1, Pallas kernels, local(): pl.pallas_call(functools.partial(panel_kernel, scale=1.0 / (snap_count -...  3.53 us
  transfers between devices with their start and end apart: 10, of which 8 were waited for; matrix products, arithmetic and copies ran while one was open for 7% of the time, Pallas kernels for 11%

profile of v3, /device:TPU:2, one launch (start us, length us, event | category | flops | bytes accessed | tf_op | source)
XLA Modules:
  0.0 103.2 jit_solution(7794802800249483177)
XLA Ops:
  0.0 0.0 copy-start.2
  0.0 0.0 copy-start.1
  0.0 1.9 %columns.1 = bf16[128,192]{1,0:T(8,128)(2,1)} custom-call(s32[8,128]{1,0:T(8,128)} %bitcast.55, s32[2,64]{1,0:T(2,128)} %modes_ref.1, bf16[8,384,768]{2,1,0:T(8,128)(2,1)} %basis_ref.5), custom_call_target="tpu_custom_call" | custom-call | tf_op jit(solution)/shard_map/columns/pallas_call | solution.py:133
  1.9 1.6 %copy.17 = bf16[128,1,192]{2,1,0:T(2,128)(2,1)} copy(bf16[128,1,192]{2,0,1:T(8,128)(2,1)} %bitcast.54) | data formatting | bytes 98304 | tf_op jit(solution)/shard_map/reshape | solution.py:145
  3.5 16.8 %all-to-all-start = ((bf16[128,1,192]{2,1,0:T(2,128)(2,1)}), bf16[128,1,192]{2,1,0:T(2,128)(2,1)S(1)}, u32[]{:S(2)}, u32[]{:S(2)}) async-start(bf16[128,1,192]{2,1,0:T(2,128)(2,1)} %copy.17), calls=%async_computation | async-start | bytes 262144 | tf_op jit(solution)/shard_map/all_to_all | solution.py:146
  20.4 0.0 copy-done.2
  20.4 0.1 copy.19
  20.5 0.1 eq.44
  20.6 0.0 copy-done.1
  20.6 0.0 copy-start.4
  20.6 0.1 copy.24
  20.7 1.5 %copy-done.4 = bf16[768,2,768,1,1]{2,0,4,3,1:T(8,128)(2,1)S(1)} copy-done((bf16[768,2,768,1,1]{2,0,4,3,1:T(8,128)(2,1)S(1)}, bf16[768,2,768,1,1]{2,0,4,3,1:T(8,128)(2,1)}, u32[]{:S(2)}) %copy-start.4) | copy-done | bytes 2359320
  22.2 1.1 %fusion.4 = f32[2,768,64,2,3]{1,2,4,3,0:T(8,128)S(1)} fusion(bf16[768,2,768,1,1]{2,0,4,3,1:T(8,128)(2,1)S(1)} %copy-done.4, bf16[64,2,3,1536]{3,0,2,1:T(8,128)(2,1)S(1)} %bitcast.52), kind=kOutput, calls=%fused_computation.13 | convolution fusion | flops 905969664 | bytes 5308416 | tf_op jit(solution)/shard_map/thjn,nrm->hjrtm/dot_general | solution.py:151
  23.3 1.1 %multiply_bitcast_fusion = f32[2,3,2,64,768]{4,3,1,0,2:T(8,128)S(1)} fusion(f32[2,768,64,2,3]{1,2,4,3,0:T(8,128)S(1)} %fusion.4, bf16[768,2,768,1,1]{2,0,4,3,1:T(8,128)(2,1)S(1)} %copy-done.4, f32[768]{0:T(1024)S(1)} %fusion.13, bf16[64,2,3,1536]{3,0,2,1:T(8,128)(2,1)S(1)} %bitcast.53), kind=kOutput, calls=%fused_computation.2 | convolution fusion | flops 907739136 | bytes 7671808 | tf_op jit(solution)/shard_map/thjn,nrm->hjrtm/dot_general | solution.py:151
  24.5 0.3 add_convert_fusion
  24.7 0.1 pad_maximum_fusion
  24.8 0.1 copy.15
  24.9 2.7 %fusion.3 = bf16[128,48,128]{2,1,0:T(8,128)(2,1)} fusion(bf16[768,768]{1,0:T(8,128)(2,1)S(1)} %bitcast.50, s32[1024]{0:T(1024)S(1)} %eq.44), kind=kOutput, calls=%fused_computation.5 | convolution fusion | flops 1209532416 | bytes 2756608 | tf_op jit(solution)/shard_map/dot_general | solution.py:161
  27.6 0.0 copy-start.3
  27.6 4.6 %all-to-all-done = bf16[128,1,192]{2,1,0:T(2,128)(2,1)S(1)} async-done(((bf16[128,1,192]{2,1,0:T(2,128)(2,1)}), bf16[128,1,192]{2,1,0:T(2,128)(2,1)S(1)}, u32[]{:S(2)}, u32[]{:S(2)}) %all-to-all-start) | async-done | bytes 49184 | tf_op jit(solution)/shard_map/all_to_all | solution.py:146
  32.2 9.3 %all-to-all-start.1 = ((bf16[128,48,128]{2,1,0:T(8,128)(2,1)}), bf16[128,48,128]{2,1,0:T(8,128)(2,1)S(1)}, u32[]{:S(2)}, u32[]{:S(2)}) async-start(bf16[128,48,128]{2,1,0:T(8,128)(2,1)} %fusion.3), calls=%async_computation.1 | async-start | bytes 3145728 | tf_op jit(solution)/shard_map/all_to_all | solution.py:172
  41.5 0.0 copy-done.3
  41.5 0.5 convolution_convert_fusion
  42.1 0.2 convert_reduce_fusion
  42.3 0.1 reshape.63
  42.4 0.1 copy.18
  42.5 0.2 multiply_reduce_fusion
  42.7 0.1 collective-permute-start.1
  42.8 1.0 collective-permute-start
  43.8 2.5 %collective-permute-done.1 = f32[64,128]{1,0:T(8,128)S(1)} collective-permute-done((f32[64,128]{1,0:T(8,128)S(1)}, f32[64,128]{1,0:T(8,128)S(1)}, u32[]{:S(2)}, u32[]{:S(2)}) %collective-permute-start.1) | collective-permute-done | bytes 32800 | tf_op jit(solution)/shard_map/ppermute | solution.py:29
  46.3 0.0 collective-permute-done
  46.3 2.2 %collective-permute-start.2 = (f32[64,128]{1,0:T(8,128)S(1)}, f32[64,128]{1,0:T(8,128)S(1)}, u32[]{:S(2)}, u32[]{:S(2)}) collective-permute-start(f32[64,128]{1,0:T(8,128)S(1)} %add.57), channel_id=1, source_target_pairs={{0,4},{2,6},{4,0},{6,2},{8,12},{10,14},{12,8},{14,10},{16,20},{18,... | collective-permute-start | bytes 98312 | tf_op jit(solution)/shard_map/ppermute | solution.py:21
  48.5 3.8 %collective-permute-done.2 = f32[64,128]{1,0:T(8,128)S(1)} collective-permute-done((f32[64,128]{1,0:T(8,128)S(1)}, f32[64,128]{1,0:T(8,128)S(1)}, u32[]{:S(2)}, u32[]{:S(2)}) %collective-permute-start.2) | collective-permute-done | bytes 32800 | tf_op jit(solution)/shard_map/ppermute | solution.py:21
  52.3 1.9 %collective-permute-start.3 = (f32[64,128]{1,0:T(8,128)S(1)}, f32[64,128]{1,0:T(8,128)S(1)}, u32[]{:S(2)}, u32[]{:S(2)}) collective-permute-start(f32[64,128]{1,0:T(8,128)S(1)} %add.58), channel_id=1, source_target_pairs={{0,8},{2,10},{4,12},{6,14},{8,0},{10,2},{12,4},{14,6},{16,24},{18,... | collective-permute-start | bytes 98312 | tf_op jit(solution)/shard_map/ppermute | solution.py:21
  54.2 2.0 %collective-permute-done.3 = f32[64,128]{1,0:T(8,128)S(1)} collective-permute-done((f32[64,128]{1,0:T(8,128)S(1)}, f32[64,128]{1,0:T(8,128)S(1)}, u32[]{:S(2)}, u32[]{:S(2)}) %collective-permute-start.3) | collective-permute-done | bytes 32800 | tf_op jit(solution)/shard_map/ppermute | solution.py:21
  56.3 3.1 %collective-permute-start.4 = (f32[64,128]{1,0:T(8,128)S(1)}, f32[64,128]{1,0:T(8,128)S(1)}, u32[]{:S(2)}, u32[]{:S(2)}) collective-permute-start(f32[64,128]{1,0:T(8,128)S(1)} %add.59), channel_id=1, source_target_pairs={{0,16},{2,18},{4,20},{6,22},{8,24},{10,26},{12,28},{14,30},{16,0},... | collective-permute-start | bytes 98312 | tf_op jit(solution)/shard_map/ppermute | solution.py:21
  59.4 2.6 %collective-permute-done.4 = f32[64,128]{1,0:T(8,128)S(1)} collective-permute-done((f32[64,128]{1,0:T(8,128)S(1)}, f32[64,128]{1,0:T(8,128)S(1)}, u32[]{:S(2)}, u32[]{:S(2)}) %collective-permute-start.4) | collective-permute-done | bytes 32800 | tf_op jit(solution)/shard_map/ppermute | solution.py:21
  62.0 1.8 %collective-permute-start.5 = (f32[64,128]{1,0:T(8,128)S(1)}, f32[64,128]{1,0:T(8,128)S(1)}, u32[]{:S(2)}, u32[]{:S(2)}) collective-permute-start(f32[64,128]{1,0:T(8,128)S(1)} %add.60), channel_id=1, source_target_pairs={{0,32},{2,34},{4,36},{6,38},{8,40},{10,42},{12,44},{14,46},{16,48}... | collective-permute-start | bytes 98312 | tf_op jit(solution)/shard_map/ppermute | solution.py:21
  63.8 12.5 %collective-permute-done.5 = f32[64,128]{1,0:T(8,128)S(1)} collective-permute-done((f32[64,128]{1,0:T(8,128)S(1)}, f32[64,128]{1,0:T(8,128)S(1)}, u32[]{:S(2)}, u32[]{:S(2)}) %collective-permute-start.5) | collective-permute-done | bytes 32800 | tf_op jit(solution)/shard_map/ppermute | solution.py:21
  76.3 6.9 %all-to-all-done.1.received_ref = bf16[128,48,128]{2,1,0:T(8,128)(2,1)S(1)} async-done(((bf16[128,48,128]{2,1,0:T(8,128)(2,1)}), bf16[128,48,128]{2,1,0:T(8,128)(2,1)S(1)}, u32[]{:S(2)}, u32[]{:S(2)}) %all-to-all-start.1) | async-done | bytes 1572896 | tf_op jit(solution)/shard_map/all_to_all | solution.py:172
  83.2 0.0 copy-start
  83.2 0.6 collective-permute-start.6
  83.8 0.5 copy-done
  84.4 5.9 %coefficients.2.first_ref = bf16[4,128,768]{2,1,0:T(8,128)(2,1)} custom-call(s32[8,128]{1,0:T(8,128)} %bitcast.56, bf16[128,48,128]{2,1,0:T(8,128)(2,1)} %copy-done, bf16[8,384,768]{2,1,0:T(8,128)(2,1)} %basis_ref.5), custom_call_target="tpu_custom_call" | custom-call | tf_op jit(solution)/shard_map/coefficients/pallas_call | solution.py:185
  90.2 0.0 collective-permute-done.6
  90.3 1.9 %collective-permute-start.7 = (f32[64,128]{1,0:T(8,128)S(1)}, f32[64,128]{1,0:T(8,128)S(1)}, u32[]{:S(2)}, u32[]{:S(2)}) collective-permute-start(f32[64,128]{1,0:T(8,128)S(1)} %add.62), channel_id=1, source_target_pairs={{0,128},{2,130},{4,132},{6,134},{8,136},{10,138},{12,140},{14,142}... | collective-permute-start | bytes 98312 | tf_op jit(solution)/shard_map/ppermute | solution.py:21
  92.1 5.9 %coefficients.3.last_ref = bf16[4,128,768]{2,1,0:T(8,128)(2,1)} custom-call(s32[8,128]{1,0:T(8,128)} %bitcast.57, bf16[128,48,128]{2,1,0:T(8,128)(2,1)} %copy-done, bf16[8,384,768]{2,1,0:T(8,128)(2,1)} %basis_ref.5), custom_call_target="tpu_custom_call" | custom-call | tf_op jit(solution)/shard_map/coefficients/pallas_call | solution.py:185
  98.1 0.5 collective-permute-done.7
  98.5 0.1 reshape.66
  98.6 0.1 copy.20
  98.7 0.1 reduce_sum.29
  98.8 0.6 fusion.8.centered_ref
  99.5 3.5 %panel.1 = bf16[1,8,1536,128]{3,2,1,0:T(8,128)(2,1)} custom-call(bf16[4,128,768]{2,1,0:T(8,128)(2,1)} %coefficients.2.first_ref, bf16[4,128,768]{2,1,0:T(8,128)(2,1)} %coefficients.3.last_ref, bf16[128,256]{1,0:T(8,128)(2,1)} %fusion.8.centered_ref), custom_call_target="tpu_custom_call" | custom-call | tf_op jit(solution)/shard_map/panel/pallas_call | solution.py:212
  (14 shorter events, 0.1 us)
Async XLA Ops:
  0.0 20.4 %copy-start.2 = (s32[128,8]{0,1:T(8,128)S(1)}, s32[128,8]{0,1:T(8,128)}, u32[]{:S(2)}) copy-start(s32[128,8]{0,1:T(8,128)} %param.7) | copy-start | bytes 12292
  0.0 20.6 %copy-start.1 = (bf16[1,64,2,3,1536]{4,2,3,1,0:T(2,128)(2,1)S(1)}, bf16[1,64,2,3,1536]{4,2,3,1,0:T(2,128)(2,1)}, u32[]{:S(2)}) copy-start(bf16[1,64,2,3,1536]{4,2,3,1,0:T(2,128)(2,1)} %param.5) | copy-start | bytes 3538948
  3.5 28.7 %all-to-all-start = ((bf16[128,1,192]{2,1,0:T(2,128)(2,1)}), bf16[128,1,192]{2,1,0:T(2,128)(2,1)S(1)}, u32[]{:S(2)}, u32[]{:S(2)}) async-start(bf16[128,1,192]{2,1,0:T(2,128)(2,1)} %copy.17), calls=%async_computation | async-start | bytes 262144 | tf_op jit(solution)/shard_map/all_to_all | solution.py:146
  20.6 1.7 %copy-start.4 = (bf16[768,2,768,1,1]{2,0,4,3,1:T(8,128)(2,1)S(1)}, bf16[768,2,768,1,1]{2,0,4,3,1:T(8,128)(2,1)}, u32[]{:S(2)}) copy-start(bf16[768,2,768,1,1]{2,0,4,3,1:T(8,128)(2,1)} %constant.47) | copy-start | bytes 7077892
  27.6 13.9 %copy-start.3 = (s32[2,64]{1,0:T(2,128)S(1)}, s32[2,64]{1,0:T(2,128)}, u32[]{:S(2)}) copy-start(s32[2,64]{1,0:T(2,128)} %modes_ref.1) | copy-start | bytes 1540
  32.2 51.0 %all-to-all-start.1 = ((bf16[128,48,128]{2,1,0:T(8,128)(2,1)}), bf16[128,48,128]{2,1,0:T(8,128)(2,1)S(1)}, u32[]{:S(2)}, u32[]{:S(2)}) async-start(bf16[128,48,128]{2,1,0:T(8,128)(2,1)} %fusion.3), calls=%async_computation.1 | async-start | bytes 3145728 | tf_op jit(solution)/shard_map/all_to_all | solution.py:172
  42.7 3.6 %collective-permute-start.1 = (f32[64,128]{1,0:T(8,128)S(1)}, f32[64,128]{1,0:T(8,128)S(1)}, u32[]{:S(2)}, u32[]{:S(2)}) collective-permute-start(f32[64,128]{1,0:T(8,128)S(1)} %multiply_reduce_fusion), channel_id=1, source_target_pairs={{0,3},{1,2},{2,1},{3,0},{4,7},{5,6},{6,5},{7,4},{8,11},{9,10},{10,... | collective-permute-start | bytes 98312 | tf_op jit(solution)/shard_map/ppermute | solution.py:29
  42.8 3.5 %collective-permute-start = (f32[64,128]{1,0:T(8,128)S(1)}, f32[64,128]{1,0:T(8,128)S(1)}, u32[]{:S(2)}, u32[]{:S(2)}) collective-permute-start(f32[64,128]{1,0:T(8,128)S(1)} %multiply_reduce_fusion), channel_id=1, source_target_pairs={{0,1},{1,0},{2,3},{3,2},{4,5},{5,4},{6,7},{7,6},{8,9},{9,8},{10,11... | collective-permute-start | bytes 98312 | tf_op jit(solution)/shard_map/ppermute | solution.py:29
  46.3 6.0 %collective-permute-start.2 = (f32[64,128]{1,0:T(8,128)S(1)}, f32[64,128]{1,0:T(8,128)S(1)}, u32[]{:S(2)}, u32[]{:S(2)}) collective-permute-start(f32[64,128]{1,0:T(8,128)S(1)} %add.57), channel_id=1, source_target_pairs={{0,4},{2,6},{4,0},{6,2},{8,12},{10,14},{12,8},{14,10},{16,20},{18,... | collective-permute-start | bytes 98312 | tf_op jit(solution)/shard_map/ppermute | solution.py:21
  52.3 3.9 %collective-permute-start.3 = (f32[64,128]{1,0:T(8,128)S(1)}, f32[64,128]{1,0:T(8,128)S(1)}, u32[]{:S(2)}, u32[]{:S(2)}) collective-permute-start(f32[64,128]{1,0:T(8,128)S(1)} %add.58), channel_id=1, source_target_pairs={{0,8},{2,10},{4,12},{6,14},{8,0},{10,2},{12,4},{14,6},{16,24},{18,... | collective-permute-start | bytes 98312 | tf_op jit(solution)/shard_map/ppermute | solution.py:21
  56.3 5.7 %collective-permute-start.4 = (f32[64,128]{1,0:T(8,128)S(1)}, f32[64,128]{1,0:T(8,128)S(1)}, u32[]{:S(2)}, u32[]{:S(2)}) collective-permute-start(f32[64,128]{1,0:T(8,128)S(1)} %add.59), channel_id=1, source_target_pairs={{0,16},{2,18},{4,20},{6,22},{8,24},{10,26},{12,28},{14,30},{16,0},... | collective-permute-start | bytes 98312 | tf_op jit(solution)/shard_map/ppermute | solution.py:21
  62.0 14.3 %collective-permute-start.5 = (f32[64,128]{1,0:T(8,128)S(1)}, f32[64,128]{1,0:T(8,128)S(1)}, u32[]{:S(2)}, u32[]{:S(2)}) collective-permute-start(f32[64,128]{1,0:T(8,128)S(1)} %add.60), channel_id=1, source_target_pairs={{0,32},{2,34},{4,36},{6,38},{8,40},{10,42},{12,44},{14,46},{16,48}... | collective-permute-start | bytes 98312 | tf_op jit(solution)/shard_map/ppermute | solution.py:21
  83.2 1.1 %copy-start = (bf16[128,48,128]{2,1,0:T(8,128)(2,1)}, bf16[128,48,128]{2,1,0:T(8,128)(2,1)S(1)}, u32[]{:S(2)}) copy-start(bf16[128,48,128]{2,1,0:T(8,128)(2,1)S(1)} %all-to-all-done.1.received_ref) | copy-start | bytes 4718596
  83.2 7.0 %collective-permute-start.6 = (f32[64,128]{1,0:T(8,128)S(1)}, f32[64,128]{1,0:T(8,128)S(1)}, u32[]{:S(2)}, u32[]{:S(2)}) collective-permute-start(f32[64,128]{1,0:T(8,128)S(1)} %add.61), channel_id=1, source_target_pairs={{0,64},{2,66},{4,68},{6,70},{8,72},{10,74},{12,76},{14,78},{16,80}... | collective-permute-start | bytes 98312 | tf_op jit(solution)/shard_map/ppermute | solution.py:21
  90.3 8.2 %collective-permute-start.7 = (f32[64,128]{1,0:T(8,128)S(1)}, f32[64,128]{1,0:T(8,128)S(1)}, u32[]{:S(2)}, u32[]{:S(2)}) collective-permute-start(f32[64,128]{1,0:T(8,128)S(1)} %add.62), channel_id=1, source_target_pairs={{0,128},{2,130},{4,132},{6,134},{8,136},{10,138},{12,140},{14,142}... | collective-permute-start | bytes 98312 | tf_op jit(solution)/shard_map/ppermute | solution.py:21

commit v4 on v3

--- a/solution.py
+++ b/solution.py
@@ -16,9 +16,13 @@
     return np.stack([np.cos(angles), -np.sin(angles)], axis=1).astype(jnp.bfloat16)
 
 
+def from_far(block, reach):
+    count = lax.axis_size("lat")
+    return lax.ppermute(block, "lat", [(i, i ^ reach) for i in range(count)])
+
+
 def stepped(block, reach):
-    count = lax.axis_size("lat")
-    return block + lax.ppermute(block, "lat", [(i, i ^ reach) for i in range(count)])
+    return block + from_far(block, reach)
 
 
 def swapped_pair_sum(block):
@@ -29,7 +33,11 @@
     return lax.ppermute(block, both, near) + lax.ppermute(block, both, far)
 
 
-def column_kernel(orders_ref, modes_ref, basis_ref, out_ref, held_ref, total_ref, sems):
+def one_hot(condition):
+    return condition.astype(jnp.float32).astype(jnp.bfloat16)
+
+
+def column_kernel(orders_ref, modes_ref, basis_ref, out_ref, held_ref, total_ref, rows_ref, sems):
     group = lax.axis_index("lat")
     slots, pairs, degrees = held_ref.shape
     modes = modes_ref.shape[1]
@@ -46,53 +54,77 @@
 
         @pl.when(wanted[s])
         def _():
-            pick = (here & owned[s]).astype(jnp.float32).astype(jnp.bfloat16)
+            pick = one_hot(here & owned[s])
             copies[s].wait()
             total_ref[...] += jnp.dot(held_ref[s], pick, preferred_element_type=jnp.float32)
 
-    share = pairs // out_ref.shape[0]
-    for j in range(share):
-        rows = total_ref[pl.ds(j, out_ref.shape[0], stride=share), :]
-        out_ref[:, j * modes : (j + 1) * modes] = rows.astype(jnp.bfloat16)
-
-
-def coefficient_kernel(
-    orders_ref, received_ref, basis_ref, out_ref, held_ref, place_ref, sems, *, first
+    groups, halves, lanes = out_ref.shape
+    share = pairs // groups
+    blocks = [total_ref[pl.ds(j, groups, stride=share), :] for j in range(share)]
+    blocks += [jnp.zeros_like(blocks[0])] * (halves * lanes // modes - share)
+    per_half = lanes // modes
+    for h in range(halves):
+        half = jnp.concatenate(blocks[h * per_half : (h + 1) * per_half], axis=1)
+        rows_ref[pl.ds(h, groups, stride=halves), :] = half
+    out_ref[...] = rows_ref[...].astype(jnp.bfloat16).reshape(out_ref.shape)
+
+
+def basis_kernel(
+    values_ref, basis_ref, out_ref, same_ref, held_ref, rows_ref, sems, out_sems, *, sources
 ):
-    group = lax.axis_index("lat")
-    here, pairs, degrees = held_ref.shape
-    slots = orders_ref.shape[0]
-    sources, _, wide = received_ref.shape
+    same_ref[...] = values_ref[...]
+    slots, pairs, _ = out_ref.shape
     share = pairs // sources
     copies = [
-        pltpu.make_async_copy(basis_ref.at[first + s], held_ref.at[s], sems.at[s])
-        for s in range(here)
+        pltpu.make_async_copy(basis_ref.at[s], held_ref.at[s], sems.at[s]) for s in range(slots)
+    ]
+    out_copies = [
+        pltpu.make_async_copy(rows_ref.at[s], out_ref.at[s], out_sems.at[s]) for s in range(slots)
     ]
     for copy in copies:
         copy.start()
     row = lax.broadcasted_iota(jnp.int32, (pairs, pairs), 0)
     column = lax.broadcasted_iota(jnp.int32, (pairs, pairs), 1)
-    place_ref[...] = (
-        (share * (row % sources) + row // sources == column).astype(jnp.float32).astype(jnp.bfloat16)
-    )
+    place = one_hot(share * (row % sources) + row // sources == column)
+    for s in range(slots):
+        copies[s].wait()
+        rows = jnp.dot(place, held_ref[s], preferred_element_type=jnp.float32)
+        rows_ref[s] = rows.astype(jnp.bfloat16)
+        out_copies[s].start()
+    for copy in out_copies:
+        copy.wait()
+
+
+def coefficient_kernel(orders_ref, received_ref, basis_ref, out_ref, held_ref, sems, *, first):
+    group = lax.axis_index("lat")
+    slots, pairs, degrees = basis_ref.shape
+    sources, _, wide = received_ref.shape
+    share = pairs // sources
+    here = out_ref.shape[0]
+    copies = [
+        pltpu.make_async_copy(basis_ref.at[first + s], held_ref.at[s], sems.at[s])
+        for s in range(here)
+    ]
+    for copy in copies:
+        copy.start()
     degree = lax.broadcasted_iota(jnp.int32, (1, degrees), 1)
     for s in range(here):
-        by_pair = []
-        for parity in range(2):
-            part = jnp.concatenate(
+        sides = [
+            jnp.concatenate(
                 [
                     received_ref[:, (parity * share + j) * slots + first + s, :]
                     for j in range(share)
                 ],
                 axis=0,
             )
-            ordered = lax.dot_general(
-                part, place_ref[...], (((0,), (0,)), ((), ())), preferred_element_type=jnp.float32
-            )
-            by_pair.append(ordered.astype(jnp.bfloat16))
+            for parity in range(2)
+        ]
         copies[s].wait()
-        both = jnp.dot(
-            jnp.concatenate(by_pair, axis=0), held_ref[s], preferred_element_type=jnp.float32
+        both = lax.dot_general(
+            jnp.concatenate(sides, axis=1),
+            held_ref[s],
+            (((0,), (0,)), ((), ())),
+            preferred_element_type=jnp.float32,
         )
         order = orders_ref[first + s, group]
         odd = ((degree - order) & 1) == 1
@@ -101,15 +133,35 @@
         out_ref[s] = jnp.where(keep, chosen, 0.0).astype(jnp.bfloat16)
 
 
-def panel_kernel(first_ref, last_ref, centered_ref, out_ref, rows_ref, sems, *, scale):
+def panel_kernel(first_ref, last_ref, values_ref, out_ref, rows_ref, sems, *, scale):
+    modes, wide = values_ref.shape
+    snaps = wide // 2
+    values = values_ref[...].astype(jnp.bfloat16).astype(jnp.float32)
+    mode = lax.broadcasted_iota(jnp.int32, (modes, 2 * modes), 0)
+    column = lax.broadcasted_iota(jnp.int32, (modes, 2 * modes), 1)
+    block = jnp.zeros((snaps, 2 * modes), jnp.float32)
+    for u in range(2):
+        part = values[:, u * snaps : (u + 1) * snaps]
+        part = (part - jnp.mean(part, axis=1, keepdims=True)).astype(jnp.bfloat16)
+        block += lax.dot_general(
+            part,
+            one_hot(2 * mode + u == column),
+            (((0,), (0,)), ((), ())),
+            preferred_element_type=jnp.float32,
+        )
+    block = block.astype(jnp.bfloat16)
+    blank = jnp.zeros_like(block)
+    centered = jnp.concatenate(
+        [jnp.concatenate([block, blank], axis=1), jnp.concatenate([blank, block], axis=1)], axis=0
+    )
     half = first_ref.shape[0]
     copies = []
     for s in range(2 * half):
-        block = first_ref[s] if s < half else last_ref[s - half]
-        values = lax.dot_general(
-            block, centered_ref[...], (((0,), (0,)), ((), ())), preferred_element_type=jnp.float32
-        )
-        rows_ref[s] = (values * scale).astype(jnp.bfloat16).reshape(rows_ref.shape[1:])
+        rows = first_ref[s] if s < half else last_ref[s - half]
+        products = lax.dot_general(
+            rows, centered, (((0,), (0,)), ((), ())), preferred_element_type=jnp.float32
+        )
+        rows_ref[s] = (products * scale).astype(jnp.bfloat16).reshape(rows_ref.shape[1:])
         copies.append(pltpu.make_async_copy(rows_ref.at[s], out_ref.at[0, s], sems.at[s]))
         copies[-1].start()
     for copy in copies:
@@ -129,22 +181,24 @@
     anywhere = pl.BlockSpec(memory_space=pl.ANY)
     mode_order, mode_degree = panel_modes[0], panel_modes[1]
     orders_by_slot = order_table.T
+    in_hbm = pl.BlockSpec(memory_space=pltpu.HBM)
+    roomy = pltpu.CompilerParams(vmem_limit_bytes=24 << 20)
 
     columns = pl.pallas_call(
         column_kernel,
-        in_specs=[in_smem, in_vmem, anywhere],
+        in_specs=[in_smem, in_vmem, in_hbm],
         out_specs=in_vmem,
-        out_shape=jax.ShapeDtypeStruct((group_count, pair_count * mode_count), jnp.bfloat16),
+        out_shape=jax.ShapeDtypeStruct((group_count, 2, wide), jnp.bfloat16),
         scratch_shapes=[
             pltpu.VMEM((slot_count, pair_total, deg_count), jnp.bfloat16),
             pltpu.VMEM((pair_total, mode_count), jnp.float32),
+            pltpu.VMEM((2 * group_count, wide), jnp.float32),
             pltpu.SemaphoreType.DMA((slot_count,)),
         ],
         name="columns",
-    )(orders_by_slot, panel_modes, basis)
-    columns = columns.reshape(group_count, 1, pair_count * mode_count)
+    )(orders_by_slot, panel_modes, pltpu.with_memory_space_constraint(basis, pltpu.HBM))
     columns = lax.all_to_all(columns, "lat", split_axis=0, concat_axis=0, tiled=True)
-    columns = jnp.sum(columns.astype(jnp.float32), axis=(0, 1)).reshape(pair_count, mode_count)
+    columns = jnp.sum(columns.astype(jnp.float32), axis=0).reshape(-1, mode_count)[:pair_count]
 
     table = jnp.asarray(dft_table(lon_count, order_count))
     halves = [
@@ -176,24 +230,47 @@
     mode_side = jnp.where(mode_odd, mode_parts[:, 1], mode_parts[:, 0]).astype(jnp.float32)
     values = swapped_pair_sum(jnp.sum(mode_side * columns.T[:, :, None], axis=1))
     reach = 2
-    while 4 * reach < group_count:
+    while 8 * reach < group_count:
         values = stepped(values, reach)
         reach *= 2
+    by_source, same = pl.pallas_call(
+        functools.partial(basis_kernel, sources=group_count),
+        in_specs=[in_vmem, in_hbm],
+        out_specs=(in_hbm, in_vmem),
+        out_shape=(
+            pltpu.HBM(basis.shape, jnp.bfloat16),
+            jax.ShapeDtypeStruct(values.shape, jnp.float32),
+        ),
+        scratch_shapes=[
+            pltpu.VMEM(basis.shape, jnp.bfloat16),
+            pltpu.VMEM(basis.shape, jnp.bfloat16),
+            pltpu.SemaphoreType.DMA((slot_count,)),
+            pltpu.SemaphoreType.DMA((slot_count,)),
+        ],
+        compiler_params=roomy,
+        name="basis",
+    )(values, pltpu.with_memory_space_constraint(basis, pltpu.HBM))
+    values = same + from_far(values, reach)
+    reach *= 2
 
     def coefficients(block, first):
         count = slot_count // 2
         return pl.pallas_call(
             functools.partial(coefficient_kernel, first=first),
-            in_specs=[in_smem, in_vmem, anywhere],
+            in_specs=[in_smem, in_vmem, in_hbm],
             out_specs=in_vmem,
-            out_shape=jax.ShapeDtypeStruct((count, wide, deg_count), jnp.bfloat16),
+            out_shape=pltpu.VMEM((count, wide, deg_count), jnp.bfloat16),
             scratch_shapes=[
                 pltpu.VMEM((count, pair_total, deg_count), jnp.bfloat16),
-                pltpu.VMEM((pair_total, pair_total), jnp.bfloat16),
                 pltpu.SemaphoreType.DMA((count,)),
             ],
-            name="coefficients",
-        )(orders_by_slot, block, basis)
+            compiler_params=roomy,
+        name="coefficients",
+        )(
+            orders_by_slot,
+            pltpu.with_memory_space_constraint(block, pltpu.VMEM),
+            pltpu.with_memory_space_constraint(by_source, pltpu.HBM),
+        )
 
     values, received = lax.optimization_barrier((values, received))
     first_half = coefficients(received, 0)
@@ -201,14 +278,6 @@
     values, first_half, received = lax.optimization_barrier((values, first_half, received))
     last_half = coefficients(received, slot_count // 2)
     values = stepped(values, 2 * reach)
-    values, last_half = lax.optimization_barrier((values, last_half))
-
-    values = lax.reduce_precision(values, 8, 7).reshape(2 * mode_count, snap_count)
-    centered = (values - jnp.mean(values, axis=1, keepdims=True)).astype(jnp.bfloat16).T
-    blank = jnp.zeros_like(centered)
-    centered = jnp.concatenate(
-        [jnp.concatenate([centered, blank], 1), jnp.concatenate([blank, centered], 1)], 0
-    )
     return pl.pallas_call(
         functools.partial(panel_kernel, scale=1.0 / (snap_count - 1)),
         in_specs=[in_vmem, in_vmem, in_vmem],
@@ -218,8 +287,13 @@
             pltpu.VMEM((slot_count, 2 * deg_count, 2 * mode_count), jnp.bfloat16),
             pltpu.SemaphoreType.DMA((slot_count,)),
         ],
+        compiler_params=roomy,
         name="panel",
-    )(first_half, last_half, centered)
+    )(
+        pltpu.with_memory_space_constraint(first_half, pltpu.VMEM),
+        pltpu.with_memory_space_constraint(last_half, pltpu.VMEM),
+        pltpu.with_memory_space_constraint(values, pltpu.VMEM),
+    )
 
 
 def solution(mesh):

time: 104 us -> 97.5 us (0.938)
  waiting for transfers between devices: 35.3 us -> 29.1 us
  Pallas kernels: 17.2 us -> 19.6 us
  local copies, waits for them, and re-layouts: 4.41 us -> 2.17 us
  starting transfers between devices: 38.8 us -> 39.9 us
    pallas_call x1 -> x2, Pallas kernels: 1.9 us -> 8.46 us  [the longest x1 6.52 us: local(): pl.pallas_call(functools.partial(basis_kernel, sources=group_count), in_s...]
    ppermute x6, waiting for transfers between devices: 21.3 us -> 15.6 us  [from_far(): return lax.ppermute(block, 'lat', [(i, i ^ reach) for i in range(count)])]
    pallas_call x2, Pallas kernels: 11.8 us -> 8.59 us  [coefficients(): pl.pallas_call(functools.partial(coefficient_kernel, first=first), in_spe...]
    reshape x4 -> x1, local copies, waits for them, and re-layouts: 1.81 us -> 0.08 us  [local(): jnp.sum(columns.astype(jnp.float32), axis=0).reshape(-1, mode_count)]
    unnamed x12 -> x10, local copies, waits for them, and re-layouts: 2.28 us -> 1.77 us
  transfers between devices with their start and end apart: 10 -> 10, of which waited for: 8 -> 8; matrix products, arithmetic and copies ran while one was open for 7% -> 7% of each run, Pallas kernels for 11% -> 16%
where the time goes in v4:
time: 97.5 us; the launch traced here: 97.3 us
  starting transfers between devices  39.9 us (41%)
  waiting for transfers between devices  29.1 us (30%)
  Pallas kernels  19.6 us (20%)
  matrix products  5.37 us (6%)
  local copies, waits for them, and re-layouts  2.17 us (2%)
    all_to_all x1, starting transfers between devices, local(): lax.all_to_all(columns, 'lat', split_axis=0, concat_axis=0, tiled=True)  16.6 us
    ppermute x6, waiting for transfers between devices, from_far(): return lax.ppermute(block, 'lat', [(i, i ^ reach) for i in range(count)])  15.6 us
    ppermute x6, starting transfers between devices, from_far(): return lax.ppermute(block, 'lat', [(i, i ^ reach) for i in range(count)])  12.4 us
    all_to_all x1, starting transfers between devices, local(): lax.all_to_all(sent, 'lat', split_axis=0, concat_axis=0, tiled=True)  9.77 us
    pallas_call x2, Pallas kernels, coefficients(): pl.pallas_call(functools.partial(coefficient_kernel, first=first), in_spe...  8.59 us
    all_to_all x1, waiting for transfers between devices, local(): lax.all_to_all(sent, 'lat', split_axis=0, concat_axis=0, tiled=True)  6.92 us
    pallas_call x1, Pallas kernels, local(): pl.pallas_call(functools.partial(basis_kernel, sources=group_count), in_s...  6.52 us
    all_to_all x1, waiting for transfers between devices, local(): lax.all_to_all(columns, 'lat', split_axis=0, concat_axis=0, tiled=True)  4.1 us
  transfers between devices with their start and end apart: 10, of which 8 were waited for; matrix products, arithmetic and copies ran while one was open for 7% of the time, Pallas kernels for 16%

profile of v4, /device:TPU:2, one launch (start us, length us, event | category | flops | bytes accessed | tf_op | source)
XLA Modules:
  0.0 97.3 jit_solution(17658956245940987774)
XLA Ops:
  0.0 0.0 copy-start
  0.0 0.0 copy-start.1
  0.0 1.9 %columns.1 = bf16[128,2,128]{2,1,0:T(2,128)(2,1)} custom-call(s32[8,128]{1,0:T(8,128)} %bitcast.48, s32[2,64]{1,0:T(2,128)} %modes_ref.1, bf16[8,384,768]{2,1,0:T(8,128)(2,1)} %basis_ref.3), custom_call_target="tpu_custom_call" | custom-call | tf_op jit(solution)/shard_map/columns/pallas_call | solution.py:187
  1.9 16.6 %all-to-all-start = ((bf16[128,2,128]{2,1,0:T(2,128)(2,1)}), bf16[128,2,128]{2,1,0:T(2,128)(2,1)S(1)}, u32[]{:S(2)}, u32[]{:S(2)}) async-start(bf16[128,2,128]{2,1,0:T(2,128)(2,1)} %columns.1), calls=%async_computation | async-start | bytes 131072 | tf_op jit(solution)/shard_map/all_to_all | solution.py:200
  18.6 0.0 copy-done
  18.6 0.1 copy.12
  18.7 0.1 eq.44
  18.8 0.0 copy-done.1
  18.8 0.0 copy-start.3
  18.8 0.1 copy.16
  18.9 1.5 %copy-done.3 = bf16[768,2,768,1,1]{2,0,4,3,1:T(8,128)(2,1)S(1)} copy-done((bf16[768,2,768,1,1]{2,0,4,3,1:T(8,128)(2,1)S(1)}, bf16[768,2,768,1,1]{2,0,4,3,1:T(8,128)(2,1)}, u32[]{:S(2)}) %copy-start.3) | copy-done | bytes 2359320
  20.5 1.1 %fusion.4 = f32[2,768,64,2,3]{1,2,4,3,0:T(8,128)S(1)} fusion(bf16[768,2,768,1,1]{2,0,4,3,1:T(8,128)(2,1)S(1)} %copy-done.3, bf16[64,2,3,1536]{3,0,2,1:T(8,128)(2,1)S(1)} %bitcast.53), kind=kOutput, calls=%fused_computation.13 | convolution fusion | flops 905969664 | bytes 5308416 | tf_op jit(solution)/shard_map/thjn,nrm->hjrtm/dot_general | solution.py:205
  21.5 1.1 %multiply_bitcast_fusion = f32[2,3,2,64,768]{4,3,1,0,2:T(8,128)S(1)} fusion(f32[2,768,64,2,3]{1,2,4,3,0:T(8,128)S(1)} %fusion.4, bf16[768,2,768,1,1]{2,0,4,3,1:T(8,128)(2,1)S(1)} %copy-done.3, f32[768]{0:T(1024)S(1)} %fusion.9, bf16[64,2,3,1536]{3,0,2,1:T(8,128)(2,1)S(1)} %bitcast.54), kind=kOutput, calls=%fused_computation.2 | convolution fusion | flops 907739136 | bytes 7671808 | tf_op jit(solution)/shard_map/thjn,nrm->hjrtm/dot_general | solution.py:205
  22.7 0.2 add_convert_fusion
  22.9 0.1 pad_maximum_fusion
  23.0 0.1 copy.9
  23.1 2.7 %fusion.3 = bf16[128,48,128]{2,1,0:T(8,128)(2,1)} fusion(bf16[768,768]{1,0:T(8,128)(2,1)S(1)} %bitcast.51, s32[1024]{0:T(1024)S(1)} %eq.44), kind=kOutput, calls=%fused_computation.5 | convolution fusion | flops 1209532416 | bytes 2756608 | tf_op jit(solution)/shard_map/dot_general | solution.py:215
  25.8 0.0 copy-start.2
  25.8 4.1 %all-to-all-done = bf16[128,2,128]{2,1,0:T(2,128)(2,1)S(1)} async-done(((bf16[128,2,128]{2,1,0:T(2,128)(2,1)}), bf16[128,2,128]{2,1,0:T(2,128)(2,1)S(1)}, u32[]{:S(2)}, u32[]{:S(2)}) %all-to-all-start) | async-done | bytes 65568 | tf_op jit(solution)/shard_map/all_to_all | solution.py:200
  29.9 9.8 %all-to-all-start.1 = ((bf16[128,48,128]{2,1,0:T(8,128)(2,1)}), bf16[128,48,128]{2,1,0:T(8,128)(2,1)S(1)}, u32[]{:S(2)}, u32[]{:S(2)}) async-start(bf16[128,48,128]{2,1,0:T(8,128)(2,1)} %fusion.3), calls=%async_computation.1 | async-start | bytes 3145728 | tf_op jit(solution)/shard_map/all_to_all | solution.py:226
  39.7 0.0 copy-done.2
  39.7 0.5 convolution_convert_fusion
  40.3 0.1 convert_reduce_fusion
  40.4 0.1 reshape.52
  40.5 0.1 copy.11
  40.6 0.2 multiply_reduce_fusion
  40.8 0.1 collective-permute-start.1
  40.9 1.0 %collective-permute-start = (f32[64,128]{1,0:T(8,128)S(1)}, f32[64,128]{1,0:T(8,128)S(1)}, u32[]{:S(2)}, u32[]{:S(2)}) collective-permute-start(f32[64,128]{1,0:T(8,128)S(1)} %multiply_reduce_fusion), channel_id=1, source_target_pairs={{0,1},{1,0},{2,3},{3,2},{4,5},{5,4},{6,7},{7,6},{8,9},{9,8},{10,11... | collective-permute-start | bytes 98312 | tf_op jit(solution)/shard_map/ppermute | solution.py:33
  41.9 2.5 %collective-permute-done.1 = f32[64,128]{1,0:T(8,128)S(1)} collective-permute-done((f32[64,128]{1,0:T(8,128)S(1)}, f32[64,128]{1,0:T(8,128)S(1)}, u32[]{:S(2)}, u32[]{:S(2)}) %collective-permute-start.1) | collective-permute-done | bytes 32800 | tf_op jit(solution)/shard_map/ppermute | solution.py:33
  44.4 0.0 collective-permute-done
  44.4 2.2 %collective-permute-start.2 = (f32[64,128]{1,0:T(8,128)S(1)}, f32[64,128]{1,0:T(8,128)S(1)}, u32[]{:S(2)}, u32[]{:S(2)}) collective-permute-start(f32[64,128]{1,0:T(8,128)S(1)} %add.53), channel_id=1, source_target_pairs={{0,4},{2,6},{4,0},{6,2},{8,12},{10,14},{12,8},{14,10},{16,20},{18,... | collective-permute-start | bytes 98312 | tf_op jit(solution)/shard_map/ppermute | solution.py:21
  46.6 3.9 %collective-permute-done.2 = f32[64,128]{1,0:T(8,128)S(1)} collective-permute-done((f32[64,128]{1,0:T(8,128)S(1)}, f32[64,128]{1,0:T(8,128)S(1)}, u32[]{:S(2)}, u32[]{:S(2)}) %collective-permute-start.2) | collective-permute-done | bytes 32800 | tf_op jit(solution)/shard_map/ppermute | solution.py:21
  50.5 1.9 %collective-permute-start.3 = (f32[64,128]{1,0:T(8,128)S(1)}, f32[64,128]{1,0:T(8,128)S(1)}, u32[]{:S(2)}, u32[]{:S(2)}) collective-permute-start(f32[64,128]{1,0:T(8,128)S(1)} %add.54), channel_id=1, source_target_pairs={{0,8},{2,10},{4,12},{6,14},{8,0},{10,2},{12,4},{14,6},{16,24},{18,... | collective-permute-start | bytes 98312 | tf_op jit(solution)/shard_map/ppermute | solution.py:21
  52.4 2.0 %collective-permute-done.3 = f32[64,128]{1,0:T(8,128)S(1)} collective-permute-done((f32[64,128]{1,0:T(8,128)S(1)}, f32[64,128]{1,0:T(8,128)S(1)}, u32[]{:S(2)}, u32[]{:S(2)}) %collective-permute-start.3) | collective-permute-done | bytes 32800 | tf_op jit(solution)/shard_map/ppermute | solution.py:21
  54.5 3.0 %collective-permute-start.4 = (f32[64,128]{1,0:T(8,128)S(1)}, f32[64,128]{1,0:T(8,128)S(1)}, u32[]{:S(2)}, u32[]{:S(2)}) collective-permute-start(f32[64,128]{1,0:T(8,128)S(1)} %add.55), channel_id=1, source_target_pairs={{0,16},{2,18},{4,20},{6,22},{8,24},{10,26},{12,28},{14,30},{16,0},... | collective-permute-start | bytes 98312 | tf_op jit(solution)/shard_map/ppermute | solution.py:21
  57.5 2.7 %collective-permute-done.4 = f32[64,128]{1,0:T(8,128)S(1)} collective-permute-done((f32[64,128]{1,0:T(8,128)S(1)}, f32[64,128]{1,0:T(8,128)S(1)}, u32[]{:S(2)}, u32[]{:S(2)}) %collective-permute-start.4) | collective-permute-done | bytes 32800 | tf_op jit(solution)/shard_map/ppermute | solution.py:21
  60.2 2.1 %collective-permute-start.5 = (f32[64,128]{1,0:T(8,128)S(1)}, f32[64,128]{1,0:T(8,128)S(1)}, u32[]{:S(2)}, u32[]{:S(2)}) collective-permute-start(f32[64,128]{1,0:T(8,128)S(1)} %add.56.values_ref), channel_id=1, source_target_pairs={{0,32},{2,34},{4,36},{6,38},{8,40},{10,42},{12,44},{14,46},{16,48}... | collective-permute-start | bytes 98312 | tf_op jit(solution)/shard_map/ppermute | solution.py:21
  62.3 6.5 %basis.1 = (bf16[8,384,768]{2,1,0:T(8,128)(2,1)}, f32[64,128]{1,0:T(8,128)S(1)}) custom-call(f32[64,128]{1,0:T(8,128)S(1)} %add.56.values_ref, bf16[8,384,768]{2,1,0:T(8,128)(2,1)} %basis_ref.3), custom_call_target="tpu_custom_call" | custom-call | tf_op jit(solution)/shard_map/basis/pallas_call | solution.py:236
  68.8 5.7 %collective-permute-done.5 = f32[64,128]{1,0:T(8,128)S(1)} collective-permute-done((f32[64,128]{1,0:T(8,128)S(1)}, f32[64,128]{1,0:T(8,128)S(1)}, u32[]{:S(2)}, u32[]{:S(2)}) %collective-permute-start.5) | collective-permute-done | bytes 32800 | tf_op jit(solution)/shard_map/ppermute | solution.py:21
  74.5 6.9 %all-to-all-done.1.received_ref = bf16[128,48,128]{2,1,0:T(8,128)(2,1)S(1)} async-done(((bf16[128,48,128]{2,1,0:T(8,128)(2,1)}), bf16[128,48,128]{2,1,0:T(8,128)(2,1)S(1)}, u32[]{:S(2)}, u32[]{:S(2)}) %all-to-all-start.1) | async-done | bytes 1572896 | tf_op jit(solution)/shard_map/all_to_all | solution.py:226
  81.4 0.6 collective-permute-start.6
  82.0 4.3 %coefficients.2.first_ref = bf16[4,128,768]{2,1,0:T(8,128)(2,1)S(1)} custom-call(s32[8,128]{1,0:T(8,128)S(1)} %bitcast.49, bf16[128,48,128]{2,1,0:T(8,128)(2,1)S(1)} %all-to-all-done.1.received_ref, bf16[8,384,768]{2,1,0:T(8,128)(2,1)} %get-tuple-element.15.basis_ref), custom_call_target="tpu_custom_call" | custom-call | tf_op jit(solution)/shard_map/coefficients/pallas_call | solution.py:258
  86.3 0.0 collective-permute-done.6
  86.3 2.6 %collective-permute-start.7 = (f32[64,128]{1,0:T(8,128)S(1)}, f32[64,128]{1,0:T(8,128)S(1)}, u32[]{:S(2)}, u32[]{:S(2)}) collective-permute-start(f32[64,128]{1,0:T(8,128)S(1)} %add.58), channel_id=1, source_target_pairs={{0,128},{2,130},{4,132},{6,134},{8,136},{10,138},{12,140},{14,142}... | collective-permute-start | bytes 98312 | tf_op jit(solution)/shard_map/ppermute | solution.py:21
  88.9 4.3 %coefficients.3.last_ref = bf16[4,128,768]{2,1,0:T(8,128)(2,1)S(1)} custom-call(s32[8,128]{1,0:T(8,128)S(1)} %bitcast.50, bf16[128,48,128]{2,1,0:T(8,128)(2,1)S(1)} %all-to-all-done.1.received_ref, bf16[8,384,768]{2,1,0:T(8,128)(2,1)} %get-tuple-element.15.basis_ref), custom_call_target="tpu_custom_call" | custom-call | tf_op jit(solution)/shard_map/coefficients/pallas_call | solution.py:258
  93.2 1.3 %collective-permute-done.7 = f32[64,128]{1,0:T(8,128)S(1)} collective-permute-done((f32[64,128]{1,0:T(8,128)S(1)}, f32[64,128]{1,0:T(8,128)S(1)}, u32[]{:S(2)}, u32[]{:S(2)}) %collective-permute-start.7) | collective-permute-done | bytes 32800 | tf_op jit(solution)/shard_map/ppermute | solution.py:21
  94.6 2.5 %panel.1 = bf16[1,8,1536,128]{3,2,1,0:T(8,128)(2,1)} custom-call(bf16[4,128,768]{2,1,0:T(8,128)(2,1)S(1)} %coefficients.2.first_ref, bf16[4,128,768]{2,1,0:T(8,128)(2,1)S(1)} %coefficients.3.last_ref, f32[64,128]{1,0:T(8,128)S(1)} %add.59.values_ref), custom_call_target="tpu_custom_call" | custom-call | tf_op jit(solution)/shard_map/panel/pallas_call | solution.py:281
  (12 shorter events, 0.1 us)
Async XLA Ops:
  0.0 18.6 %copy-start = (s32[128,8]{0,1:T(8,128)S(1)}, s32[128,8]{0,1:T(8,128)}, u32[]{:S(2)}) copy-start(s32[128,8]{0,1:T(8,128)} %param.7) | copy-start | bytes 12292
  0.0 18.8 %copy-start.1 = (bf16[1,64,2,3,1536]{4,2,3,1,0:T(2,128)(2,1)S(1)}, bf16[1,64,2,3,1536]{4,2,3,1,0:T(2,128)(2,1)}, u32[]{:S(2)}) copy-start(bf16[1,64,2,3,1536]{4,2,3,1,0:T(2,128)(2,1)} %param.5) | copy-start | bytes 3538948
  1.9 27.9 %all-to-all-start = ((bf16[128,2,128]{2,1,0:T(2,128)(2,1)}), bf16[128,2,128]{2,1,0:T(2,128)(2,1)S(1)}, u32[]{:S(2)}, u32[]{:S(2)}) async-start(bf16[128,2,128]{2,1,0:T(2,128)(2,1)} %columns.1), calls=%async_computation | async-start | bytes 131072 | tf_op jit(solution)/shard_map/all_to_all | solution.py:200
  18.8 1.7 %copy-start.3 = (bf16[768,2,768,1,1]{2,0,4,3,1:T(8,128)(2,1)S(1)}, bf16[768,2,768,1,1]{2,0,4,3,1:T(8,128)(2,1)}, u32[]{:S(2)}) copy-start(bf16[768,2,768,1,1]{2,0,4,3,1:T(8,128)(2,1)} %constant.38) | copy-start | bytes 7077892
  25.8 13.9 %copy-start.2 = (s32[2,64]{1,0:T(2,128)S(1)}, s32[2,64]{1,0:T(2,128)}, u32[]{:S(2)}) copy-start(s32[2,64]{1,0:T(2,128)} %modes_ref.1) | copy-start | bytes 1540
  29.9 51.5 %all-to-all-start.1 = ((bf16[128,48,128]{2,1,0:T(8,128)(2,1)}), bf16[128,48,128]{2,1,0:T(8,128)(2,1)S(1)}, u32[]{:S(2)}, u32[]{:S(2)}) async-start(bf16[128,48,128]{2,1,0:T(8,128)(2,1)} %fusion.3), calls=%async_computation.1 | async-start | bytes 3145728 | tf_op jit(solution)/shard_map/all_to_all | solution.py:226
  40.8 3.6 %collective-permute-start.1 = (f32[64,128]{1,0:T(8,128)S(1)}, f32[64,128]{1,0:T(8,128)S(1)}, u32[]{:S(2)}, u32[]{:S(2)}) collective-permute-start(f32[64,128]{1,0:T(8,128)S(1)} %multiply_reduce_fusion), channel_id=1, source_target_pairs={{0,3},{1,2},{2,1},{3,0},{4,7},{5,6},{6,5},{7,4},{8,11},{9,10},{10,... | collective-permute-start | bytes 98312 | tf_op jit(solution)/shard_map/ppermute | solution.py:33
  40.9 3.5 %collective-permute-start = (f32[64,128]{1,0:T(8,128)S(1)}, f32[64,128]{1,0:T(8,128)S(1)}, u32[]{:S(2)}, u32[]{:S(2)}) collective-permute-start(f32[64,128]{1,0:T(8,128)S(1)} %multiply_reduce_fusion), channel_id=1, source_target_pairs={{0,1},{1,0},{2,3},{3,2},{4,5},{5,4},{6,7},{7,6},{8,9},{9,8},{10,11... | collective-permute-start | bytes 98312 | tf_op jit(solution)/shard_map/ppermute | solution.py:33
  44.4 6.1 %collective-permute-start.2 = (f32[64,128]{1,0:T(8,128)S(1)}, f32[64,128]{1,0:T(8,128)S(1)}, u32[]{:S(2)}, u32[]{:S(2)}) collective-permute-start(f32[64,128]{1,0:T(8,128)S(1)} %add.53), channel_id=1, source_target_pairs={{0,4},{2,6},{4,0},{6,2},{8,12},{10,14},{12,8},{14,10},{16,20},{18,... | collective-permute-start | bytes 98312 | tf_op jit(solution)/shard_map/ppermute | solution.py:21
  50.5 3.9 %collective-permute-start.3 = (f32[64,128]{1,0:T(8,128)S(1)}, f32[64,128]{1,0:T(8,128)S(1)}, u32[]{:S(2)}, u32[]{:S(2)}) collective-permute-start(f32[64,128]{1,0:T(8,128)S(1)} %add.54), channel_id=1, source_target_pairs={{0,8},{2,10},{4,12},{6,14},{8,0},{10,2},{12,4},{14,6},{16,24},{18,... | collective-permute-start | bytes 98312 | tf_op jit(solution)/shard_map/ppermute | solution.py:21
  54.5 5.7 %collective-permute-start.4 = (f32[64,128]{1,0:T(8,128)S(1)}, f32[64,128]{1,0:T(8,128)S(1)}, u32[]{:S(2)}, u32[]{:S(2)}) collective-permute-start(f32[64,128]{1,0:T(8,128)S(1)} %add.55), channel_id=1, source_target_pairs={{0,16},{2,18},{4,20},{6,22},{8,24},{10,26},{12,28},{14,30},{16,0},... | collective-permute-start | bytes 98312 | tf_op jit(solution)/shard_map/ppermute | solution.py:21
  60.2 14.3 %collective-permute-start.5 = (f32[64,128]{1,0:T(8,128)S(1)}, f32[64,128]{1,0:T(8,128)S(1)}, u32[]{:S(2)}, u32[]{:S(2)}) collective-permute-start(f32[64,128]{1,0:T(8,128)S(1)} %add.56.values_ref), channel_id=1, source_target_pairs={{0,32},{2,34},{4,36},{6,38},{8,40},{10,42},{12,44},{14,46},{16,48}... | collective-permute-start | bytes 98312 | tf_op jit(solution)/shard_map/ppermute | solution.py:21
  81.4 4.9 %collective-permute-start.6 = (f32[64,128]{1,0:T(8,128)S(1)}, f32[64,128]{1,0:T(8,128)S(1)}, u32[]{:S(2)}, u32[]{:S(2)}) collective-permute-start(f32[64,128]{1,0:T(8,128)S(1)} %add.57), channel_id=1, source_target_pairs={{0,64},{2,66},{4,68},{6,70},{8,72},{10,74},{12,76},{14,78},{16,80}... | collective-permute-start | bytes 98312 | tf_op jit(solution)/shard_map/ppermute | solution.py:21
  86.3 8.2 %collective-permute-start.7 = (f32[64,128]{1,0:T(8,128)S(1)}, f32[64,128]{1,0:T(8,128)S(1)}, u32[]{:S(2)}, u32[]{:S(2)}) collective-permute-start(f32[64,128]{1,0:T(8,128)S(1)} %add.58), channel_id=1, source_target_pairs={{0,128},{2,130},{4,132},{6,134},{8,136},{10,138},{12,140},{14,142}... | collective-permute-start | bytes 98312 | tf_op jit(solution)/shard_map/ppermute | solution.py:21

commit v5 on v4

--- a/solution.py
+++ b/solution.py
@@ -70,13 +70,14 @@
 
 
 def basis_kernel(
-    values_ref, basis_ref, out_ref, same_ref, held_ref, rows_ref, sems, out_sems, *, sources
+    values_ref, basis_ref, out_ref, same_ref, held_ref, rows_ref, sems, out_sems, *, first, sources
 ):
     same_ref[...] = values_ref[...]
-    slots, pairs, _ = out_ref.shape
+    slots, _, pairs = out_ref.shape
     share = pairs // sources
     copies = [
-        pltpu.make_async_copy(basis_ref.at[s], held_ref.at[s], sems.at[s]) for s in range(slots)
+        pltpu.make_async_copy(basis_ref.at[first + s], held_ref.at[s], sems.at[s])
+        for s in range(slots)
     ]
     out_copies = [
         pltpu.make_async_copy(rows_ref.at[s], out_ref.at[s], out_sems.at[s]) for s in range(slots)
@@ -85,58 +86,22 @@
         copy.start()
     row = lax.broadcasted_iota(jnp.int32, (pairs, pairs), 0)
     column = lax.broadcasted_iota(jnp.int32, (pairs, pairs), 1)
-    place = one_hot(share * (row % sources) + row // sources == column)
+    place = one_hot(share * (column % sources) + column // sources == row)
     for s in range(slots):
         copies[s].wait()
-        rows = jnp.dot(place, held_ref[s], preferred_element_type=jnp.float32)
+        rows = lax.dot_general(
+            held_ref[s], place, (((0,), (0,)), ((), ())), preferred_element_type=jnp.float32
+        )
         rows_ref[s] = rows.astype(jnp.bfloat16)
         out_copies[s].start()
     for copy in out_copies:
         copy.wait()
 
 
-def coefficient_kernel(orders_ref, received_ref, basis_ref, out_ref, held_ref, sems, *, first):
-    group = lax.axis_index("lat")
-    slots, pairs, degrees = basis_ref.shape
-    sources, _, wide = received_ref.shape
-    share = pairs // sources
-    here = out_ref.shape[0]
-    copies = [
-        pltpu.make_async_copy(basis_ref.at[first + s], held_ref.at[s], sems.at[s])
-        for s in range(here)
-    ]
-    for copy in copies:
-        copy.start()
-    degree = lax.broadcasted_iota(jnp.int32, (1, degrees), 1)
-    for s in range(here):
-        sides = [
-            jnp.concatenate(
-                [
-                    received_ref[:, (parity * share + j) * slots + first + s, :]
-                    for j in range(share)
-                ],
-                axis=0,
-            )
-            for parity in range(2)
-        ]
-        copies[s].wait()
-        both = lax.dot_general(
-            jnp.concatenate(sides, axis=1),
-            held_ref[s],
-            (((0,), (0,)), ((), ())),
-            preferred_element_type=jnp.float32,
-        )
-        order = orders_ref[first + s, group]
-        odd = ((degree - order) & 1) == 1
-        keep = (degree >= order) & (order >= 0)
-        chosen = jnp.where(odd, both[wide:], both[:wide])
-        out_ref[s] = jnp.where(keep, chosen, 0.0).astype(jnp.bfloat16)
-
-
-def panel_kernel(first_ref, last_ref, values_ref, out_ref, rows_ref, sems, *, scale):
-    modes, wide = values_ref.shape
+def centered_columns(values):
+    modes, wide = values.shape
     snaps = wide // 2
-    values = values_ref[...].astype(jnp.bfloat16).astype(jnp.float32)
+    values = values.astype(jnp.bfloat16).astype(jnp.float32)
     mode = lax.broadcasted_iota(jnp.int32, (modes, 2 * modes), 0)
     column = lax.broadcasted_iota(jnp.int32, (modes, 2 * modes), 1)
     block = jnp.zeros((snaps, 2 * modes), jnp.float32)
@@ -151,20 +116,61 @@
         )
     block = block.astype(jnp.bfloat16)
     blank = jnp.zeros_like(block)
-    centered = jnp.concatenate(
+    return jnp.concatenate(
         [jnp.concatenate([block, blank], axis=1), jnp.concatenate([blank, block], axis=1)], axis=0
     )
-    half = first_ref.shape[0]
+
+
+def panel_kernel(
+    orders_ref,
+    received_ref,
+    first_ref,
+    last_ref,
+    values_ref,
+    out_ref,
+    held_ref,
+    rows_ref,
+    sems,
+    out_sems,
+    *,
+    scale,
+):
+    group = lax.axis_index("lat")
+    slots, degrees, pairs = held_ref.shape
+    half = slots // 2
+    sources, _, wide = received_ref.shape
+    share = pairs // sources
     copies = []
-    for s in range(2 * half):
-        rows = first_ref[s] if s < half else last_ref[s - half]
-        products = lax.dot_general(
-            rows, centered, (((0,), (0,)), ((), ())), preferred_element_type=jnp.float32
-        )
+    for s in range(slots):
+        source = first_ref.at[s] if s < half else last_ref.at[s - half]
+        copies.append(pltpu.make_async_copy(source, held_ref.at[s], sems.at[s]))
+        copies[s].start()
+    out_copies = [
+        pltpu.make_async_copy(rows_ref.at[s], out_ref.at[0, s], out_sems.at[s])
+        for s in range(slots)
+    ]
+    centered = centered_columns(values_ref[...])
+    degree = lax.broadcasted_iota(jnp.int32, (degrees, 1), 0)
+    for s in range(slots):
+        sides = [
+            jnp.concatenate(
+                [received_ref[:, (parity * share + j) * slots + s, :] for j in range(share)], axis=0
+            )
+            for parity in range(2)
+        ]
+        copies[s].wait()
+        both = jnp.dot(
+            held_ref[s], jnp.concatenate(sides, axis=1), preferred_element_type=jnp.float32
+        )
+        order = orders_ref[s, group]
+        odd = ((degree - order) & 1) == 1
+        keep = (degree >= order) & (order >= 0)
+        chosen = jnp.where(odd, both[:, wide:], both[:, :wide])
+        coefficients = jnp.where(keep, chosen, 0.0).astype(jnp.bfloat16)
+        products = jnp.dot(coefficients, centered, preferred_element_type=jnp.float32)
         rows_ref[s] = (products * scale).astype(jnp.bfloat16).reshape(rows_ref.shape[1:])
-        copies.append(pltpu.make_async_copy(rows_ref.at[s], out_ref.at[0, s], sems.at[s]))
-        copies[-1].start()
-    for copy in copies:
+        out_copies[s].start()
+    for copy in out_copies:
         copy.wait()
 
 
@@ -201,12 +207,12 @@
     columns = jnp.sum(columns.astype(jnp.float32), axis=0).reshape(-1, mode_count)[:pair_count]
 
     table = jnp.asarray(dft_table(lon_count, order_count))
-    halves = [
+    products = [
         jnp.einsum("thjn,nrm->hjrtm", half, table, preferred_element_type=jnp.float32)
         for half in (grid_one[..., :order_count], grid_one[..., order_count:])
     ]
     sign = 1.0 - 2.0 * (lax.iota(jnp.int32, order_count) % 2).astype(jnp.float32)
-    fourier = (halves[0] + halves[1] * sign) * (1.0 / math.sqrt(lon_count))
+    fourier = (products[0] + products[1] * sign) * (1.0 / math.sqrt(lon_count))
     parts = jnp.stack([fourier[0] + fourier[1], fourier[0] - fourier[1]]).astype(jnp.bfloat16)
     parts = parts.reshape(2 * pair_count * wide, order_count)
 
@@ -229,69 +235,53 @@
     mode_odd = ((mode_degree - mode_order) % 2 == 1)[:, None, None]
     mode_side = jnp.where(mode_odd, mode_parts[:, 1], mode_parts[:, 0]).astype(jnp.float32)
     values = swapped_pair_sum(jnp.sum(mode_side * columns.T[:, :, None], axis=1))
-    reach = 2
-    while 8 * reach < group_count:
-        values = stepped(values, reach)
-        reach *= 2
-    by_source, same = pl.pallas_call(
-        functools.partial(basis_kernel, sources=group_count),
-        in_specs=[in_vmem, in_hbm],
-        out_specs=(in_hbm, in_vmem),
-        out_shape=(
-            pltpu.HBM(basis.shape, jnp.bfloat16),
-            jax.ShapeDtypeStruct(values.shape, jnp.float32),
-        ),
-        scratch_shapes=[
-            pltpu.VMEM(basis.shape, jnp.bfloat16),
-            pltpu.VMEM(basis.shape, jnp.bfloat16),
-            pltpu.SemaphoreType.DMA((slot_count,)),
-            pltpu.SemaphoreType.DMA((slot_count,)),
-        ],
-        compiler_params=roomy,
-        name="basis",
-    )(values, pltpu.with_memory_space_constraint(basis, pltpu.HBM))
-    values = same + from_far(values, reach)
-    reach *= 2
-
-    def coefficients(block, first):
+    halves = []
+    for reach in (2, 4, 8):
+        if reach == 2:
+            values = stepped(values, reach)
+            continue
         count = slot_count // 2
-        return pl.pallas_call(
-            functools.partial(coefficient_kernel, first=first),
-            in_specs=[in_smem, in_vmem, in_hbm],
-            out_specs=in_vmem,
-            out_shape=pltpu.VMEM((count, wide, deg_count), jnp.bfloat16),
+        half, same = pl.pallas_call(
+            functools.partial(basis_kernel, first=len(halves) * count, sources=group_count),
+            in_specs=[in_vmem, in_hbm],
+            out_specs=(in_hbm, in_vmem),
+            out_shape=(
+                pltpu.HBM((count, deg_count, pair_total), jnp.bfloat16),
+                jax.ShapeDtypeStruct(values.shape, jnp.float32),
+            ),
             scratch_shapes=[
                 pltpu.VMEM((count, pair_total, deg_count), jnp.bfloat16),
+                pltpu.VMEM((count, deg_count, pair_total), jnp.bfloat16),
+                pltpu.SemaphoreType.DMA((count,)),
                 pltpu.SemaphoreType.DMA((count,)),
             ],
             compiler_params=roomy,
-        name="coefficients",
-        )(
-            orders_by_slot,
-            pltpu.with_memory_space_constraint(block, pltpu.VMEM),
-            pltpu.with_memory_space_constraint(by_source, pltpu.HBM),
-        )
-
-    values, received = lax.optimization_barrier((values, received))
-    first_half = coefficients(received, 0)
-    values = stepped(values, reach)
-    values, first_half, received = lax.optimization_barrier((values, first_half, received))
-    last_half = coefficients(received, slot_count // 2)
-    values = stepped(values, 2 * reach)
+            name="basis",
+        )(values, pltpu.with_memory_space_constraint(basis, pltpu.HBM))
+        halves.append(pltpu.with_memory_space_constraint(half, pltpu.HBM))
+        values = same + from_far(values, reach)
+    plane = 16
+    own = values.astype(jnp.bfloat16)
+    for step in range(1, group_count // plane):
+        route = [(i, (i + step * plane) % group_count) for i in range(group_count)]
+        values = values + lax.ppermute(own, "lat", route).astype(jnp.float32)
     return pl.pallas_call(
         functools.partial(panel_kernel, scale=1.0 / (snap_count - 1)),
-        in_specs=[in_vmem, in_vmem, in_vmem],
+        in_specs=[in_smem, in_vmem, in_hbm, in_hbm, in_vmem],
         out_specs=anywhere,
         out_shape=jax.ShapeDtypeStruct((1, slot_count, 2 * deg_count, 2 * mode_count), jnp.bfloat16),
         scratch_shapes=[
+            pltpu.VMEM((slot_count, deg_count, pair_total), jnp.bfloat16),
             pltpu.VMEM((slot_count, 2 * deg_count, 2 * mode_count), jnp.bfloat16),
+            pltpu.SemaphoreType.DMA((slot_count,)),
             pltpu.SemaphoreType.DMA((slot_count,)),
         ],
         compiler_params=roomy,
         name="panel",
     )(
-        pltpu.with_memory_space_constraint(first_half, pltpu.VMEM),
-        pltpu.with_memory_space_constraint(last_half, pltpu.VMEM),
+        orders_by_slot,
+        pltpu.with_memory_space_constraint(received, pltpu.VMEM),
+        *halves,
         pltpu.with_memory_space_constraint(values, pltpu.VMEM),
     )
 

time: 97.5 us -> 94 us (0.964); the launches traced: 97.3 us -> 92.7 us
  waiting for transfers between devices: 29.1 us -> 13.4 us
  starting transfers between devices: 39.9 us -> 50.5 us
    ppermute x0 -> x7, starting transfers between devices: none -> 16.3 us  [local(): values = values + lax.ppermute(own, 'lat', route).astype(jnp.float32)]
    ppermute x6 -> x3, waiting for transfers between devices: 15.6 us -> 3.87 us  [from_far(): return lax.ppermute(block, 'lat', [(i, i ^ reach) for i in range(count)])]
    all_to_all x1, waiting for transfers between devices: 6.92 us -> 0.01 us  [local(): lax.all_to_all(sent, 'lat', split_axis=0, concat_axis=0, tiled=True)]
    pallas_call x1, Pallas kernels: 2.53 us -> 9.34 us  [local(): pl.pallas_call(functools.partial(panel_kernel, scale=1.0 / (snap_count -...]
    pallas_call x3 -> x2, Pallas kernels: 15.1 us -> 8.73 us  [local(): pl.pallas_call(functools.partial(basis_kernel, first=len(halves) * count,...]
    ppermute x6 -> x3, starting transfers between devices: 12.4 us -> 6.87 us  [from_far(): return lax.ppermute(block, 'lat', [(i, i ^ reach) for i in range(count)])]
    ppermute x0 -> x7, waiting for transfers between devices: none -> 2.97 us  [local(): values = values + lax.ppermute(own, 'lat', route).astype(jnp.float32)]
  transfers between devices with their start and end apart: 10 -> 14, of which waited for: 8 -> 6; matrix products, arithmetic and copies ran while one was open for 7% -> 7% of each run, Pallas kernels for 16% -> 9%
where the time goes in v5:
time: 94 us; the launch traced here: 92.7 us
  starting transfers between devices  50.5 us (54%)
  Pallas kernels  20 us (21%)
  waiting for transfers between devices  13.4 us (14%)
  matrix products  5.37 us (6%)
  local copies, waits for them, and re-layouts  2.17 us (2%)
    all_to_all x1, starting transfers between devices, local(): lax.all_to_all(columns, 'lat', split_axis=0, concat_axis=0, tiled=True)  16.5 us
    ppermute x7, starting transfers between devices, local(): values = values + lax.ppermute(own, 'lat', route).astype(jnp.float32)  16.3 us
    all_to_all x1, starting transfers between devices, local(): lax.all_to_all(sent, 'lat', split_axis=0, concat_axis=0, tiled=True)  9.77 us
    pallas_call x1, Pallas kernels, local(): pl.pallas_call(functools.partial(panel_kernel, scale=1.0 / (snap_count -...  9.34 us
    pallas_call x2, Pallas kernels, local(): pl.pallas_call(functools.partial(basis_kernel, first=len(halves) * count,...  8.73 us
    ppermute x3, starting transfers between devices, from_far(): return lax.ppermute(block, 'lat', [(i, i ^ reach) for i in range(count)])  6.87 us
    all_to_all x1, waiting for transfers between devices, local(): lax.all_to_all(columns, 'lat', split_axis=0, concat_axis=0, tiled=True)  4.1 us
    ppermute x3, waiting for transfers between devices, from_far(): return lax.ppermute(block, 'lat', [(i, i ^ reach) for i in range(count)])  3.87 us
  transfers between devices with their start and end apart: 14, of which 6 were waited for; matrix products, arithmetic and copies ran while one was open for 7% of the time, Pallas kernels for 9%

profile of v5, /device:TPU:2, one launch (start us, length us, event | category | flops | bytes accessed | tf_op | source)
XLA Modules:
  0.0 92.7 jit_solution(3417463873439250620)
XLA Ops:
  0.0 0.0 copy-start
  0.0 0.0 copy-start.1
  0.0 1.9 %columns.1 = bf16[128,2,128]{2,1,0:T(2,128)(2,1)} custom-call(s32[8,128]{1,0:T(8,128)} %bitcast.48, s32[2,64]{1,0:T(2,128)} %modes_ref.1, bf16[8,384,768]{2,1,0:T(8,128)(2,1)} %basis_ref.5), custom_call_target="tpu_custom_call" | custom-call | tf_op jit(solution)/shard_map/columns/pallas_call | solution.py:193
  1.9 16.5 %all-to-all-start.1 = ((bf16[128,2,128]{2,1,0:T(2,128)(2,1)}), bf16[128,2,128]{2,1,0:T(2,128)(2,1)S(1)}, u32[]{:S(2)}, u32[]{:S(2)}) async-start(bf16[128,2,128]{2,1,0:T(2,128)(2,1)} %columns.1), calls=%async_computation.1 | async-start | bytes 131072 | tf_op jit(solution)/shard_map/all_to_all | solution.py:206
  18.5 0.0 copy-done
  18.5 0.1 copy.8
  18.6 0.1 eq.40
  18.7 0.0 copy-done.1
  18.7 0.0 copy-start.3
  18.7 0.1 copy.16
  18.9 1.5 %copy-done.3 = bf16[768,2,768,1,1]{2,0,4,3,1:T(8,128)(2,1)S(1)} copy-done((bf16[768,2,768,1,1]{2,0,4,3,1:T(8,128)(2,1)S(1)}, bf16[768,2,768,1,1]{2,0,4,3,1:T(8,128)(2,1)}, u32[]{:S(2)}) %copy-start.3) | copy-done | bytes 2359320
  20.4 1.1 %fusion.4 = f32[2,768,64,2,3]{1,2,4,3,0:T(8,128)S(1)} fusion(bf16[768,2,768,1,1]{2,0,4,3,1:T(8,128)(2,1)S(1)} %copy-done.3, bf16[64,2,3,1536]{3,0,2,1:T(8,128)(2,1)S(1)} %bitcast.52), kind=kOutput, calls=%fused_computation.13 | convolution fusion | flops 905969664 | bytes 5308416 | tf_op jit(solution)/shard_map/thjn,nrm->hjrtm/dot_general | solution.py:211
  21.5 1.1 %multiply_bitcast_fusion = f32[2,3,2,64,768]{4,3,1,0,2:T(8,128)S(1)} fusion(f32[2,768,64,2,3]{1,2,4,3,0:T(8,128)S(1)} %fusion.4, bf16[768,2,768,1,1]{2,0,4,3,1:T(8,128)(2,1)S(1)} %copy-done.3, f32[768]{0:T(1024)S(1)} %fusion.9, bf16[64,2,3,1536]{3,0,2,1:T(8,128)(2,1)S(1)} %bitcast.53), kind=kOutput, calls=%fused_computation.2 | convolution fusion | flops 907739136 | bytes 7671808 | tf_op jit(solution)/shard_map/thjn,nrm->hjrtm/dot_general | solution.py:211
  22.6 0.2 add_convert_fusion
  22.8 0.1 pad_maximum_fusion
  22.9 0.1 copy.10
  23.0 2.7 %fusion.3 = bf16[128,48,128]{2,1,0:T(8,128)(2,1)} fusion(bf16[768,768]{1,0:T(8,128)(2,1)S(1)} %bitcast.50, s32[1024]{0:T(1024)S(1)} %eq.40), kind=kOutput, calls=%fused_computation.5 | convolution fusion | flops 1209532416 | bytes 2756608 | tf_op jit(solution)/shard_map/dot_general | solution.py:221
  25.7 0.0 copy-start.2
  25.7 4.1 %all-to-all-done.1 = bf16[128,2,128]{2,1,0:T(2,128)(2,1)S(1)} async-done(((bf16[128,2,128]{2,1,0:T(2,128)(2,1)}), bf16[128,2,128]{2,1,0:T(2,128)(2,1)S(1)}, u32[]{:S(2)}, u32[]{:S(2)}) %all-to-all-start.1) | async-done | bytes 65568 | tf_op jit(solution)/shard_map/all_to_all | solution.py:206
  29.8 9.8 %all-to-all-start = ((bf16[128,48,128]{2,1,0:T(8,128)(2,1)}), bf16[128,48,128]{2,1,0:T(8,128)(2,1)S(1)}, u32[]{:S(2)}, u32[]{:S(2)}) async-start(bf16[128,48,128]{2,1,0:T(8,128)(2,1)} %fusion.3), calls=%async_computation | async-start | bytes 3145728 | tf_op jit(solution)/shard_map/all_to_all | solution.py:232
  39.6 0.0 copy-done.2
  39.6 0.5 convolution_convert_fusion
  40.2 0.1 convert_reduce_fusion
  40.3 0.1 reshape.54
  40.4 0.1 copy.12
  40.5 0.2 multiply_reduce_fusion
  40.7 0.1 collective-permute-start.1
  40.8 1.0 %collective-permute-start = (f32[64,128]{1,0:T(8,128)S(1)}, f32[64,128]{1,0:T(8,128)S(1)}, u32[]{:S(2)}, u32[]{:S(2)}) collective-permute-start(f32[64,128]{1,0:T(8,128)S(1)} %multiply_reduce_fusion), channel_id=1, source_target_pairs={{0,1},{1,0},{2,3},{3,2},{4,5},{5,4},{6,7},{7,6},{8,9},{9,8},{10,11... | collective-permute-start | bytes 98312 | tf_op jit(solution)/shard_map/ppermute | solution.py:33
  41.8 2.5 %collective-permute-done.1 = f32[64,128]{1,0:T(8,128)S(1)} collective-permute-done((f32[64,128]{1,0:T(8,128)S(1)}, f32[64,128]{1,0:T(8,128)S(1)}, u32[]{:S(2)}, u32[]{:S(2)}) %collective-permute-start.1) | collective-permute-done | bytes 32800 | tf_op jit(solution)/shard_map/ppermute | solution.py:33
  44.3 0.0 collective-permute-done
  44.3 2.2 %collective-permute-start.2 = (f32[64,128]{1,0:T(8,128)S(1)}, f32[64,128]{1,0:T(8,128)S(1)}, u32[]{:S(2)}, u32[]{:S(2)}) collective-permute-start(f32[64,128]{1,0:T(8,128)S(1)} %add.65), channel_id=1, source_target_pairs={{0,4},{2,6},{4,0},{6,2},{8,12},{10,14},{12,8},{14,10},{16,20},{18,... | collective-permute-start | bytes 98312 | tf_op jit(solution)/shard_map/ppermute | solution.py:21
  46.5 3.9 %collective-permute-done.2 = f32[64,128]{1,0:T(8,128)S(1)} collective-permute-done((f32[64,128]{1,0:T(8,128)S(1)}, f32[64,128]{1,0:T(8,128)S(1)}, u32[]{:S(2)}, u32[]{:S(2)}) %collective-permute-start.2) | collective-permute-done | bytes 32800 | tf_op jit(solution)/shard_map/ppermute | solution.py:21
  50.4 1.9 %collective-permute-start.3 = (f32[64,128]{1,0:T(8,128)S(1)}, f32[64,128]{1,0:T(8,128)S(1)}, u32[]{:S(2)}, u32[]{:S(2)}) collective-permute-start(f32[64,128]{1,0:T(8,128)S(1)} %add.66.values_ref), channel_id=1, source_target_pairs={{0,8},{2,10},{4,12},{6,14},{8,0},{10,2},{12,4},{14,6},{16,24},{18,... | collective-permute-start | bytes 98312 | tf_op jit(solution)/shard_map/ppermute | solution.py:21
  52.3 4.4 %basis.2 = (bf16[4,768,384]{2,1,0:T(8,128)(2,1)}, f32[64,128]{1,0:T(8,128)S(1)}) custom-call(f32[64,128]{1,0:T(8,128)S(1)} %add.66.values_ref, bf16[8,384,768]{2,1,0:T(8,128)(2,1)} %basis_ref.5), custom_call_target="tpu_custom_call" | custom-call | tf_op jit(solution)/shard_map/basis/pallas_call | solution.py:244
  56.7 0.0 collective-permute-done.3
  56.7 2.7 %collective-permute-start.4 = (f32[64,128]{1,0:T(8,128)S(1)}, f32[64,128]{1,0:T(8,128)S(1)}, u32[]{:S(2)}, u32[]{:S(2)}) collective-permute-start(f32[64,128]{1,0:T(8,128)S(1)} %add.67.values_ref), channel_id=1, source_target_pairs={{0,16},{2,18},{4,20},{6,22},{8,24},{10,26},{12,28},{14,30},{16,0},... | collective-permute-start | bytes 98312 | tf_op jit(solution)/shard_map/ppermute | solution.py:21
  59.4 4.4 %basis.3 = (bf16[4,768,384]{2,1,0:T(8,128)(2,1)}, f32[64,128]{1,0:T(8,128)S(1)}) custom-call(f32[64,128]{1,0:T(8,128)S(1)} %add.67.values_ref, bf16[8,384,768]{2,1,0:T(8,128)(2,1)} %basis_ref.5), custom_call_target="tpu_custom_call" | custom-call | tf_op jit(solution)/shard_map/basis/pallas_call | solution.py:244
  63.8 0.0 collective-permute-done.4
  63.9 2.9 %collective-permute-start.11 = (bf16[64,128]{1,0:T(8,128)(2,1)S(1)}, bf16[64,128]{1,0:T(8,128)(2,1)S(1)}, u32[]{:S(2)}, u32[]{:S(2)}) collective-permute-start(bf16[64,128]{1,0:T(8,128)(2,1)S(1)} %get-tuple-element.13), channel_id=1, source_target_pairs={{0,224},{2,226},{4,228},{6,230},{8,232},{10,234},{12,236},{14,238}... | collective-permute-start | bytes 49160 | tf_op jit(solution)/shard_map/ppermute | solution.py:267
  66.7 2.4 %collective-permute-start.10 = (bf16[64,128]{1,0:T(8,128)(2,1)S(1)}, bf16[64,128]{1,0:T(8,128)(2,1)S(1)}, u32[]{:S(2)}, u32[]{:S(2)}) collective-permute-start(bf16[64,128]{1,0:T(8,128)(2,1)S(1)} %get-tuple-element.13), channel_id=1, source_target_pairs={{0,192},{2,194},{4,196},{6,198},{8,200},{10,202},{12,204},{14,206}... | collective-permute-start | bytes 49160 | tf_op jit(solution)/shard_map/ppermute | solution.py:267
  69.1 2.3 %collective-permute-start.9 = (bf16[64,128]{1,0:T(8,128)(2,1)S(1)}, bf16[64,128]{1,0:T(8,128)(2,1)S(1)}, u32[]{:S(2)}, u32[]{:S(2)}) collective-permute-start(bf16[64,128]{1,0:T(8,128)(2,1)S(1)} %get-tuple-element.13), channel_id=1, source_target_pairs={{0,160},{2,162},{4,164},{6,166},{8,168},{10,170},{12,172},{14,174}... | collective-permute-start | bytes 49160 | tf_op jit(solution)/shard_map/ppermute | solution.py:267
  71.5 3.1 %collective-permute-start.8 = (bf16[64,128]{1,0:T(8,128)(2,1)S(1)}, bf16[64,128]{1,0:T(8,128)(2,1)S(1)}, u32[]{:S(2)}, u32[]{:S(2)}) collective-permute-start(bf16[64,128]{1,0:T(8,128)(2,1)S(1)} %get-tuple-element.13), channel_id=1, source_target_pairs={{0,128},{2,130},{4,132},{6,134},{8,136},{10,138},{12,140},{14,142}... | collective-permute-start | bytes 49160 | tf_op jit(solution)/shard_map/ppermute | solution.py:267
  74.5 0.3 collective-permute-start.7
  74.8 0.5 collective-permute-done.11
  75.3 2.9 %collective-permute-start.6 = (bf16[64,128]{1,0:T(8,128)(2,1)S(1)}, bf16[64,128]{1,0:T(8,128)(2,1)S(1)}, u32[]{:S(2)}, u32[]{:S(2)}) collective-permute-start(bf16[64,128]{1,0:T(8,128)(2,1)S(1)} %get-tuple-element.13), channel_id=1, source_target_pairs={{0,64},{2,66},{4,68},{6,70},{8,72},{10,74},{12,76},{14,78},{16,80}... | collective-permute-start | bytes 49160 | tf_op jit(solution)/shard_map/ppermute | solution.py:267
  78.2 0.0 collective-permute-done.10
  78.2 2.5 %collective-permute-start.5 = (bf16[64,128]{1,0:T(8,128)(2,1)S(1)}, bf16[64,128]{1,0:T(8,128)(2,1)S(1)}, u32[]{:S(2)}, u32[]{:S(2)}) collective-permute-start(bf16[64,128]{1,0:T(8,128)(2,1)S(1)} %get-tuple-element.13), channel_id=1, source_target_pairs={{0,32},{2,34},{4,36},{6,38},{8,40},{10,42},{12,44},{14,46},{16,48}... | collective-permute-start | bytes 49160 | tf_op jit(solution)/shard_map/ppermute | solution.py:267
  80.6 0.0 collective-permute-done.9
  80.6 0.0 collective-permute-done.8
  80.6 0.7 collective-permute-done.7
  81.3 0.0 collective-permute-done.6
  81.3 1.8 %collective-permute-done.5 = bf16[64,128]{1,0:T(8,128)(2,1)S(1)} collective-permute-done((bf16[64,128]{1,0:T(8,128)(2,1)S(1)}, bf16[64,128]{1,0:T(8,128)(2,1)S(1)}, u32[]{:S(2)}, u32[]{:S(2)}) %collective-permute-start.5) | collective-permute-done | bytes 16416 | tf_op jit(solution)/shard_map/ppermute | solution.py:267
  83.1 0.0 all-to-all-done.received_ref
  83.1 9.3 %panel.1 = bf16[1,8,1536,128]{3,2,1,0:T(8,128)(2,1)} custom-call(s32[8,128]{1,0:T(8,128)S(1)} %bitcast.49, bf16[128,48,128]{2,1,0:T(8,128)(2,1)S(1)} %all-to-all-done.received_ref, bf16[4,768,384]{2,1,0:T(8,128)(2,1)} %get-tuple-element.9.first_ref, bf16[4,768,384]{2,1,0:T(8,128)(2,1)} %get-tuple-element.11.last_ref, f32[64,128]{1,0:T(8,128)S(1)} %convert_add_fusion.values_ref), custom_call_target="tpu_custom_call" | custom-call | tf_op jit(solution)/shard_map/panel/pallas_call | solution.py:268
  (10 shorter events, 0.1 us)
Async XLA Ops:
  0.0 18.5 %copy-start = (s32[128,8]{0,1:T(8,128)S(1)}, s32[128,8]{0,1:T(8,128)}, u32[]{:S(2)}) copy-start(s32[128,8]{0,1:T(8,128)} %param.7) | copy-start | bytes 12292
  0.0 18.7 %copy-start.1 = (bf16[1,64,2,3,1536]{4,2,3,1,0:T(2,128)(2,1)S(1)}, bf16[1,64,2,3,1536]{4,2,3,1,0:T(2,128)(2,1)}, u32[]{:S(2)}) copy-start(bf16[1,64,2,3,1536]{4,2,3,1,0:T(2,128)(2,1)} %param.5) | copy-start | bytes 3538948
  1.9 27.9 %all-to-all-start.1 = ((bf16[128,2,128]{2,1,0:T(2,128)(2,1)}), bf16[128,2,128]{2,1,0:T(2,128)(2,1)S(1)}, u32[]{:S(2)}, u32[]{:S(2)}) async-start(bf16[128,2,128]{2,1,0:T(2,128)(2,1)} %columns.1), calls=%async_computation.1 | async-start | bytes 131072 | tf_op jit(solution)/shard_map/all_to_all | solution.py:206
  18.7 1.7 %copy-start.3 = (bf16[768,2,768,1,1]{2,0,4,3,1:T(8,128)(2,1)S(1)}, bf16[768,2,768,1,1]{2,0,4,3,1:T(8,128)(2,1)}, u32[]{:S(2)}) copy-start(bf16[768,2,768,1,1]{2,0,4,3,1:T(8,128)(2,1)} %constant.38) | copy-start | bytes 7077892
  25.7 13.9 %copy-start.2 = (s32[2,64]{1,0:T(2,128)S(1)}, s32[2,64]{1,0:T(2,128)}, u32[]{:S(2)}) copy-start(s32[2,64]{1,0:T(2,128)} %modes_ref.1) | copy-start | bytes 1540
  29.8 53.3 %all-to-all-start = ((bf16[128,48,128]{2,1,0:T(8,128)(2,1)}), bf16[128,48,128]{2,1,0:T(8,128)(2,1)S(1)}, u32[]{:S(2)}, u32[]{:S(2)}) async-start(bf16[128,48,128]{2,1,0:T(8,128)(2,1)} %fusion.3), calls=%async_computation | async-start | bytes 3145728 | tf_op jit(solution)/shard_map/all_to_all | solution.py:232
  40.7 3.6 %collective-permute-start.1 = (f32[64,128]{1,0:T(8,128)S(1)}, f32[64,128]{1,0:T(8,128)S(1)}, u32[]{:S(2)}, u32[]{:S(2)}) collective-permute-start(f32[64,128]{1,0:T(8,128)S(1)} %multiply_reduce_fusion), channel_id=1, source_target_pairs={{0,3},{1,2},{2,1},{3,0},{4,7},{5,6},{6,5},{7,4},{8,11},{9,10},{10,... | collective-permute-start | bytes 98312 | tf_op jit(solution)/shard_map/ppermute | solution.py:33
  40.8 3.5 %collective-permute-start = (f32[64,128]{1,0:T(8,128)S(1)}, f32[64,128]{1,0:T(8,128)S(1)}, u32[]{:S(2)}, u32[]{:S(2)}) collective-permute-start(f32[64,128]{1,0:T(8,128)S(1)} %multiply_reduce_fusion), channel_id=1, source_target_pairs={{0,1},{1,0},{2,3},{3,2},{4,5},{5,4},{6,7},{7,6},{8,9},{9,8},{10,11... | collective-permute-start | bytes 98312 | tf_op jit(solution)/shard_map/ppermute | solution.py:33
  44.3 6.1 %collective-permute-start.2 = (f32[64,128]{1,0:T(8,128)S(1)}, f32[64,128]{1,0:T(8,128)S(1)}, u32[]{:S(2)}, u32[]{:S(2)}) collective-permute-start(f32[64,128]{1,0:T(8,128)S(1)} %add.65), channel_id=1, source_target_pairs={{0,4},{2,6},{4,0},{6,2},{8,12},{10,14},{12,8},{14,10},{16,20},{18,... | collective-permute-start | bytes 98312 | tf_op jit(solution)/shard_map/ppermute | solution.py:21
  50.4 6.3 %collective-permute-start.3 = (f32[64,128]{1,0:T(8,128)S(1)}, f32[64,128]{1,0:T(8,128)S(1)}, u32[]{:S(2)}, u32[]{:S(2)}) collective-permute-start(f32[64,128]{1,0:T(8,128)S(1)} %add.66.values_ref), channel_id=1, source_target_pairs={{0,8},{2,10},{4,12},{6,14},{8,0},{10,2},{12,4},{14,6},{16,24},{18,... | collective-permute-start | bytes 98312 | tf_op jit(solution)/shard_map/ppermute | solution.py:21
  56.7 7.1 %collective-permute-start.4 = (f32[64,128]{1,0:T(8,128)S(1)}, f32[64,128]{1,0:T(8,128)S(1)}, u32[]{:S(2)}, u32[]{:S(2)}) collective-permute-start(f32[64,128]{1,0:T(8,128)S(1)} %add.67.values_ref), channel_id=1, source_target_pairs={{0,16},{2,18},{4,20},{6,22},{8,24},{10,26},{12,28},{14,30},{16,0},... | collective-permute-start | bytes 98312 | tf_op jit(solution)/shard_map/ppermute | solution.py:21
  63.9 11.4 %collective-permute-start.11 = (bf16[64,128]{1,0:T(8,128)(2,1)S(1)}, bf16[64,128]{1,0:T(8,128)(2,1)S(1)}, u32[]{:S(2)}, u32[]{:S(2)}) collective-permute-start(bf16[64,128]{1,0:T(8,128)(2,1)S(1)} %get-tuple-element.13), channel_id=1, source_target_pairs={{0,224},{2,226},{4,228},{6,230},{8,232},{10,234},{12,236},{14,238}... | collective-permute-start | bytes 49160 | tf_op jit(solution)/shard_map/ppermute | solution.py:267
  66.7 11.4 %collective-permute-start.10 = (bf16[64,128]{1,0:T(8,128)(2,1)S(1)}, bf16[64,128]{1,0:T(8,128)(2,1)S(1)}, u32[]{:S(2)}, u32[]{:S(2)}) collective-permute-start(bf16[64,128]{1,0:T(8,128)(2,1)S(1)} %get-tuple-element.13), channel_id=1, source_target_pairs={{0,192},{2,194},{4,196},{6,198},{8,200},{10,202},{12,204},{14,206}... | collective-permute-start | bytes 49160 | tf_op jit(solution)/shard_map/ppermute | solution.py:267
  69.1 11.5 %collective-permute-start.9 = (bf16[64,128]{1,0:T(8,128)(2,1)S(1)}, bf16[64,128]{1,0:T(8,128)(2,1)S(1)}, u32[]{:S(2)}, u32[]{:S(2)}) collective-permute-start(bf16[64,128]{1,0:T(8,128)(2,1)S(1)} %get-tuple-element.13), channel_id=1, source_target_pairs={{0,160},{2,162},{4,164},{6,166},{8,168},{10,170},{12,172},{14,174}... | collective-permute-start | bytes 49160 | tf_op jit(solution)/shard_map/ppermute | solution.py:267
  71.5 9.2 %collective-permute-start.8 = (bf16[64,128]{1,0:T(8,128)(2,1)S(1)}, bf16[64,128]{1,0:T(8,128)(2,1)S(1)}, u32[]{:S(2)}, u32[]{:S(2)}) collective-permute-start(bf16[64,128]{1,0:T(8,128)(2,1)S(1)} %get-tuple-element.13), channel_id=1, source_target_pairs={{0,128},{2,130},{4,132},{6,134},{8,136},{10,138},{12,140},{14,142}... | collective-permute-start | bytes 49160 | tf_op jit(solution)/shard_map/ppermute | solution.py:267
  74.5 6.8 %collective-permute-start.7 = (bf16[64,128]{1,0:T(8,128)(2,1)S(1)}, bf16[64,128]{1,0:T(8,128)(2,1)S(1)}, u32[]{:S(2)}, u32[]{:S(2)}) collective-permute-start(bf16[64,128]{1,0:T(8,128)(2,1)S(1)} %get-tuple-element.13), channel_id=1, source_target_pairs={{0,96},{2,98},{4,100},{6,102},{8,104},{10,106},{12,108},{14,110},{... | collective-permute-start | bytes 49160 | tf_op jit(solution)/shard_map/ppermute | solution.py:267
  75.3 6.0 %collective-permute-start.6 = (bf16[64,128]{1,0:T(8,128)(2,1)S(1)}, bf16[64,128]{1,0:T(8,128)(2,1)S(1)}, u32[]{:S(2)}, u32[]{:S(2)}) collective-permute-start(bf16[64,128]{1,0:T(8,128)(2,1)S(1)} %get-tuple-element.13), channel_id=1, source_target_pairs={{0,64},{2,66},{4,68},{6,70},{8,72},{10,74},{12,76},{14,78},{16,80}... | collective-permute-start | bytes 49160 | tf_op jit(solution)/shard_map/ppermute | solution.py:267
  78.2 5.0 %collective-permute-start.5 = (bf16[64,128]{1,0:T(8,128)(2,1)S(1)}, bf16[64,128]{1,0:T(8,128)(2,1)S(1)}, u32[]{:S(2)}, u32[]{:S(2)}) collective-permute-start(bf16[64,128]{1,0:T(8,128)(2,1)S(1)} %get-tuple-element.13), channel_id=1, source_target_pairs={{0,32},{2,34},{4,36},{6,38},{8,40},{10,42},{12,44},{14,46},{16,48}... | collective-permute-start | bytes 49160 | tf_op jit(solution)/shard_map/ppermute | solution.py:267

commit v6 on v5

--- a/solution.py
+++ b/solution.py
@@ -136,10 +136,10 @@
     scale,
 ):
     group = lax.axis_index("lat")
-    slots, degrees, pairs = held_ref.shape
+    slots, degrees, _ = held_ref.shape
     half = slots // 2
-    sources, _, wide = received_ref.shape
-    share = pairs // sources
+    wide = received_ref.shape[2]
+    parts = received_ref.shape[0] // slots
     copies = []
     for s in range(slots):
         source = first_ref.at[s] if s < half else last_ref.at[s - half]
@@ -151,17 +151,18 @@
     ]
     centered = centered_columns(values_ref[...])
     degree = lax.broadcasted_iota(jnp.int32, (degrees, 1), 0)
-    for s in range(slots):
+
+    def of_both_parities(s):
+        rows = [received_ref[k * slots + s] for k in range(parts)]
         sides = [
-            jnp.concatenate(
-                [received_ref[:, (parity * share + j) * slots + s, :] for j in range(share)], axis=0
-            )
-            for parity in range(2)
+            jnp.concatenate(rows[: parts // 2], axis=0),
+            jnp.concatenate(rows[parts // 2 :], axis=0),
         ]
-        copies[s].wait()
-        both = jnp.dot(
+        return jnp.dot(
             held_ref[s], jnp.concatenate(sides, axis=1), preferred_element_type=jnp.float32
         )
+
+    def finish(s, both):
         order = orders_ref[s, group]
         odd = ((degree - order) & 1) == 1
         keep = (degree >= order) & (order >= 0)
@@ -169,7 +170,18 @@
         coefficients = jnp.where(keep, chosen, 0.0).astype(jnp.bfloat16)
         products = jnp.dot(coefficients, centered, preferred_element_type=jnp.float32)
         rows_ref[s] = (products * scale).astype(jnp.bfloat16).reshape(rows_ref.shape[1:])
-        out_copies[s].start()
+
+    begun = []
+    for start in range(0, slots + 2, 2):
+        coming = range(start, min(start + 2, slots))
+        for s in coming:
+            copies[s].wait()
+        new = [(s, of_both_parities(s)) for s in coming]
+        for s, both in begun:
+            finish(s, both)
+        for s, _ in begun:
+            out_copies[s].start()
+        begun = new
     for copy in out_copies:
         copy.wait()
 
@@ -188,7 +200,7 @@
     mode_order, mode_degree = panel_modes[0], panel_modes[1]
     orders_by_slot = order_table.T
     in_hbm = pl.BlockSpec(memory_space=pltpu.HBM)
-    roomy = pltpu.CompilerParams(vmem_limit_bytes=24 << 20)
+    roomy = pltpu.CompilerParams(vmem_limit_bytes=32 << 20)
 
     columns = pl.pallas_call(
         column_kernel,
@@ -280,7 +292,7 @@
         name="panel",
     )(
         orders_by_slot,
-        pltpu.with_memory_space_constraint(received, pltpu.VMEM),
+        pltpu.with_memory_space_constraint(received.transpose(1, 0, 2), pltpu.VMEM),
         *halves,
         pltpu.with_memory_space_constraint(values, pltpu.VMEM),
     )

time: 94 us -> 91.8 us (0.977)
  Pallas kernels: 20 us -> 17.3 us
    pallas_call x1, Pallas kernels: 9.34 us -> 6.57 us  [local(): pl.pallas_call(functools.partial(panel_kernel, scale=1.0 / (snap_count -...]
  transfers between devices with their start and end apart: 14 -> 14, of which waited for: 6 -> 6; matrix products, arithmetic and copies ran while one was open for 7% -> 8% of each run, Pallas kernels for 9% -> 10%
where the time goes in v6:
time: 91.8 us; the launch traced here: 90.4 us
  starting transfers between devices  50.6 us (55%)
  Pallas kernels  17.3 us (19%)
  waiting for transfers between devices  13.4 us (15%)
  matrix products  5.38 us (6%)
  local copies, waits for them, and re-layouts  2.58 us (3%)
    all_to_all x1, starting transfers between devices, local(): lax.all_to_all(columns, 'lat', split_axis=0, concat_axis=0, tiled=True)  16.6 us
    ppermute x7, starting transfers between devices, local(): values = values + lax.ppermute(own, 'lat', route).astype(jnp.float32)  16.2 us
    all_to_all x1, starting transfers between devices, local(): lax.all_to_all(sent, 'lat', split_axis=0, concat_axis=0, tiled=True)  9.78 us
    pallas_call x2, Pallas kernels, local(): pl.pallas_call(functools.partial(basis_kernel, first=len(halves) * count,...  8.74 us
    ppermute x3, starting transfers between devices, from_far(): return lax.ppermute(block, 'lat', [(i, i ^ reach) for i in range(count)])  6.91 us
    pallas_call x1, Pallas kernels, local(): pl.pallas_call(functools.partial(panel_kernel, scale=1.0 / (snap_count -...  6.57 us
    all_to_all x1, waiting for transfers between devices, local(): lax.all_to_all(columns, 'lat', split_axis=0, concat_axis=0, tiled=True)  4.09 us
    ppermute x3, waiting for transfers between devices, from_far(): return lax.ppermute(block, 'lat', [(i, i ^ reach) for i in range(count)])  3.87 us
  transfers between devices with their start and end apart: 14, of which 6 were waited for; matrix products, arithmetic and copies ran while one was open for 8% of the time, Pallas kernels for 10%

profile of v6, /device:TPU:2, one launch (start us, length us, event | category | flops | bytes accessed | tf_op | source)
XLA Modules:
  0.0 90.4 jit_solution(14943605139401743506)
XLA Ops:
  0.0 0.0 copy-start
  0.0 0.0 copy-start.1
  0.0 1.9 %columns.1 = bf16[128,2,128]{2,1,0:T(2,128)(2,1)} custom-call(s32[8,128]{1,0:T(8,128)} %bitcast.52, s32[2,64]{1,0:T(2,128)} %modes_ref.1, bf16[8,384,768]{2,1,0:T(8,128)(2,1)} %basis_ref.5), custom_call_target="tpu_custom_call" | custom-call | tf_op jit(solution)/shard_map/columns/pallas_call | solution.py:205
  1.9 16.6 %all-to-all-start.1 = ((bf16[128,2,128]{2,1,0:T(2,128)(2,1)}), bf16[128,2,128]{2,1,0:T(2,128)(2,1)S(1)}, u32[]{:S(2)}, u32[]{:S(2)}) async-start(bf16[128,2,128]{2,1,0:T(2,128)(2,1)} %columns.1), calls=%async_computation.1 | async-start | bytes 131072 | tf_op jit(solution)/shard_map/all_to_all | solution.py:218
  18.6 0.0 copy-done
  18.6 0.1 copy.15
  18.7 0.1 eq.40
  18.8 0.0 copy-done.1
  18.8 0.0 copy-start.3
  18.8 0.1 copy.26
  19.0 1.5 %copy-done.3 = bf16[768,2,768,1,1]{2,0,4,3,1:T(8,128)(2,1)S(1)} copy-done((bf16[768,2,768,1,1]{2,0,4,3,1:T(8,128)(2,1)S(1)}, bf16[768,2,768,1,1]{2,0,4,3,1:T(8,128)(2,1)}, u32[]{:S(2)}) %copy-start.3) | copy-done | bytes 2359320
  20.5 1.1 %fusion.4 = f32[2,768,64,2,3]{1,2,4,3,0:T(8,128)S(1)} fusion(bf16[768,2,768,1,1]{2,0,4,3,1:T(8,128)(2,1)S(1)} %copy-done.3, bf16[64,2,3,1536]{3,0,2,1:T(8,128)(2,1)S(1)} %bitcast.56), kind=kOutput, calls=%fused_computation.14 | convolution fusion | flops 905969664 | bytes 5308416 | tf_op jit(solution)/shard_map/thjn,nrm->hjrtm/dot_general | solution.py:223
  21.6 1.1 %multiply_bitcast_fusion = f32[2,3,2,64,768]{4,3,1,0,2:T(8,128)S(1)} fusion(f32[2,768,64,2,3]{1,2,4,3,0:T(8,128)S(1)} %fusion.4, bf16[768,2,768,1,1]{2,0,4,3,1:T(8,128)(2,1)S(1)} %copy-done.3, f32[768]{0:T(1024)S(1)} %fusion.9, bf16[64,2,3,1536]{3,0,2,1:T(8,128)(2,1)S(1)} %bitcast.57), kind=kOutput, calls=%fused_computation.2 | convolution fusion | flops 907739136 | bytes 7671808 | tf_op jit(solution)/shard_map/thjn,nrm->hjrtm/dot_general | solution.py:223
  22.7 0.2 add_convert_fusion
  22.9 0.1 pad_maximum_fusion
  23.0 0.1 copy.17
  23.1 2.7 %fusion.3 = bf16[128,48,128]{2,1,0:T(8,128)(2,1)} fusion(bf16[768,768]{1,0:T(8,128)(2,1)S(1)} %bitcast.54, s32[1024]{0:T(1024)S(1)} %eq.40), kind=kOutput, calls=%fused_computation.6 | convolution fusion | flops 1209532416 | bytes 2756608 | tf_op jit(solution)/shard_map/dot_general | solution.py:233
  25.8 0.0 copy-start.2
  25.8 4.1 %all-to-all-done.1 = bf16[128,2,128]{2,1,0:T(2,128)(2,1)S(1)} async-done(((bf16[128,2,128]{2,1,0:T(2,128)(2,1)}), bf16[128,2,128]{2,1,0:T(2,128)(2,1)S(1)}, u32[]{:S(2)}, u32[]{:S(2)}) %all-to-all-start.1) | async-done | bytes 65568 | tf_op jit(solution)/shard_map/all_to_all | solution.py:218
  29.9 9.8 %all-to-all-start = ((bf16[128,48,128]{2,1,0:T(8,128)(2,1)}), bf16[128,48,128]{2,1,0:T(8,128)(2,1)S(1)}, u32[]{:S(2)}, u32[]{:S(2)}) async-start(bf16[128,48,128]{2,1,0:T(8,128)(2,1)} %fusion.3), calls=%async_computation | async-start | bytes 3145728 | tf_op jit(solution)/shard_map/all_to_all | solution.py:244
  39.7 0.0 copy-done.2
  39.7 0.5 convolution_convert_fusion
  40.3 0.1 convert_reduce_fusion
  40.4 0.1 reshape.54
  40.5 0.1 copy.20
  40.6 0.2 multiply_reduce_fusion
  40.8 0.1 collective-permute-start.1
  40.9 1.0 %collective-permute-start = (f32[64,128]{1,0:T(8,128)S(1)}, f32[64,128]{1,0:T(8,128)S(1)}, u32[]{:S(2)}, u32[]{:S(2)}) collective-permute-start(f32[64,128]{1,0:T(8,128)S(1)} %multiply_reduce_fusion), channel_id=1, source_target_pairs={{0,1},{1,0},{2,3},{3,2},{4,5},{5,4},{6,7},{7,6},{8,9},{9,8},{10,11... | collective-permute-start | bytes 98312 | tf_op jit(solution)/shard_map/ppermute | solution.py:33
  41.9 2.5 %collective-permute-done.1 = f32[64,128]{1,0:T(8,128)S(1)} collective-permute-done((f32[64,128]{1,0:T(8,128)S(1)}, f32[64,128]{1,0:T(8,128)S(1)}, u32[]{:S(2)}, u32[]{:S(2)}) %collective-permute-start.1) | collective-permute-done | bytes 32800 | tf_op jit(solution)/shard_map/ppermute | solution.py:33
  44.4 0.0 collective-permute-done
  44.4 2.2 %collective-permute-start.2 = (f32[64,128]{1,0:T(8,128)S(1)}, f32[64,128]{1,0:T(8,128)S(1)}, u32[]{:S(2)}, u32[]{:S(2)}) collective-permute-start(f32[64,128]{1,0:T(8,128)S(1)} %add.65), channel_id=1, source_target_pairs={{0,4},{2,6},{4,0},{6,2},{8,12},{10,14},{12,8},{14,10},{16,20},{18,... | collective-permute-start | bytes 98312 | tf_op jit(solution)/shard_map/ppermute | solution.py:21
  46.6 3.9 %collective-permute-done.2 = f32[64,128]{1,0:T(8,128)S(1)} collective-permute-done((f32[64,128]{1,0:T(8,128)S(1)}, f32[64,128]{1,0:T(8,128)S(1)}, u32[]{:S(2)}, u32[]{:S(2)}) %collective-permute-start.2) | collective-permute-done | bytes 32800 | tf_op jit(solution)/shard_map/ppermute | solution.py:21
  50.5 1.9 %collective-permute-start.3 = (f32[64,128]{1,0:T(8,128)S(1)}, f32[64,128]{1,0:T(8,128)S(1)}, u32[]{:S(2)}, u32[]{:S(2)}) collective-permute-start(f32[64,128]{1,0:T(8,128)S(1)} %add.66.values_ref), channel_id=1, source_target_pairs={{0,8},{2,10},{4,12},{6,14},{8,0},{10,2},{12,4},{14,6},{16,24},{18,... | collective-permute-start | bytes 98312 | tf_op jit(solution)/shard_map/ppermute | solution.py:21
  52.4 4.4 %basis.2 = (bf16[4,768,384]{2,1,0:T(8,128)(2,1)}, f32[64,128]{1,0:T(8,128)S(1)}) custom-call(f32[64,128]{1,0:T(8,128)S(1)} %add.66.values_ref, bf16[8,384,768]{2,1,0:T(8,128)(2,1)} %basis_ref.5), custom_call_target="tpu_custom_call" | custom-call | tf_op jit(solution)/shard_map/basis/pallas_call | solution.py:256
  56.8 0.0 collective-permute-done.3
  56.8 2.8 %collective-permute-start.4 = (f32[64,128]{1,0:T(8,128)S(1)}, f32[64,128]{1,0:T(8,128)S(1)}, u32[]{:S(2)}, u32[]{:S(2)}) collective-permute-start(f32[64,128]{1,0:T(8,128)S(1)} %add.67.values_ref), channel_id=1, source_target_pairs={{0,16},{2,18},{4,20},{6,22},{8,24},{10,26},{12,28},{14,30},{16,0},... | collective-permute-start | bytes 98312 | tf_op jit(solution)/shard_map/ppermute | solution.py:21
  59.6 4.4 %basis.3 = (bf16[4,768,384]{2,1,0:T(8,128)(2,1)}, f32[64,128]{1,0:T(8,128)S(1)}) custom-call(f32[64,128]{1,0:T(8,128)S(1)} %add.67.values_ref, bf16[8,384,768]{2,1,0:T(8,128)(2,1)} %basis_ref.5), custom_call_target="tpu_custom_call" | custom-call | tf_op jit(solution)/shard_map/basis/pallas_call | solution.py:256
  64.0 0.0 collective-permute-done.4
  64.0 2.8 %collective-permute-start.11 = (bf16[64,128]{1,0:T(8,128)(2,1)S(1)}, bf16[64,128]{1,0:T(8,128)(2,1)S(1)}, u32[]{:S(2)}, u32[]{:S(2)}) collective-permute-start(bf16[64,128]{1,0:T(8,128)(2,1)S(1)} %get-tuple-element.13), channel_id=1, source_target_pairs={{0,224},{2,226},{4,228},{6,230},{8,232},{10,234},{12,236},{14,238}... | collective-permute-start | bytes 49160 | tf_op jit(solution)/shard_map/ppermute | solution.py:279
  66.8 2.4 %collective-permute-start.10 = (bf16[64,128]{1,0:T(8,128)(2,1)S(1)}, bf16[64,128]{1,0:T(8,128)(2,1)S(1)}, u32[]{:S(2)}, u32[]{:S(2)}) collective-permute-start(bf16[64,128]{1,0:T(8,128)(2,1)S(1)} %get-tuple-element.13), channel_id=1, source_target_pairs={{0,192},{2,194},{4,196},{6,198},{8,200},{10,202},{12,204},{14,206}... | collective-permute-start | bytes 49160 | tf_op jit(solution)/shard_map/ppermute | solution.py:279
  69.2 2.4 %collective-permute-start.9 = (bf16[64,128]{1,0:T(8,128)(2,1)S(1)}, bf16[64,128]{1,0:T(8,128)(2,1)S(1)}, u32[]{:S(2)}, u32[]{:S(2)}) collective-permute-start(bf16[64,128]{1,0:T(8,128)(2,1)S(1)} %get-tuple-element.13), channel_id=1, source_target_pairs={{0,160},{2,162},{4,164},{6,166},{8,168},{10,170},{12,172},{14,174}... | collective-permute-start | bytes 49160 | tf_op jit(solution)/shard_map/ppermute | solution.py:279
  71.6 3.0 %collective-permute-start.8 = (bf16[64,128]{1,0:T(8,128)(2,1)S(1)}, bf16[64,128]{1,0:T(8,128)(2,1)S(1)}, u32[]{:S(2)}, u32[]{:S(2)}) collective-permute-start(bf16[64,128]{1,0:T(8,128)(2,1)S(1)} %get-tuple-element.13), channel_id=1, source_target_pairs={{0,128},{2,130},{4,132},{6,134},{8,136},{10,138},{12,140},{14,142}... | collective-permute-start | bytes 49160 | tf_op jit(solution)/shard_map/ppermute | solution.py:279
  74.6 0.3 collective-permute-start.7
  74.9 0.5 collective-permute-done.11
  75.4 2.8 %collective-permute-start.6 = (bf16[64,128]{1,0:T(8,128)(2,1)S(1)}, bf16[64,128]{1,0:T(8,128)(2,1)S(1)}, u32[]{:S(2)}, u32[]{:S(2)}) collective-permute-start(bf16[64,128]{1,0:T(8,128)(2,1)S(1)} %get-tuple-element.13), channel_id=1, source_target_pairs={{0,64},{2,66},{4,68},{6,70},{8,72},{10,74},{12,76},{14,78},{16,80}... | collective-permute-start | bytes 49160 | tf_op jit(solution)/shard_map/ppermute | solution.py:279
  78.2 0.0 collective-permute-done.10
  78.2 2.5 %collective-permute-start.5 = (bf16[64,128]{1,0:T(8,128)(2,1)S(1)}, bf16[64,128]{1,0:T(8,128)(2,1)S(1)}, u32[]{:S(2)}, u32[]{:S(2)}) collective-permute-start(bf16[64,128]{1,0:T(8,128)(2,1)S(1)} %get-tuple-element.13), channel_id=1, source_target_pairs={{0,32},{2,34},{4,36},{6,38},{8,40},{10,42},{12,44},{14,46},{16,48}... | collective-permute-start | bytes 49160 | tf_op jit(solution)/shard_map/ppermute | solution.py:279
  80.7 0.0 collective-permute-done.9
  80.7 0.0 collective-permute-done.8
  80.7 0.7 collective-permute-done.7
  81.4 0.0 collective-permute-done.6
  81.4 1.8 %collective-permute-done.5 = bf16[64,128]{1,0:T(8,128)(2,1)S(1)} collective-permute-done((bf16[64,128]{1,0:T(8,128)(2,1)S(1)}, bf16[64,128]{1,0:T(8,128)(2,1)S(1)}, u32[]{:S(2)}, u32[]{:S(2)}) %collective-permute-start.5) | collective-permute-done | bytes 16416 | tf_op jit(solution)/shard_map/ppermute | solution.py:279
  83.2 0.0 all-to-all-done
  83.2 0.4 copy.25
  83.6 6.6 %panel.1 = bf16[1,8,1536,128]{3,2,1,0:T(8,128)(2,1)} custom-call(s32[8,128]{1,0:T(8,128)S(1)} %bitcast.53, bf16[48,128,128]{2,1,0:T(8,128)(2,1)S(1)} %bitcast.51, bf16[4,768,384]{2,1,0:T(8,128)(2,1)} %get-tuple-element.9.first_ref, bf16[4,768,384]{2,1,0:T(8,128)(2,1)} %get-tuple-element.11.last_ref, f32[64,128]{1,0:T(8,128)S(1)} %convert_add_fusion.values_ref), custom_call_target="tpu_custom_call" | custom-call | tf_op jit(solution)/shard_map/panel/pallas_call | solution.py:280
  (10 shorter events, 0.1 us)
Async XLA Ops:
  0.0 18.6 %copy-start = (s32[128,8]{0,1:T(8,128)S(1)}, s32[128,8]{0,1:T(8,128)}, u32[]{:S(2)}) copy-start(s32[128,8]{0,1:T(8,128)} %param.7) | copy-start | bytes 12292
  0.0 18.8 %copy-start.1 = (bf16[1,64,2,3,1536]{4,2,3,1,0:T(2,128)(2,1)S(1)}, bf16[1,64,2,3,1536]{4,2,3,1,0:T(2,128)(2,1)}, u32[]{:S(2)}) copy-start(bf16[1,64,2,3,1536]{4,2,3,1,0:T(2,128)(2,1)} %param.5) | copy-start | bytes 3538948
  1.9 27.9 %all-to-all-start.1 = ((bf16[128,2,128]{2,1,0:T(2,128)(2,1)}), bf16[128,2,128]{2,1,0:T(2,128)(2,1)S(1)}, u32[]{:S(2)}, u32[]{:S(2)}) async-start(bf16[128,2,128]{2,1,0:T(2,128)(2,1)} %columns.1), calls=%async_computation.1 | async-start | bytes 131072 | tf_op jit(solution)/shard_map/all_to_all | solution.py:218
  18.8 1.7 %copy-start.3 = (bf16[768,2,768,1,1]{2,0,4,3,1:T(8,128)(2,1)S(1)}, bf16[768,2,768,1,1]{2,0,4,3,1:T(8,128)(2,1)}, u32[]{:S(2)}) copy-start(bf16[768,2,768,1,1]{2,0,4,3,1:T(8,128)(2,1)} %constant.38) | copy-start | bytes 7077892
  25.8 13.9 %copy-start.2 = (s32[2,64]{1,0:T(2,128)S(1)}, s32[2,64]{1,0:T(2,128)}, u32[]{:S(2)}) copy-start(s32[2,64]{1,0:T(2,128)} %modes_ref.1) | copy-start | bytes 1540
  29.9 53.3 %all-to-all-start = ((bf16[128,48,128]{2,1,0:T(8,128)(2,1)}), bf16[128,48,128]{2,1,0:T(8,128)(2,1)S(1)}, u32[]{:S(2)}, u32[]{:S(2)}) async-start(bf16[128,48,128]{2,1,0:T(8,128)(2,1)} %fusion.3), calls=%async_computation | async-start | bytes 3145728 | tf_op jit(solution)/shard_map/all_to_all | solution.py:244
  40.8 3.6 %collective-permute-start.1 = (f32[64,128]{1,0:T(8,128)S(1)}, f32[64,128]{1,0:T(8,128)S(1)}, u32[]{:S(2)}, u32[]{:S(2)}) collective-permute-start(f32[64,128]{1,0:T(8,128)S(1)} %multiply_reduce_fusion), channel_id=1, source_target_pairs={{0,3},{1,2},{2,1},{3,0},{4,7},{5,6},{6,5},{7,4},{8,11},{9,10},{10,... | collective-permute-start | bytes 98312 | tf_op jit(solution)/shard_map/ppermute | solution.py:33
  40.9 3.5 %collective-permute-start = (f32[64,128]{1,0:T(8,128)S(1)}, f32[64,128]{1,0:T(8,128)S(1)}, u32[]{:S(2)}, u32[]{:S(2)}) collective-permute-start(f32[64,128]{1,0:T(8,128)S(1)} %multiply_reduce_fusion), channel_id=1, source_target_pairs={{0,1},{1,0},{2,3},{3,2},{4,5},{5,4},{6,7},{7,6},{8,9},{9,8},{10,11... | collective-permute-start | bytes 98312 | tf_op jit(solution)/shard_map/ppermute | solution.py:33
  44.4 6.1 %collective-permute-start.2 = (f32[64,128]{1,0:T(8,128)S(1)}, f32[64,128]{1,0:T(8,128)S(1)}, u32[]{:S(2)}, u32[]{:S(2)}) collective-permute-start(f32[64,128]{1,0:T(8,128)S(1)} %add.65), channel_id=1, source_target_pairs={{0,4},{2,6},{4,0},{6,2},{8,12},{10,14},{12,8},{14,10},{16,20},{18,... | collective-permute-start | bytes 98312 | tf_op jit(solution)/shard_map/ppermute | solution.py:21
  50.5 6.3 %collective-permute-start.3 = (f32[64,128]{1,0:T(8,128)S(1)}, f32[64,128]{1,0:T(8,128)S(1)}, u32[]{:S(2)}, u32[]{:S(2)}) collective-permute-start(f32[64,128]{1,0:T(8,128)S(1)} %add.66.values_ref), channel_id=1, source_target_pairs={{0,8},{2,10},{4,12},{6,14},{8,0},{10,2},{12,4},{14,6},{16,24},{18,... | collective-permute-start | bytes 98312 | tf_op jit(solution)/shard_map/ppermute | solution.py:21
  56.8 7.2 %collective-permute-start.4 = (f32[64,128]{1,0:T(8,128)S(1)}, f32[64,128]{1,0:T(8,128)S(1)}, u32[]{:S(2)}, u32[]{:S(2)}) collective-permute-start(f32[64,128]{1,0:T(8,128)S(1)} %add.67.values_ref), channel_id=1, source_target_pairs={{0,16},{2,18},{4,20},{6,22},{8,24},{10,26},{12,28},{14,30},{16,0},... | collective-permute-start | bytes 98312 | tf_op jit(solution)/shard_map/ppermute | solution.py:21
  64.0 11.4 %collective-permute-start.11 = (bf16[64,128]{1,0:T(8,128)(2,1)S(1)}, bf16[64,128]{1,0:T(8,128)(2,1)S(1)}, u32[]{:S(2)}, u32[]{:S(2)}) collective-permute-start(bf16[64,128]{1,0:T(8,128)(2,1)S(1)} %get-tuple-element.13), channel_id=1, source_target_pairs={{0,224},{2,226},{4,228},{6,230},{8,232},{10,234},{12,236},{14,238}... | collective-permute-start | bytes 49160 | tf_op jit(solution)/shard_map/ppermute | solution.py:279
  66.8 11.4 %collective-permute-start.10 = (bf16[64,128]{1,0:T(8,128)(2,1)S(1)}, bf16[64,128]{1,0:T(8,128)(2,1)S(1)}, u32[]{:S(2)}, u32[]{:S(2)}) collective-permute-start(bf16[64,128]{1,0:T(8,128)(2,1)S(1)} %get-tuple-element.13), channel_id=1, source_target_pairs={{0,192},{2,194},{4,196},{6,198},{8,200},{10,202},{12,204},{14,206}... | collective-permute-start | bytes 49160 | tf_op jit(solution)/shard_map/ppermute | solution.py:279
  69.2 11.5 %collective-permute-start.9 = (bf16[64,128]{1,0:T(8,128)(2,1)S(1)}, bf16[64,128]{1,0:T(8,128)(2,1)S(1)}, u32[]{:S(2)}, u32[]{:S(2)}) collective-permute-start(bf16[64,128]{1,0:T(8,128)(2,1)S(1)} %get-tuple-element.13), channel_id=1, source_target_pairs={{0,160},{2,162},{4,164},{6,166},{8,168},{10,170},{12,172},{14,174}... | collective-permute-start | bytes 49160 | tf_op jit(solution)/shard_map/ppermute | solution.py:279
  71.6 9.1 %collective-permute-start.8 = (bf16[64,128]{1,0:T(8,128)(2,1)S(1)}, bf16[64,128]{1,0:T(8,128)(2,1)S(1)}, u32[]{:S(2)}, u32[]{:S(2)}) collective-permute-start(bf16[64,128]{1,0:T(8,128)(2,1)S(1)} %get-tuple-element.13), channel_id=1, source_target_pairs={{0,128},{2,130},{4,132},{6,134},{8,136},{10,138},{12,140},{14,142}... | collective-permute-start | bytes 49160 | tf_op jit(solution)/shard_map/ppermute | solution.py:279
  74.6 6.8 %collective-permute-start.7 = (bf16[64,128]{1,0:T(8,128)(2,1)S(1)}, bf16[64,128]{1,0:T(8,128)(2,1)S(1)}, u32[]{:S(2)}, u32[]{:S(2)}) collective-permute-start(bf16[64,128]{1,0:T(8,128)(2,1)S(1)} %get-tuple-element.13), channel_id=1, source_target_pairs={{0,96},{2,98},{4,100},{6,102},{8,104},{10,106},{12,108},{14,110},{... | collective-permute-start | bytes 49160 | tf_op jit(solution)/shard_map/ppermute | solution.py:279
  75.4 6.0 %collective-permute-start.6 = (bf16[64,128]{1,0:T(8,128)(2,1)S(1)}, bf16[64,128]{1,0:T(8,128)(2,1)S(1)}, u32[]{:S(2)}, u32[]{:S(2)}) collective-permute-start(bf16[64,128]{1,0:T(8,128)(2,1)S(1)} %get-tuple-element.13), channel_id=1, source_target_pairs={{0,64},{2,66},{4,68},{6,70},{8,72},{10,74},{12,76},{14,78},{16,80}... | collective-permute-start | bytes 49160 | tf_op jit(solution)/shard_map/ppermute | solution.py:279
  78.2 5.0 %collective-permute-start.5 = (bf16[64,128]{1,0:T(8,128)(2,1)S(1)}, bf16[64,128]{1,0:T(8,128)(2,1)S(1)}, u32[]{:S(2)}, u32[]{:S(2)}) collective-permute-start(bf16[64,128]{1,0:T(8,128)(2,1)S(1)} %get-tuple-element.13), channel_id=1, source_target_pairs={{0,32},{2,34},{4,36},{6,38},{8,40},{10,42},{12,44},{14,46},{16,48}... | collective-permute-start | bytes 49160 | tf_op jit(solution)/shard_map/ppermute | solution.py:279

commit v7 on v6

--- a/solution.py
+++ b/solution.py
@@ -124,26 +124,19 @@
 def panel_kernel(
     orders_ref,
     received_ref,
-    first_ref,
-    last_ref,
     values_ref,
-    out_ref,
-    held_ref,
-    rows_ref,
-    sems,
-    out_sems,
-    *,
+    *refs,
     scale,
 ):
+    *basis_refs, out_ref, held_ref, rows_ref, sems, out_sems = refs
     group = lax.axis_index("lat")
     slots, degrees, _ = held_ref.shape
-    half = slots // 2
     wide = received_ref.shape[2]
     parts = received_ref.shape[0] // slots
+    sources = [ref.at[i] for ref in basis_refs for i in range(ref.shape[0])]
     copies = []
     for s in range(slots):
-        source = first_ref.at[s] if s < half else last_ref.at[s - half]
-        copies.append(pltpu.make_async_copy(source, held_ref.at[s], sems.at[s]))
+        copies.append(pltpu.make_async_copy(sources[s], held_ref.at[s], sems.at[s]))
         copies[s].start()
     out_copies = [
         pltpu.make_async_copy(rows_ref.at[s], out_ref.at[0, s], out_sems.at[s])
@@ -247,14 +240,10 @@
     mode_odd = ((mode_degree - mode_order) % 2 == 1)[:, None, None]
     mode_side = jnp.where(mode_odd, mode_parts[:, 1], mode_parts[:, 0]).astype(jnp.float32)
     values = swapped_pair_sum(jnp.sum(mode_side * columns.T[:, :, None], axis=1))
-    halves = []
-    for reach in (2, 4, 8):
-        if reach == 2:
-            values = stepped(values, reach)
-            continue
-        count = slot_count // 2
-        half, same = pl.pallas_call(
-            functools.partial(basis_kernel, first=len(halves) * count, sources=group_count),
+    pieces, first = [], 0
+    for reach, count in ((2, 3), (4, 2), (8, slot_count - 5)):
+        piece, same = pl.pallas_call(
+            functools.partial(basis_kernel, first=first, sources=group_count),
             in_specs=[in_vmem, in_hbm],
             out_specs=(in_hbm, in_vmem),
             out_shape=(
@@ -270,7 +259,8 @@
             compiler_params=roomy,
             name="basis",
         )(values, pltpu.with_memory_space_constraint(basis, pltpu.HBM))
-        halves.append(pltpu.with_memory_space_constraint(half, pltpu.HBM))
+        pieces.append(pltpu.with_memory_space_constraint(piece, pltpu.HBM))
+        first += count
         values = same + from_far(values, reach)
     plane = 16
     own = values.astype(jnp.bfloat16)
@@ -279,7 +269,7 @@
         values = values + lax.ppermute(own, "lat", route).astype(jnp.float32)
     return pl.pallas_call(
         functools.partial(panel_kernel, scale=1.0 / (snap_count - 1)),
-        in_specs=[in_smem, in_vmem, in_hbm, in_hbm, in_vmem],
+        in_specs=[in_smem, in_vmem, in_vmem] + [in_hbm] * len(pieces),
         out_specs=anywhere,
         out_shape=jax.ShapeDtypeStruct((1, slot_count, 2 * deg_count, 2 * mode_count), jnp.bfloat16),
         scratch_shapes=[
@@ -293,8 +283,8 @@
     )(
         orders_by_slot,
         pltpu.with_memory_space_constraint(received.transpose(1, 0, 2), pltpu.VMEM),
-        *halves,
         pltpu.with_memory_space_constraint(values, pltpu.VMEM),
+        *pieces,
     )
 
 

time: 91.8 us -> 90.3 us (0.984)
  waiting for transfers between devices: 13.4 us -> 10.5 us
  Pallas kernels: 17.3 us -> 19.1 us
    ppermute x3, waiting for transfers between devices: 3.87 us -> 0.13 us  [from_far(): return lax.ppermute(block, 'lat', [(i, i ^ reach) for i in range(count)])]
    pallas_call x2 -> x3, Pallas kernels: 8.74 us -> 10.6 us  [local(): pl.pallas_call(functools.partial(basis_kernel, first=first, sources=group...]
  transfers between devices with their start and end apart: 14 -> 14, of which waited for: 6 -> 6; matrix products, arithmetic and copies ran while one was open for 8% -> 8% of each run, Pallas kernels for 10% -> 12%
where the time goes in v7:
time: 90.3 us; the launch traced here: 89.7 us
  starting transfers between devices  51 us (56%)
  Pallas kernels  19.1 us (21%)
  waiting for transfers between devices  10.5 us (12%)
  matrix products  5.39 us (6%)
  local copies, waits for them, and re-layouts  2.58 us (3%)
    all_to_all x1, starting transfers between devices, local(): lax.all_to_all(columns, 'lat', split_axis=0, concat_axis=0, tiled=True)  16.9 us
    ppermute x7, starting transfers between devices, local(): values = values + lax.ppermute(own, 'lat', route).astype(jnp.float32)  15.9 us
    pallas_call x3, Pallas kernels, local(): pl.pallas_call(functools.partial(basis_kernel, first=first, sources=group...  10.6 us
    all_to_all x1, starting transfers between devices, local(): lax.all_to_all(sent, 'lat', split_axis=0, concat_axis=0, tiled=True)  9.79 us
    ppermute x3, starting transfers between devices, from_far(): return lax.ppermute(block, 'lat', [(i, i ^ reach) for i in range(count)])  7.22 us
    pallas_call x1, Pallas kernels, local(): pl.pallas_call(functools.partial(panel_kernel, scale=1.0 / (snap_count -...  6.58 us
    all_to_all x1, waiting for transfers between devices, local(): lax.all_to_all(columns, 'lat', split_axis=0, concat_axis=0, tiled=True)  4.09 us
    ppermute x7, waiting for transfers between devices, local(): values = values + lax.ppermute(own, 'lat', route).astype(jnp.float32)  3.77 us
  transfers between devices with their start and end apart: 14, of which 6 were waited for; matrix products, arithmetic and copies ran while one was open for 8% of the time, Pallas kernels for 12%

profile of v7, /device:TPU:2, one launch (start us, length us, event | category | flops | bytes accessed | tf_op | source)
XLA Modules:
  0.0 89.7 jit_solution(5682494727355844788)
XLA Ops:
  0.0 0.0 copy-start
  0.0 0.0 copy-start.1
  0.0 1.9 %columns.1 = bf16[128,2,128]{2,1,0:T(2,128)(2,1)} custom-call(s32[8,128]{1,0:T(8,128)} %bitcast.52, s32[2,64]{1,0:T(2,128)} %modes_ref.1, bf16[8,384,768]{2,1,0:T(8,128)(2,1)} %basis_ref.7), custom_call_target="tpu_custom_call" | custom-call | tf_op jit(solution)/shard_map/columns/pallas_call | solution.py:198
  1.9 16.9 %all-to-all-start.1 = ((bf16[128,2,128]{2,1,0:T(2,128)(2,1)}), bf16[128,2,128]{2,1,0:T(2,128)(2,1)S(1)}, u32[]{:S(2)}, u32[]{:S(2)}) async-start(bf16[128,2,128]{2,1,0:T(2,128)(2,1)} %columns.1), calls=%async_computation.1 | async-start | bytes 131072 | tf_op jit(solution)/shard_map/all_to_all | solution.py:211
  18.9 0.0 copy-done
  18.9 0.1 copy.15
  19.0 0.1 eq.40
  19.1 0.0 copy-done.1
  19.1 0.0 copy-start.3
  19.1 0.1 copy.26
  19.3 1.5 %copy-done.3 = bf16[768,2,768,1,1]{2,0,4,3,1:T(8,128)(2,1)S(1)} copy-done((bf16[768,2,768,1,1]{2,0,4,3,1:T(8,128)(2,1)S(1)}, bf16[768,2,768,1,1]{2,0,4,3,1:T(8,128)(2,1)}, u32[]{:S(2)}) %copy-start.3) | copy-done | bytes 2359320
  20.8 1.1 %fusion.4 = f32[2,768,64,2,3]{1,2,4,3,0:T(8,128)S(1)} fusion(bf16[768,2,768,1,1]{2,0,4,3,1:T(8,128)(2,1)S(1)} %copy-done.3, bf16[64,2,3,1536]{3,0,2,1:T(8,128)(2,1)S(1)} %bitcast.56), kind=kOutput, calls=%fused_computation.14 | convolution fusion | flops 905969664 | bytes 5308416 | tf_op jit(solution)/shard_map/thjn,nrm->hjrtm/dot_general | solution.py:216
  21.9 1.1 %multiply_bitcast_fusion = f32[2,3,2,64,768]{4,3,1,0,2:T(8,128)S(1)} fusion(f32[2,768,64,2,3]{1,2,4,3,0:T(8,128)S(1)} %fusion.4, bf16[768,2,768,1,1]{2,0,4,3,1:T(8,128)(2,1)S(1)} %copy-done.3, f32[768]{0:T(1024)S(1)} %fusion.9, bf16[64,2,3,1536]{3,0,2,1:T(8,128)(2,1)S(1)} %bitcast.57), kind=kOutput, calls=%fused_computation.2 | convolution fusion | flops 907739136 | bytes 7671808 | tf_op jit(solution)/shard_map/thjn,nrm->hjrtm/dot_general | solution.py:216
  23.0 0.2 add_convert_fusion
  23.2 0.1 pad_maximum_fusion
  23.3 0.1 copy.17
  23.4 2.7 %fusion.3 = bf16[128,48,128]{2,1,0:T(8,128)(2,1)} fusion(bf16[768,768]{1,0:T(8,128)(2,1)S(1)} %bitcast.54, s32[1024]{0:T(1024)S(1)} %eq.40), kind=kOutput, calls=%fused_computation.6 | convolution fusion | flops 1209532416 | bytes 2756608 | tf_op jit(solution)/shard_map/dot_general | solution.py:226
  26.1 0.0 copy-start.2
  26.1 4.1 %all-to-all-done.1 = bf16[128,2,128]{2,1,0:T(2,128)(2,1)S(1)} async-done(((bf16[128,2,128]{2,1,0:T(2,128)(2,1)}), bf16[128,2,128]{2,1,0:T(2,128)(2,1)S(1)}, u32[]{:S(2)}, u32[]{:S(2)}) %all-to-all-start.1) | async-done | bytes 65568 | tf_op jit(solution)/shard_map/all_to_all | solution.py:211
  30.2 9.8 %all-to-all-start = ((bf16[128,48,128]{2,1,0:T(8,128)(2,1)}), bf16[128,48,128]{2,1,0:T(8,128)(2,1)S(1)}, u32[]{:S(2)}, u32[]{:S(2)}) async-start(bf16[128,48,128]{2,1,0:T(8,128)(2,1)} %fusion.3), calls=%async_computation | async-start | bytes 3145728 | tf_op jit(solution)/shard_map/all_to_all | solution.py:237
  40.0 0.0 copy-done.2
  40.0 0.5 convolution_convert_fusion
  40.6 0.1 convert_reduce_fusion
  40.8 0.1 reshape.54
  40.8 0.1 copy.20
  40.9 0.2 multiply_reduce_fusion
  41.2 0.1 collective-permute-start.1
  41.3 1.0 %collective-permute-start = (f32[64,128]{1,0:T(8,128)S(1)}, f32[64,128]{1,0:T(8,128)S(1)}, u32[]{:S(2)}, u32[]{:S(2)}) collective-permute-start(f32[64,128]{1,0:T(8,128)S(1)} %multiply_reduce_fusion), channel_id=1, source_target_pairs={{0,1},{1,0},{2,3},{3,2},{4,5},{5,4},{6,7},{7,6},{8,9},{9,8},{10,11... | collective-permute-start | bytes 98312 | tf_op jit(solution)/shard_map/ppermute | solution.py:33
  42.3 2.5 %collective-permute-done.1 = f32[64,128]{1,0:T(8,128)S(1)} collective-permute-done((f32[64,128]{1,0:T(8,128)S(1)}, f32[64,128]{1,0:T(8,128)S(1)}, u32[]{:S(2)}, u32[]{:S(2)}) %collective-permute-start.1) | collective-permute-done | bytes 32800 | tf_op jit(solution)/shard_map/ppermute | solution.py:33
  44.7 0.0 collective-permute-done
  44.7 2.2 %collective-permute-start.2 = (f32[64,128]{1,0:T(8,128)S(1)}, f32[64,128]{1,0:T(8,128)S(1)}, u32[]{:S(2)}, u32[]{:S(2)}) collective-permute-start(f32[64,128]{1,0:T(8,128)S(1)} %add.65.values_ref), channel_id=1, source_target_pairs={{0,4},{2,6},{4,0},{6,2},{8,12},{10,14},{12,8},{14,10},{16,20},{18,... | collective-permute-start | bytes 98312 | tf_op jit(solution)/shard_map/ppermute | solution.py:21
  47.0 3.7 %basis.3 = (bf16[3,768,384]{2,1,0:T(8,128)(2,1)}, f32[64,128]{1,0:T(8,128)S(1)}) custom-call(f32[64,128]{1,0:T(8,128)S(1)} %add.65.values_ref, bf16[8,384,768]{2,1,0:T(8,128)(2,1)} %basis_ref.7), custom_call_target="tpu_custom_call" | custom-call | tf_op jit(solution)/shard_map/basis/pallas_call | solution.py:245
  50.7 0.1 collective-permute-done.2
  50.8 1.9 %collective-permute-start.3 = (f32[64,128]{1,0:T(8,128)S(1)}, f32[64,128]{1,0:T(8,128)S(1)}, u32[]{:S(2)}, u32[]{:S(2)}) collective-permute-start(f32[64,128]{1,0:T(8,128)S(1)} %add.66.values_ref), channel_id=1, source_target_pairs={{0,8},{2,10},{4,12},{6,14},{8,0},{10,2},{12,4},{14,6},{16,24},{18,... | collective-permute-start | bytes 98312 | tf_op jit(solution)/shard_map/ppermute | solution.py:21
  52.7 3.1 %basis.4 = (bf16[2,768,384]{2,1,0:T(8,128)(2,1)}, f32[64,128]{1,0:T(8,128)S(1)}) custom-call(f32[64,128]{1,0:T(8,128)S(1)} %add.66.values_ref, bf16[8,384,768]{2,1,0:T(8,128)(2,1)} %basis_ref.7), custom_call_target="tpu_custom_call" | custom-call | tf_op jit(solution)/shard_map/basis/pallas_call | solution.py:245
  55.9 0.0 collective-permute-done.3
  55.9 3.1 %collective-permute-start.4 = (f32[64,128]{1,0:T(8,128)S(1)}, f32[64,128]{1,0:T(8,128)S(1)}, u32[]{:S(2)}, u32[]{:S(2)}) collective-permute-start(f32[64,128]{1,0:T(8,128)S(1)} %add.67.values_ref), channel_id=1, source_target_pairs={{0,16},{2,18},{4,20},{6,22},{8,24},{10,26},{12,28},{14,30},{16,0},... | collective-permute-start | bytes 98312 | tf_op jit(solution)/shard_map/ppermute | solution.py:21
  59.0 3.7 %basis.5 = (bf16[3,768,384]{2,1,0:T(8,128)(2,1)}, f32[64,128]{1,0:T(8,128)S(1)}) custom-call(f32[64,128]{1,0:T(8,128)S(1)} %add.67.values_ref, bf16[8,384,768]{2,1,0:T(8,128)(2,1)} %basis_ref.7), custom_call_target="tpu_custom_call" | custom-call | tf_op jit(solution)/shard_map/basis/pallas_call | solution.py:245
  62.7 0.0 collective-permute-done.4
  62.7 3.2 %collective-permute-start.11 = (bf16[64,128]{1,0:T(8,128)(2,1)S(1)}, bf16[64,128]{1,0:T(8,128)(2,1)S(1)}, u32[]{:S(2)}, u32[]{:S(2)}) collective-permute-start(bf16[64,128]{1,0:T(8,128)(2,1)S(1)} %get-tuple-element.17), channel_id=1, source_target_pairs={{0,224},{2,226},{4,228},{6,230},{8,232},{10,234},{12,236},{14,238}... | collective-permute-start | bytes 49160 | tf_op jit(solution)/shard_map/ppermute | solution.py:269
  66.0 2.1 %collective-permute-start.10 = (bf16[64,128]{1,0:T(8,128)(2,1)S(1)}, bf16[64,128]{1,0:T(8,128)(2,1)S(1)}, u32[]{:S(2)}, u32[]{:S(2)}) collective-permute-start(bf16[64,128]{1,0:T(8,128)(2,1)S(1)} %get-tuple-element.17), channel_id=1, source_target_pairs={{0,192},{2,194},{4,196},{6,198},{8,200},{10,202},{12,204},{14,206}... | collective-permute-start | bytes 49160 | tf_op jit(solution)/shard_map/ppermute | solution.py:269
  68.1 1.9 %collective-permute-start.9 = (bf16[64,128]{1,0:T(8,128)(2,1)S(1)}, bf16[64,128]{1,0:T(8,128)(2,1)S(1)}, u32[]{:S(2)}, u32[]{:S(2)}) collective-permute-start(bf16[64,128]{1,0:T(8,128)(2,1)S(1)} %get-tuple-element.17), channel_id=1, source_target_pairs={{0,160},{2,162},{4,164},{6,166},{8,168},{10,170},{12,172},{14,174}... | collective-permute-start | bytes 49160 | tf_op jit(solution)/shard_map/ppermute | solution.py:269
  70.0 3.1 %collective-permute-start.8 = (bf16[64,128]{1,0:T(8,128)(2,1)S(1)}, bf16[64,128]{1,0:T(8,128)(2,1)S(1)}, u32[]{:S(2)}, u32[]{:S(2)}) collective-permute-start(bf16[64,128]{1,0:T(8,128)(2,1)S(1)} %get-tuple-element.17), channel_id=1, source_target_pairs={{0,128},{2,130},{4,132},{6,134},{8,136},{10,138},{12,140},{14,142}... | collective-permute-start | bytes 49160 | tf_op jit(solution)/shard_map/ppermute | solution.py:269
  73.1 0.3 collective-permute-start.7
  73.4 2.3 %collective-permute-done.11 = bf16[64,128]{1,0:T(8,128)(2,1)S(1)} collective-permute-done((bf16[64,128]{1,0:T(8,128)(2,1)S(1)}, bf16[64,128]{1,0:T(8,128)(2,1)S(1)}, u32[]{:S(2)}, u32[]{:S(2)}) %collective-permute-start.11) | collective-permute-done | bytes 16416 | tf_op jit(solution)/shard_map/ppermute | solution.py:269
  75.7 1.6 %collective-permute-start.6 = (bf16[64,128]{1,0:T(8,128)(2,1)S(1)}, bf16[64,128]{1,0:T(8,128)(2,1)S(1)}, u32[]{:S(2)}, u32[]{:S(2)}) collective-permute-start(bf16[64,128]{1,0:T(8,128)(2,1)S(1)} %get-tuple-element.17), channel_id=1, source_target_pairs={{0,64},{2,66},{4,68},{6,70},{8,72},{10,74},{12,76},{14,78},{16,80}... | collective-permute-start | bytes 49160 | tf_op jit(solution)/shard_map/ppermute | solution.py:269
  77.3 0.0 collective-permute-done.10
  77.3 3.7 %collective-permute-start.5 = (bf16[64,128]{1,0:T(8,128)(2,1)S(1)}, bf16[64,128]{1,0:T(8,128)(2,1)S(1)}, u32[]{:S(2)}, u32[]{:S(2)}) collective-permute-start(bf16[64,128]{1,0:T(8,128)(2,1)S(1)} %get-tuple-element.17), channel_id=1, source_target_pairs={{0,32},{2,34},{4,36},{6,38},{8,40},{10,42},{12,44},{14,46},{16,48}... | collective-permute-start | bytes 49160 | tf_op jit(solution)/shard_map/ppermute | solution.py:269
  81.0 0.0 collective-permute-done.9
  81.0 0.0 collective-permute-done.8
  81.0 0.0 collective-permute-done.7
  81.0 0.5 collective-permute-done.6
  81.5 0.9 %collective-permute-done.5 = bf16[64,128]{1,0:T(8,128)(2,1)S(1)} collective-permute-done((bf16[64,128]{1,0:T(8,128)(2,1)S(1)}, bf16[64,128]{1,0:T(8,128)(2,1)S(1)}, u32[]{:S(2)}, u32[]{:S(2)}) %collective-permute-start.5) | collective-permute-done | bytes 16416 | tf_op jit(solution)/shard_map/ppermute | solution.py:269
  82.5 0.0 all-to-all-done
  82.5 0.4 copy.25
  82.9 6.6 %panel.1 = bf16[1,8,1536,128]{3,2,1,0:T(8,128)(2,1)} custom-call(s32[8,128]{1,0:T(8,128)S(1)} %bitcast.53, bf16[48,128,128]{2,1,0:T(8,128)(2,1)S(1)} %bitcast.51, f32[64,128]{1,0:T(8,128)S(1)} %convert_add_fusion.values_ref, bf16[3,768,384]{2,1,0:T(8,128)(2,1)} %get-tuple-element.14.refs_0_, bf16[2,768,384]{2,1,0:T(8,128)(2,1)} %get-tuple-element.15.refs_1_, ...), custom_call_target="tpu_custom_call" | custom-call | tf_op jit(solution)/shard_map/panel/pallas_call | solution.py:270
  (10 shorter events, 0.1 us)
Async XLA Ops:
  0.0 18.9 %copy-start = (s32[128,8]{0,1:T(8,128)S(1)}, s32[128,8]{0,1:T(8,128)}, u32[]{:S(2)}) copy-start(s32[128,8]{0,1:T(8,128)} %param.7) | copy-start | bytes 12292
  0.0 19.1 %copy-start.1 = (bf16[1,64,2,3,1536]{4,2,3,1,0:T(2,128)(2,1)S(1)}, bf16[1,64,2,3,1536]{4,2,3,1,0:T(2,128)(2,1)}, u32[]{:S(2)}) copy-start(bf16[1,64,2,3,1536]{4,2,3,1,0:T(2,128)(2,1)} %param.5) | copy-start | bytes 3538948
  1.9 28.3 %all-to-all-start.1 = ((bf16[128,2,128]{2,1,0:T(2,128)(2,1)}), bf16[128,2,128]{2,1,0:T(2,128)(2,1)S(1)}, u32[]{:S(2)}, u32[]{:S(2)}) async-start(bf16[128,2,128]{2,1,0:T(2,128)(2,1)} %columns.1), calls=%async_computation.1 | async-start | bytes 131072 | tf_op jit(solution)/shard_map/all_to_all | solution.py:211
  19.1 1.7 %copy-start.3 = (bf16[768,2,768,1,1]{2,0,4,3,1:T(8,128)(2,1)S(1)}, bf16[768,2,768,1,1]{2,0,4,3,1:T(8,128)(2,1)}, u32[]{:S(2)}) copy-start(bf16[768,2,768,1,1]{2,0,4,3,1:T(8,128)(2,1)} %constant.38) | copy-start | bytes 7077892
  26.1 13.9 %copy-start.2 = (s32[2,64]{1,0:T(2,128)S(1)}, s32[2,64]{1,0:T(2,128)}, u32[]{:S(2)}) copy-start(s32[2,64]{1,0:T(2,128)} %modes_ref.1) | copy-start | bytes 1540
  30.2 52.3 %all-to-all-start = ((bf16[128,48,128]{2,1,0:T(8,128)(2,1)}), bf16[128,48,128]{2,1,0:T(8,128)(2,1)S(1)}, u32[]{:S(2)}, u32[]{:S(2)}) async-start(bf16[128,48,128]{2,1,0:T(8,128)(2,1)} %fusion.3), calls=%async_computation | async-start | bytes 3145728 | tf_op jit(solution)/shard_map/all_to_all | solution.py:237
  41.2 3.6 %collective-permute-start.1 = (f32[64,128]{1,0:T(8,128)S(1)}, f32[64,128]{1,0:T(8,128)S(1)}, u32[]{:S(2)}, u32[]{:S(2)}) collective-permute-start(f32[64,128]{1,0:T(8,128)S(1)} %multiply_reduce_fusion), channel_id=1, source_target_pairs={{0,3},{1,2},{2,1},{3,0},{4,7},{5,6},{6,5},{7,4},{8,11},{9,10},{10,... | collective-permute-start | bytes 98312 | tf_op jit(solution)/shard_map/ppermute | solution.py:33
  41.3 3.5 %collective-permute-start = (f32[64,128]{1,0:T(8,128)S(1)}, f32[64,128]{1,0:T(8,128)S(1)}, u32[]{:S(2)}, u32[]{:S(2)}) collective-permute-start(f32[64,128]{1,0:T(8,128)S(1)} %multiply_reduce_fusion), channel_id=1, source_target_pairs={{0,1},{1,0},{2,3},{3,2},{4,5},{5,4},{6,7},{7,6},{8,9},{9,8},{10,11... | collective-permute-start | bytes 98312 | tf_op jit(solution)/shard_map/ppermute | solution.py:33
  44.7 6.1 %collective-permute-start.2 = (f32[64,128]{1,0:T(8,128)S(1)}, f32[64,128]{1,0:T(8,128)S(1)}, u32[]{:S(2)}, u32[]{:S(2)}) collective-permute-start(f32[64,128]{1,0:T(8,128)S(1)} %add.65.values_ref), channel_id=1, source_target_pairs={{0,4},{2,6},{4,0},{6,2},{8,12},{10,14},{12,8},{14,10},{16,20},{18,... | collective-permute-start | bytes 98312 | tf_op jit(solution)/shard_map/ppermute | solution.py:21
  50.8 5.0 %collective-permute-start.3 = (f32[64,128]{1,0:T(8,128)S(1)}, f32[64,128]{1,0:T(8,128)S(1)}, u32[]{:S(2)}, u32[]{:S(2)}) collective-permute-start(f32[64,128]{1,0:T(8,128)S(1)} %add.66.values_ref), channel_id=1, source_target_pairs={{0,8},{2,10},{4,12},{6,14},{8,0},{10,2},{12,4},{14,6},{16,24},{18,... | collective-permute-start | bytes 98312 | tf_op jit(solution)/shard_map/ppermute | solution.py:21
  55.9 6.8 %collective-permute-start.4 = (f32[64,128]{1,0:T(8,128)S(1)}, f32[64,128]{1,0:T(8,128)S(1)}, u32[]{:S(2)}, u32[]{:S(2)}) collective-permute-start(f32[64,128]{1,0:T(8,128)S(1)} %add.67.values_ref), channel_id=1, source_target_pairs={{0,16},{2,18},{4,20},{6,22},{8,24},{10,26},{12,28},{14,30},{16,0},... | collective-permute-start | bytes 98312 | tf_op jit(solution)/shard_map/ppermute | solution.py:21
  62.7 12.9 %collective-permute-start.11 = (bf16[64,128]{1,0:T(8,128)(2,1)S(1)}, bf16[64,128]{1,0:T(8,128)(2,1)S(1)}, u32[]{:S(2)}, u32[]{:S(2)}) collective-permute-start(bf16[64,128]{1,0:T(8,128)(2,1)S(1)} %get-tuple-element.17), channel_id=1, source_target_pairs={{0,224},{2,226},{4,228},{6,230},{8,232},{10,234},{12,236},{14,238}... | collective-permute-start | bytes 49160 | tf_op jit(solution)/shard_map/ppermute | solution.py:269
  66.0 11.3 %collective-permute-start.10 = (bf16[64,128]{1,0:T(8,128)(2,1)S(1)}, bf16[64,128]{1,0:T(8,128)(2,1)S(1)}, u32[]{:S(2)}, u32[]{:S(2)}) collective-permute-start(bf16[64,128]{1,0:T(8,128)(2,1)S(1)} %get-tuple-element.17), channel_id=1, source_target_pairs={{0,192},{2,194},{4,196},{6,198},{8,200},{10,202},{12,204},{14,206}... | collective-permute-start | bytes 49160 | tf_op jit(solution)/shard_map/ppermute | solution.py:269
  68.1 12.9 %collective-permute-start.9 = (bf16[64,128]{1,0:T(8,128)(2,1)S(1)}, bf16[64,128]{1,0:T(8,128)(2,1)S(1)}, u32[]{:S(2)}, u32[]{:S(2)}) collective-permute-start(bf16[64,128]{1,0:T(8,128)(2,1)S(1)} %get-tuple-element.17), channel_id=1, source_target_pairs={{0,160},{2,162},{4,164},{6,166},{8,168},{10,170},{12,172},{14,174}... | collective-permute-start | bytes 49160 | tf_op jit(solution)/shard_map/ppermute | solution.py:269
  70.0 11.0 %collective-permute-start.8 = (bf16[64,128]{1,0:T(8,128)(2,1)S(1)}, bf16[64,128]{1,0:T(8,128)(2,1)S(1)}, u32[]{:S(2)}, u32[]{:S(2)}) collective-permute-start(bf16[64,128]{1,0:T(8,128)(2,1)S(1)} %get-tuple-element.17), channel_id=1, source_target_pairs={{0,128},{2,130},{4,132},{6,134},{8,136},{10,138},{12,140},{14,142}... | collective-permute-start | bytes 49160 | tf_op jit(solution)/shard_map/ppermute | solution.py:269
  73.1 7.9 %collective-permute-start.7 = (bf16[64,128]{1,0:T(8,128)(2,1)S(1)}, bf16[64,128]{1,0:T(8,128)(2,1)S(1)}, u32[]{:S(2)}, u32[]{:S(2)}) collective-permute-start(bf16[64,128]{1,0:T(8,128)(2,1)S(1)} %get-tuple-element.17), channel_id=1, source_target_pairs={{0,96},{2,98},{4,100},{6,102},{8,104},{10,106},{12,108},{14,110},{... | collective-permute-start | bytes 49160 | tf_op jit(solution)/shard_map/ppermute | solution.py:269
  75.7 5.9 %collective-permute-start.6 = (bf16[64,128]{1,0:T(8,128)(2,1)S(1)}, bf16[64,128]{1,0:T(8,128)(2,1)S(1)}, u32[]{:S(2)}, u32[]{:S(2)}) collective-permute-start(bf16[64,128]{1,0:T(8,128)(2,1)S(1)} %get-tuple-element.17), channel_id=1, source_target_pairs={{0,64},{2,66},{4,68},{6,70},{8,72},{10,74},{12,76},{14,78},{16,80}... | collective-permute-start | bytes 49160 | tf_op jit(solution)/shard_map/ppermute | solution.py:269
  77.3 5.2 %collective-permute-start.5 = (bf16[64,128]{1,0:T(8,128)(2,1)S(1)}, bf16[64,128]{1,0:T(8,128)(2,1)S(1)}, u32[]{:S(2)}, u32[]{:S(2)}) collective-permute-start(bf16[64,128]{1,0:T(8,128)(2,1)S(1)} %get-tuple-element.17), channel_id=1, source_target_pairs={{0,32},{2,34},{4,36},{6,38},{8,40},{10,42},{12,44},{14,46},{16,48}... | collective-permute-start | bytes 49160 | tf_op jit(solution)/shard_map/ppermute | solution.py:269

commit v8 on v7

--- a/solution.py
+++ b/solution.py
@@ -165,8 +165,9 @@
         rows_ref[s] = (products * scale).astype(jnp.bfloat16).reshape(rows_ref.shape[1:])
 
     begun = []
-    for start in range(0, slots + 2, 2):
-        coming = range(start, min(start + 2, slots))
+    bounds = list(range(0, slots, 2)) + [slots - 1, slots, slots]
+    for start, end in zip(bounds[:-1], bounds[1:]):
+        coming = range(start, end)
         for s in coming:
             copies[s].wait()
         new = [(s, of_both_parities(s)) for s in coming]
@@ -265,8 +266,7 @@
     plane = 16
     own = values.astype(jnp.bfloat16)
     for step in range(1, group_count // plane):
-        route = [(i, (i + step * plane) % group_count) for i in range(group_count)]
-        values = values + lax.ppermute(own, "lat", route).astype(jnp.float32)
+        values = values + from_far(own, step * plane).astype(jnp.float32)
     return pl.pallas_call(
         functools.partial(panel_kernel, scale=1.0 / (snap_count - 1)),
         in_specs=[in_smem, in_vmem, in_vmem] + [in_hbm] * len(pieces),

time: 90.3 us -> 91.8 us (1.017)
  starting transfers between devices: 51 us -> 52.9 us
    ppermute x3 -> x10, starting transfers between devices: 7.22 us -> 24.9 us  [from_far(): return lax.ppermute(block, 'lat', [(i, i ^ reach) for i in range(count)])]
    ppermute x7 -> x0, starting transfers between devices: 15.9 us -> none  [local(): values = values + lax.ppermute(own, 'lat', route).astype(jnp.float32)]
    ppermute x7 -> x0, waiting for transfers between devices: 3.77 us -> none  [local(): values = values + lax.ppermute(own, 'lat', route).astype(jnp.float32)]
    ppermute x3 -> x10, waiting for transfers between devices: 0.13 us -> 3.8 us  [from_far(): return lax.ppermute(block, 'lat', [(i, i ^ reach) for i in range(count)])]
  transfers between devices with their start and end apart: 14 -> 14, of which waited for: 6 -> 6; matrix products, arithmetic and copies ran while one was open for 8% -> 7% of each run, Pallas kernels for 12% -> 12%
where the time goes in v8:
time: 91.8 us; the launch traced here: 91.3 us
  starting transfers between devices  52.9 us (58%)
  Pallas kernels  18.9 us (21%)
  waiting for transfers between devices  10.4 us (11%)
  matrix products  5.37 us (6%)
  local copies, waits for them, and re-layouts  2.58 us (3%)
    ppermute x10, starting transfers between devices, from_far(): return lax.ppermute(block, 'lat', [(i, i ^ reach) for i in range(count)])  24.9 us
    all_to_all x1, starting transfers between devices, local(): lax.all_to_all(columns, 'lat', split_axis=0, concat_axis=0, tiled=True)  17.1 us
    pallas_call x3, Pallas kernels, local(): pl.pallas_call(functools.partial(basis_kernel, first=first, sources=group...  10.6 us
    all_to_all x1, starting transfers between devices, local(): lax.all_to_all(sent, 'lat', split_axis=0, concat_axis=0, tiled=True)  9.77 us
    pallas_call x1, Pallas kernels, local(): pl.pallas_call(functools.partial(panel_kernel, scale=1.0 / (snap_count -...  6.41 us
    all_to_all x1, waiting for transfers between devices, local(): lax.all_to_all(columns, 'lat', split_axis=0, concat_axis=0, tiled=True)  4.1 us
    ppermute x10, waiting for transfers between devices, from_far(): return lax.ppermute(block, 'lat', [(i, i ^ reach) for i in range(count)])  3.8 us
    dot_general x2, matrix products, rows_of(): lax.dot_general(placed.astype(jnp.bfloat16), parts, (((1,), (1,)), ((), (...  3.2 us
  transfers between devices with their start and end apart: 14, of which 6 were waited for; matrix products, arithmetic and copies ran while one was open for 7% of the time, Pallas kernels for 12%

profile of v8, /device:TPU:2, one launch (start us, length us, event | category | flops | bytes accessed | tf_op | source)
XLA Modules:
  0.0 91.3 jit_solution(7839197716663722522)
XLA Ops:
  0.0 0.0 copy-start
  0.0 0.0 copy-start.1
  0.0 1.9 %columns.1 = bf16[128,2,128]{2,1,0:T(2,128)(2,1)} custom-call(s32[8,128]{1,0:T(8,128)} %bitcast.52, s32[2,64]{1,0:T(2,128)} %modes_ref.1, bf16[8,384,768]{2,1,0:T(8,128)(2,1)} %basis_ref.7), custom_call_target="tpu_custom_call" | custom-call | tf_op jit(solution)/shard_map/columns/pallas_call | solution.py:199
  1.9 17.1 %all-to-all-start.1 = ((bf16[128,2,128]{2,1,0:T(2,128)(2,1)}), bf16[128,2,128]{2,1,0:T(2,128)(2,1)S(1)}, u32[]{:S(2)}, u32[]{:S(2)}) async-start(bf16[128,2,128]{2,1,0:T(2,128)(2,1)} %columns.1), calls=%async_computation.1 | async-start | bytes 131072 | tf_op jit(solution)/shard_map/all_to_all | solution.py:212
  19.1 0.0 copy-done
  19.1 0.1 copy.15
  19.2 0.1 eq.40
  19.3 0.0 copy-done.1
  19.3 0.0 copy-start.3
  19.3 0.1 copy.26
  19.4 1.5 %copy-done.3 = bf16[768,2,768,1,1]{2,0,4,3,1:T(8,128)(2,1)S(1)} copy-done((bf16[768,2,768,1,1]{2,0,4,3,1:T(8,128)(2,1)S(1)}, bf16[768,2,768,1,1]{2,0,4,3,1:T(8,128)(2,1)}, u32[]{:S(2)}) %copy-start.3) | copy-done | bytes 2359320
  21.0 1.1 %fusion.4 = f32[2,768,64,2,3]{1,2,4,3,0:T(8,128)S(1)} fusion(bf16[768,2,768,1,1]{2,0,4,3,1:T(8,128)(2,1)S(1)} %copy-done.3, bf16[64,2,3,1536]{3,0,2,1:T(8,128)(2,1)S(1)} %bitcast.56), kind=kOutput, calls=%fused_computation.14 | convolution fusion | flops 905969664 | bytes 5308416 | tf_op jit(solution)/shard_map/thjn,nrm->hjrtm/dot_general | solution.py:217
  22.0 1.1 %multiply_bitcast_fusion = f32[2,3,2,64,768]{4,3,1,0,2:T(8,128)S(1)} fusion(f32[2,768,64,2,3]{1,2,4,3,0:T(8,128)S(1)} %fusion.4, bf16[768,2,768,1,1]{2,0,4,3,1:T(8,128)(2,1)S(1)} %copy-done.3, f32[768]{0:T(1024)S(1)} %fusion.9, bf16[64,2,3,1536]{3,0,2,1:T(8,128)(2,1)S(1)} %bitcast.57), kind=kOutput, calls=%fused_computation.2 | convolution fusion | flops 907739136 | bytes 7671808 | tf_op jit(solution)/shard_map/thjn,nrm->hjrtm/dot_general | solution.py:217
  23.2 0.2 add_convert_fusion
  23.4 0.1 pad_maximum_fusion
  23.5 0.1 copy.17
  23.6 2.7 %fusion.3 = bf16[128,48,128]{2,1,0:T(8,128)(2,1)} fusion(bf16[768,768]{1,0:T(8,128)(2,1)S(1)} %bitcast.54, s32[1024]{0:T(1024)S(1)} %eq.40), kind=kOutput, calls=%fused_computation.6 | convolution fusion | flops 1209532416 | bytes 2756608 | tf_op jit(solution)/shard_map/dot_general | solution.py:227
  26.3 0.0 copy-start.2
  26.3 4.1 %all-to-all-done.1 = bf16[128,2,128]{2,1,0:T(2,128)(2,1)S(1)} async-done(((bf16[128,2,128]{2,1,0:T(2,128)(2,1)}), bf16[128,2,128]{2,1,0:T(2,128)(2,1)S(1)}, u32[]{:S(2)}, u32[]{:S(2)}) %all-to-all-start.1) | async-done | bytes 65568 | tf_op jit(solution)/shard_map/all_to_all | solution.py:212
  30.4 9.8 %all-to-all-start = ((bf16[128,48,128]{2,1,0:T(8,128)(2,1)}), bf16[128,48,128]{2,1,0:T(8,128)(2,1)S(1)}, u32[]{:S(2)}, u32[]{:S(2)}) async-start(bf16[128,48,128]{2,1,0:T(8,128)(2,1)} %fusion.3), calls=%async_computation | async-start | bytes 3145728 | tf_op jit(solution)/shard_map/all_to_all | solution.py:238
  40.2 0.0 copy-done.2
  40.2 0.5 convolution_convert_fusion
  40.8 0.1 convert_reduce_fusion
  40.9 0.1 reshape.54
  41.0 0.1 copy.20
  41.1 0.2 multiply_reduce_fusion
  41.3 0.1 collective-permute-start.1
  41.4 1.0 %collective-permute-start = (f32[64,128]{1,0:T(8,128)S(1)}, f32[64,128]{1,0:T(8,128)S(1)}, u32[]{:S(2)}, u32[]{:S(2)}) collective-permute-start(f32[64,128]{1,0:T(8,128)S(1)} %multiply_reduce_fusion), channel_id=1, source_target_pairs={{0,1},{1,0},{2,3},{3,2},{4,5},{5,4},{6,7},{7,6},{8,9},{9,8},{10,11... | collective-permute-start | bytes 98312 | tf_op jit(solution)/shard_map/ppermute | solution.py:33
  42.4 2.5 %collective-permute-done.1 = f32[64,128]{1,0:T(8,128)S(1)} collective-permute-done((f32[64,128]{1,0:T(8,128)S(1)}, f32[64,128]{1,0:T(8,128)S(1)}, u32[]{:S(2)}, u32[]{:S(2)}) %collective-permute-start.1) | collective-permute-done | bytes 32800 | tf_op jit(solution)/shard_map/ppermute | solution.py:33
  44.9 0.0 collective-permute-done
  44.9 2.2 %collective-permute-start.2 = (f32[64,128]{1,0:T(8,128)S(1)}, f32[64,128]{1,0:T(8,128)S(1)}, u32[]{:S(2)}, u32[]{:S(2)}) collective-permute-start(f32[64,128]{1,0:T(8,128)S(1)} %add.65.values_ref), channel_id=1, source_target_pairs={{0,4},{2,6},{4,0},{6,2},{8,12},{10,14},{12,8},{14,10},{16,20},{18,... | collective-permute-start | bytes 98312 | tf_op jit(solution)/shard_map/ppermute | solution.py:21
  47.1 3.7 %basis.3 = (bf16[3,768,384]{2,1,0:T(8,128)(2,1)}, f32[64,128]{1,0:T(8,128)S(1)}) custom-call(f32[64,128]{1,0:T(8,128)S(1)} %add.65.values_ref, bf16[8,384,768]{2,1,0:T(8,128)(2,1)} %basis_ref.7), custom_call_target="tpu_custom_call" | custom-call | tf_op jit(solution)/shard_map/basis/pallas_call | solution.py:246
  50.9 0.1 collective-permute-done.2
  51.0 1.9 %collective-permute-start.3 = (f32[64,128]{1,0:T(8,128)S(1)}, f32[64,128]{1,0:T(8,128)S(1)}, u32[]{:S(2)}, u32[]{:S(2)}) collective-permute-start(f32[64,128]{1,0:T(8,128)S(1)} %add.66.values_ref), channel_id=1, source_target_pairs={{0,8},{2,10},{4,12},{6,14},{8,0},{10,2},{12,4},{14,6},{16,24},{18,... | collective-permute-start | bytes 98312 | tf_op jit(solution)/shard_map/ppermute | solution.py:21
  52.9 3.1 %basis.4 = (bf16[2,768,384]{2,1,0:T(8,128)(2,1)}, f32[64,128]{1,0:T(8,128)S(1)}) custom-call(f32[64,128]{1,0:T(8,128)S(1)} %add.66.values_ref, bf16[8,384,768]{2,1,0:T(8,128)(2,1)} %basis_ref.7), custom_call_target="tpu_custom_call" | custom-call | tf_op jit(solution)/shard_map/basis/pallas_call | solution.py:246
  56.0 0.0 collective-permute-done.3
  56.1 3.1 %collective-permute-start.4 = (f32[64,128]{1,0:T(8,128)S(1)}, f32[64,128]{1,0:T(8,128)S(1)}, u32[]{:S(2)}, u32[]{:S(2)}) collective-permute-start(f32[64,128]{1,0:T(8,128)S(1)} %add.67.values_ref), channel_id=1, source_target_pairs={{0,16},{2,18},{4,20},{6,22},{8,24},{10,26},{12,28},{14,30},{16,0},... | collective-permute-start | bytes 98312 | tf_op jit(solution)/shard_map/ppermute | solution.py:21
  59.1 3.7 %basis.5 = (bf16[3,768,384]{2,1,0:T(8,128)(2,1)}, f32[64,128]{1,0:T(8,128)S(1)}) custom-call(f32[64,128]{1,0:T(8,128)S(1)} %add.67.values_ref, bf16[8,384,768]{2,1,0:T(8,128)(2,1)} %basis_ref.7), custom_call_target="tpu_custom_call" | custom-call | tf_op jit(solution)/shard_map/basis/pallas_call | solution.py:246
  62.9 0.0 collective-permute-done.4
  62.9 3.3 %collective-permute-start.11 = (bf16[64,128]{1,0:T(8,128)(2,1)S(1)}, bf16[64,128]{1,0:T(8,128)(2,1)S(1)}, u32[]{:S(2)}, u32[]{:S(2)}) collective-permute-start(bf16[64,128]{1,0:T(8,128)(2,1)S(1)} %get-tuple-element.17), channel_id=1, source_target_pairs={{0,224},{2,226},{4,228},{6,230},{8,232},{10,234},{12,236},{14,238}... | collective-permute-start | bytes 49160 | tf_op jit(solution)/shard_map/ppermute | solution.py:21
  66.2 1.4 %collective-permute-start.10 = (bf16[64,128]{1,0:T(8,128)(2,1)S(1)}, bf16[64,128]{1,0:T(8,128)(2,1)S(1)}, u32[]{:S(2)}, u32[]{:S(2)}) collective-permute-start(bf16[64,128]{1,0:T(8,128)(2,1)S(1)} %get-tuple-element.17), channel_id=1, source_target_pairs={{0,192},{2,194},{4,196},{6,198},{8,200},{10,202},{12,204},{14,206}... | collective-permute-start | bytes 49160 | tf_op jit(solution)/shard_map/ppermute | solution.py:21
  67.6 4.1 %collective-permute-start.9 = (bf16[64,128]{1,0:T(8,128)(2,1)S(1)}, bf16[64,128]{1,0:T(8,128)(2,1)S(1)}, u32[]{:S(2)}, u32[]{:S(2)}) collective-permute-start(bf16[64,128]{1,0:T(8,128)(2,1)S(1)} %get-tuple-element.17), channel_id=1, source_target_pairs={{0,160},{2,162},{4,164},{6,166},{8,168},{10,170},{12,172},{14,174}... | collective-permute-start | bytes 49160 | tf_op jit(solution)/shard_map/ppermute | solution.py:21
  71.7 1.1 %collective-permute-start.8 = (bf16[64,128]{1,0:T(8,128)(2,1)S(1)}, bf16[64,128]{1,0:T(8,128)(2,1)S(1)}, u32[]{:S(2)}, u32[]{:S(2)}) collective-permute-start(bf16[64,128]{1,0:T(8,128)(2,1)S(1)} %get-tuple-element.17), channel_id=1, source_target_pairs={{0,128},{2,130},{4,132},{6,134},{8,136},{10,138},{12,140},{14,142}... | collective-permute-start | bytes 49160 | tf_op jit(solution)/shard_map/ppermute | solution.py:21
  72.8 3.2 %collective-permute-start.7 = (bf16[64,128]{1,0:T(8,128)(2,1)S(1)}, bf16[64,128]{1,0:T(8,128)(2,1)S(1)}, u32[]{:S(2)}, u32[]{:S(2)}) collective-permute-start(bf16[64,128]{1,0:T(8,128)(2,1)S(1)} %get-tuple-element.17), channel_id=1, source_target_pairs={{0,96},{2,98},{4,100},{6,102},{8,104},{10,106},{12,108},{14,110},{... | collective-permute-start | bytes 49160 | tf_op jit(solution)/shard_map/ppermute | solution.py:21
  76.0 1.5 %collective-permute-done.11 = bf16[64,128]{1,0:T(8,128)(2,1)S(1)} collective-permute-done((bf16[64,128]{1,0:T(8,128)(2,1)S(1)}, bf16[64,128]{1,0:T(8,128)(2,1)S(1)}, u32[]{:S(2)}, u32[]{:S(2)}) %collective-permute-start.11) | collective-permute-done | bytes 16416 | tf_op jit(solution)/shard_map/ppermute | solution.py:21
  77.4 3.1 %collective-permute-start.6 = (bf16[64,128]{1,0:T(8,128)(2,1)S(1)}, bf16[64,128]{1,0:T(8,128)(2,1)S(1)}, u32[]{:S(2)}, u32[]{:S(2)}) collective-permute-start(bf16[64,128]{1,0:T(8,128)(2,1)S(1)} %get-tuple-element.17), channel_id=1, source_target_pairs={{0,64},{2,66},{4,68},{6,70},{8,72},{10,74},{12,76},{14,78},{16,80}... | collective-permute-start | bytes 49160 | tf_op jit(solution)/shard_map/ppermute | solution.py:21
  80.5 0.0 collective-permute-done.10
  80.5 1.5 %collective-permute-start.5 = (bf16[64,128]{1,0:T(8,128)(2,1)S(1)}, bf16[64,128]{1,0:T(8,128)(2,1)S(1)}, u32[]{:S(2)}, u32[]{:S(2)}) collective-permute-start(bf16[64,128]{1,0:T(8,128)(2,1)S(1)} %get-tuple-element.17), channel_id=1, source_target_pairs={{0,32},{2,34},{4,36},{6,38},{8,40},{10,42},{12,44},{14,46},{16,48}... | collective-permute-start | bytes 49160 | tf_op jit(solution)/shard_map/ppermute | solution.py:21
  82.1 0.0 collective-permute-done.9
  82.1 0.0 collective-permute-done.8
  82.1 0.0 collective-permute-done.7
  82.1 0.2 collective-permute-done.6
  82.2 2.0 %collective-permute-done.5 = bf16[64,128]{1,0:T(8,128)(2,1)S(1)} collective-permute-done((bf16[64,128]{1,0:T(8,128)(2,1)S(1)}, bf16[64,128]{1,0:T(8,128)(2,1)S(1)}, u32[]{:S(2)}, u32[]{:S(2)}) %collective-permute-start.5) | collective-permute-done | bytes 16416 | tf_op jit(solution)/shard_map/ppermute | solution.py:21
  84.3 0.0 all-to-all-done
  84.3 0.4 copy.25
  84.7 6.4 %panel.1 = bf16[1,8,1536,128]{3,2,1,0:T(8,128)(2,1)} custom-call(s32[8,128]{1,0:T(8,128)S(1)} %bitcast.53, bf16[48,128,128]{2,1,0:T(8,128)(2,1)S(1)} %bitcast.51, f32[64,128]{1,0:T(8,128)S(1)} %convert_add_fusion.values_ref, bf16[3,768,384]{2,1,0:T(8,128)(2,1)} %get-tuple-element.14.refs_0_, bf16[2,768,384]{2,1,0:T(8,128)(2,1)} %get-tuple-element.15.refs_1_, ...), custom_call_target="tpu_custom_call" | custom-call | tf_op jit(solution)/shard_map/panel/pallas_call | solution.py:270
  (10 shorter events, 0.1 us)
Async XLA Ops:
  0.0 19.1 %copy-start = (s32[128,8]{0,1:T(8,128)S(1)}, s32[128,8]{0,1:T(8,128)}, u32[]{:S(2)}) copy-start(s32[128,8]{0,1:T(8,128)} %param.7) | copy-start | bytes 12292
  0.0 19.3 %copy-start.1 = (bf16[1,64,2,3,1536]{4,2,3,1,0:T(2,128)(2,1)S(1)}, bf16[1,64,2,3,1536]{4,2,3,1,0:T(2,128)(2,1)}, u32[]{:S(2)}) copy-start(bf16[1,64,2,3,1536]{4,2,3,1,0:T(2,128)(2,1)} %param.5) | copy-start | bytes 3538948
  1.9 28.4 %all-to-all-start.1 = ((bf16[128,2,128]{2,1,0:T(2,128)(2,1)}), bf16[128,2,128]{2,1,0:T(2,128)(2,1)S(1)}, u32[]{:S(2)}, u32[]{:S(2)}) async-start(bf16[128,2,128]{2,1,0:T(2,128)(2,1)} %columns.1), calls=%async_computation.1 | async-start | bytes 131072 | tf_op jit(solution)/shard_map/all_to_all | solution.py:212
  19.3 1.7 %copy-start.3 = (bf16[768,2,768,1,1]{2,0,4,3,1:T(8,128)(2,1)S(1)}, bf16[768,2,768,1,1]{2,0,4,3,1:T(8,128)(2,1)}, u32[]{:S(2)}) copy-start(bf16[768,2,768,1,1]{2,0,4,3,1:T(8,128)(2,1)} %constant.38) | copy-start | bytes 7077892
  26.3 13.9 %copy-start.2 = (s32[2,64]{1,0:T(2,128)S(1)}, s32[2,64]{1,0:T(2,128)}, u32[]{:S(2)}) copy-start(s32[2,64]{1,0:T(2,128)} %modes_ref.1) | copy-start | bytes 1540
  30.4 53.9 %all-to-all-start = ((bf16[128,48,128]{2,1,0:T(8,128)(2,1)}), bf16[128,48,128]{2,1,0:T(8,128)(2,1)S(1)}, u32[]{:S(2)}, u32[]{:S(2)}) async-start(bf16[128,48,128]{2,1,0:T(8,128)(2,1)} %fusion.3), calls=%async_computation | async-start | bytes 3145728 | tf_op jit(solution)/shard_map/all_to_all | solution.py:238
  41.3 3.6 %collective-permute-start.1 = (f32[64,128]{1,0:T(8,128)S(1)}, f32[64,128]{1,0:T(8,128)S(1)}, u32[]{:S(2)}, u32[]{:S(2)}) collective-permute-start(f32[64,128]{1,0:T(8,128)S(1)} %multiply_reduce_fusion), channel_id=1, source_target_pairs={{0,3},{1,2},{2,1},{3,0},{4,7},{5,6},{6,5},{7,4},{8,11},{9,10},{10,... | collective-permute-start | bytes 98312 | tf_op jit(solution)/shard_map/ppermute | solution.py:33
  41.4 3.5 %collective-permute-start = (f32[64,128]{1,0:T(8,128)S(1)}, f32[64,128]{1,0:T(8,128)S(1)}, u32[]{:S(2)}, u32[]{:S(2)}) collective-permute-start(f32[64,128]{1,0:T(8,128)S(1)} %multiply_reduce_fusion), channel_id=1, source_target_pairs={{0,1},{1,0},{2,3},{3,2},{4,5},{5,4},{6,7},{7,6},{8,9},{9,8},{10,11... | collective-permute-start | bytes 98312 | tf_op jit(solution)/shard_map/ppermute | solution.py:33
  44.9 6.1 %collective-permute-start.2 = (f32[64,128]{1,0:T(8,128)S(1)}, f32[64,128]{1,0:T(8,128)S(1)}, u32[]{:S(2)}, u32[]{:S(2)}) collective-permute-start(f32[64,128]{1,0:T(8,128)S(1)} %add.65.values_ref), channel_id=1, source_target_pairs={{0,4},{2,6},{4,0},{6,2},{8,12},{10,14},{12,8},{14,10},{16,20},{18,... | collective-permute-start | bytes 98312 | tf_op jit(solution)/shard_map/ppermute | solution.py:21
  51.0 5.1 %collective-permute-start.3 = (f32[64,128]{1,0:T(8,128)S(1)}, f32[64,128]{1,0:T(8,128)S(1)}, u32[]{:S(2)}, u32[]{:S(2)}) collective-permute-start(f32[64,128]{1,0:T(8,128)S(1)} %add.66.values_ref), channel_id=1, source_target_pairs={{0,8},{2,10},{4,12},{6,14},{8,0},{10,2},{12,4},{14,6},{16,24},{18,... | collective-permute-start | bytes 98312 | tf_op jit(solution)/shard_map/ppermute | solution.py:21
  56.1 6.8 %collective-permute-start.4 = (f32[64,128]{1,0:T(8,128)S(1)}, f32[64,128]{1,0:T(8,128)S(1)}, u32[]{:S(2)}, u32[]{:S(2)}) collective-permute-start(f32[64,128]{1,0:T(8,128)S(1)} %add.67.values_ref), channel_id=1, source_target_pairs={{0,16},{2,18},{4,20},{6,22},{8,24},{10,26},{12,28},{14,30},{16,0},... | collective-permute-start | bytes 98312 | tf_op jit(solution)/shard_map/ppermute | solution.py:21
  62.9 14.5 %collective-permute-start.11 = (bf16[64,128]{1,0:T(8,128)(2,1)S(1)}, bf16[64,128]{1,0:T(8,128)(2,1)S(1)}, u32[]{:S(2)}, u32[]{:S(2)}) collective-permute-start(bf16[64,128]{1,0:T(8,128)(2,1)S(1)} %get-tuple-element.17), channel_id=1, source_target_pairs={{0,224},{2,226},{4,228},{6,230},{8,232},{10,234},{12,236},{14,238}... | collective-permute-start | bytes 49160 | tf_op jit(solution)/shard_map/ppermute | solution.py:21
  66.2 14.4 %collective-permute-start.10 = (bf16[64,128]{1,0:T(8,128)(2,1)S(1)}, bf16[64,128]{1,0:T(8,128)(2,1)S(1)}, u32[]{:S(2)}, u32[]{:S(2)}) collective-permute-start(bf16[64,128]{1,0:T(8,128)(2,1)S(1)} %get-tuple-element.17), channel_id=1, source_target_pairs={{0,192},{2,194},{4,196},{6,198},{8,200},{10,202},{12,204},{14,206}... | collective-permute-start | bytes 49160 | tf_op jit(solution)/shard_map/ppermute | solution.py:21
  67.6 14.5 %collective-permute-start.9 = (bf16[64,128]{1,0:T(8,128)(2,1)S(1)}, bf16[64,128]{1,0:T(8,128)(2,1)S(1)}, u32[]{:S(2)}, u32[]{:S(2)}) collective-permute-start(bf16[64,128]{1,0:T(8,128)(2,1)S(1)} %get-tuple-element.17), channel_id=1, source_target_pairs={{0,160},{2,162},{4,164},{6,166},{8,168},{10,170},{12,172},{14,174}... | collective-permute-start | bytes 49160 | tf_op jit(solution)/shard_map/ppermute | solution.py:21
  71.7 10.4 %collective-permute-start.8 = (bf16[64,128]{1,0:T(8,128)(2,1)S(1)}, bf16[64,128]{1,0:T(8,128)(2,1)S(1)}, u32[]{:S(2)}, u32[]{:S(2)}) collective-permute-start(bf16[64,128]{1,0:T(8,128)(2,1)S(1)} %get-tuple-element.17), channel_id=1, source_target_pairs={{0,128},{2,130},{4,132},{6,134},{8,136},{10,138},{12,140},{14,142}... | collective-permute-start | bytes 49160 | tf_op jit(solution)/shard_map/ppermute | solution.py:21
  72.8 9.3 %collective-permute-start.7 = (bf16[64,128]{1,0:T(8,128)(2,1)S(1)}, bf16[64,128]{1,0:T(8,128)(2,1)S(1)}, u32[]{:S(2)}, u32[]{:S(2)}) collective-permute-start(bf16[64,128]{1,0:T(8,128)(2,1)S(1)} %get-tuple-element.17), channel_id=1, source_target_pairs={{0,96},{2,98},{4,100},{6,102},{8,104},{10,106},{12,108},{14,110},{... | collective-permute-start | bytes 49160 | tf_op jit(solution)/shard_map/ppermute | solution.py:21
  77.4 4.8 %collective-permute-start.6 = (bf16[64,128]{1,0:T(8,128)(2,1)S(1)}, bf16[64,128]{1,0:T(8,128)(2,1)S(1)}, u32[]{:S(2)}, u32[]{:S(2)}) collective-permute-start(bf16[64,128]{1,0:T(8,128)(2,1)S(1)} %get-tuple-element.17), channel_id=1, source_target_pairs={{0,64},{2,66},{4,68},{6,70},{8,72},{10,74},{12,76},{14,78},{16,80}... | collective-permute-start | bytes 49160 | tf_op jit(solution)/shard_map/ppermute | solution.py:21
  80.5 3.7 %collective-permute-start.5 = (bf16[64,128]{1,0:T(8,128)(2,1)S(1)}, bf16[64,128]{1,0:T(8,128)(2,1)S(1)}, u32[]{:S(2)}, u32[]{:S(2)}) collective-permute-start(bf16[64,128]{1,0:T(8,128)(2,1)S(1)} %get-tuple-element.17), channel_id=1, source_target_pairs={{0,32},{2,34},{4,36},{6,38},{8,40},{10,42},{12,44},{14,46},{16,48}... | collective-permute-start | bytes 49160 | tf_op jit(solution)/shard_map/ppermute | solution.py:21
